TPU v7x, 32 devices: a whole 2x2x4 slice. The times are simulated.
32 devices in a mesh: parts: 2 (over x), gz: 8 (over z, y), view: 2 (over core).
Axes of the slice: x: 2, y: 2, z: 4, core: 2. Of those that a mesh axis runs over, the one named last changes fastest.
Arguments:
- observed: bfloat16 [8, 64, 256, 256], P('view', 'parts', 'gz'), parts along dimension 1, may hold values from 0.19921875 to 2
- initial: float32 [64, 256, 256], P('parts', 'gz'), parts along dimension 0, may hold values from 0.5 to 2
- psf_taps: float32 [8, 3, 15], replicated, may hold values from 0.05 to 1
- view_shifts: int32 [8, 2], replicated, may hold values from -7 to 7
- view_map: int32 [8], replicated, may hold values from 0 to 7, each once
Outputs:
- estimate: float32 [64, 256, 256], P('parts', 'gz'), parts along dimension 0
- surfaces: float32 [8, 64, 256, 256], P('view', 'parts', 'gz'), parts along dimension 1
There are 2 independent parts, one for each index of `parts`. A program takes and returns all parts, laid end to end along the dimension named above; an argument that names none is the same for every part. Nothing has to cross between parts.
Inputs may be any that keep to these rules, and one draw needn't show every extreme that they name: `view_map`: each view number stands in exactly one slot; view 0 is the reference view.
All inputs are finite; a program needn't handle non-finite values.
Results may differ from a plain program's by a relative error of at most 0.0014.
Values may be sent and summed in bfloat16 or wider, within the bound.
No kernel may reach another device: no remote copies, remote signals or barrier semaphores. Data moves between devices by JAX's collectives and lax.ppermute only.
A program may use at most 128 MiB of HBM per device.

v0:
```python
import functools
import math

import jax
import jax.numpy as jnp
import ml_dtypes
import numpy as np
from jax import lax
from jax.experimental import pallas as pl
from jax.experimental.pallas import tpu as pltpu
from jax.sharding import PartitionSpec as P


TAPS = 15
HALF = TAPS // 2
ROWS = 8
MID = 1.099609375


F32 = jnp.float32
BF16 = jnp.bfloat16


def dot(a, b):
    return jnp.dot(a, b, preferred_element_type=F32)


def dot_t(a, b):
    return lax.dot_general(a, b, (((1,), (1,)), ((), ())), preferred_element_type=F32)


def split(value):
    high = value.astype(BF16)
    return high, (value - high.astype(F32)).astype(BF16)


def np_split(table):
    high = table.astype(ml_dtypes.bfloat16)
    low = (table - high.astype(np.float64)).astype(ml_dtypes.bfloat16)
    return high, low


def side_by_side(table):
    return jnp.asarray(np.concatenate(np_split(table), 1))


def depth_order(depth):
    order = [0, depth // 2]
    for m in range(1, depth // 2):
        order += [m, depth - m]
    return np.array(order)


def angle_table(rows, columns, length):
    return 2.0 * np.pi * ((rows[:, None] * columns[None, :]) % length) / length


def depth_transform(real, imag, orient):
    count = len(real)
    if count == 1:
        return real, imag
    if count == 2:
        return [real[0] + real[1], real[0] - real[1]], [imag[0] + imag[1], imag[0] - imag[1]]
    quarter = count // 4
    parts = [depth_transform(real[j::4], imag[j::4], orient) for j in range(4)]
    out_real, out_imag = [None] * count, [None] * count
    for k in range(quarter):
        turned_parts = []
        for j in range(4):
            part_real, part_imag = parts[j][0][k], parts[j][1][k]
            if j * k:
                angle = -orient * 2.0 * math.pi * j * k / count
                cos, sin = math.cos(angle), math.sin(angle)
                if 8 * j * k == count:
                    part_real, part_imag = (part_real + orient * part_imag) * cos, (part_imag - orient * part_real) * cos
                else:
                    part_real, part_imag = part_real * cos - part_imag * sin, part_real * sin + part_imag * cos
            turned_parts.append((part_real, part_imag))
        (ar, ai), (br, bi), (cr, ci), (dr, di) = turned_parts
        sum_ac, dif_ac = (ar + cr, ai + ci), (ar - cr, ai - ci)
        sum_bd, dif_bd = (br + dr, bi + di), (br - dr, bi - di)
        out_real[k], out_imag[k] = sum_ac[0] + sum_bd[0], sum_ac[1] + sum_bd[1]
        out_real[k + 2 * quarter], out_imag[k + 2 * quarter] = sum_ac[0] - sum_bd[0], sum_ac[1] - sum_bd[1]
        plus = (dif_ac[0] + dif_bd[1], dif_ac[1] - dif_bd[0])
        minus = (dif_ac[0] - dif_bd[1], dif_ac[1] + dif_bd[0])
        first_part, second_part = (plus, minus) if orient > 0 else (minus, plus)
        out_real[k + quarter], out_imag[k + quarter] = first_part
        out_real[k + 3 * quarter], out_imag[k + 3 * quarter] = second_part
    return out_real, out_imag


def forward_bound(depth, width):
    return 0.9005 * math.sqrt(depth * width)


def backward_bound(length):
    return 1.0005 * math.sqrt(length)


def code_scale(bound):
    return bound / 32767.0**2


def encode(value, bound):
    scaled = value * lax.rsqrt(jnp.abs(value) + 1e-30) * (32767.0 / math.sqrt(bound))
    return (scaled + jnp.where(value < 0.0, -0.5, 0.5)).astype(jnp.int32).astype(jnp.int16)


def decode(code):
    value = code.astype(jnp.int32).astype(F32)
    return value * jnp.abs(value)


def row_tables(length, depth, width):
    half = length // 2
    positions = np.arange(length)
    freqs = np.arange(half)
    angles = angle_table(positions, freqs, length)
    cos_part, sin_part = np.cos(angles), np.sin(angles)
    sin_part[:, 0] = 1.0 - 2.0 * (positions % 2)
    both = np.concatenate([cos_part, sin_part], 1) / math.sqrt(length)
    return side_by_side(both.T * code_scale(forward_bound(depth, width))), side_by_side(both)


def column_tables(width, depth, length):
    half = width // 2
    positions = np.arange(width)
    freqs = np.arange(half)
    angles = angle_table(positions, freqs, width)
    scale = 1.0 / math.sqrt(width * depth)
    cos_part = np.cos(angles)
    sin_part = -np.sin(angles)
    sin_part[:, 0] = 1.0 - 2.0 * (positions % 2)
    forward = np.concatenate([cos_part, sin_part], 1) * scale
    weights = np.where(freqs == 0, 1.0, 2.0)
    inverse = np.concatenate([cos_part * weights, sin_part * weights], 1).T * scale
    return side_by_side(forward), side_by_side(inverse * code_scale(backward_bound(length)))


def table_times(table, block):
    size = block.shape[0]
    high, low = split(block)
    return dot(table, jnp.concatenate([high, high], 0)) + dot(table[:, :size], low)


def replace_row(array, row):
    top = array[:ROWS]
    row_id = lax.broadcasted_iota(jnp.int32, top.shape, 0)
    return jnp.concatenate([jnp.where(row_id == 0, row[:1], top), array[ROWS:]], 0)


def rows_forward(table, plane):
    both = table_times(table, plane)
    count = both.shape[0] // 2
    half = both.shape[1] // 2
    cos_real, cos_imag = both[:count, :half], both[:count, half:]
    sin_real, sin_imag = both[count:, :half], both[count:, half:]
    above = (replace_row(cos_real + sin_imag, cos_real), replace_row(cos_imag - sin_real, cos_imag))
    below = (replace_row(cos_real - sin_imag, sin_real), replace_row(cos_imag + sin_real, sin_imag))
    return above, below


def rows_inverse(table, above, below):
    even_real = replace_row(above[0] + below[0], above[0])
    even_imag = replace_row(above[1] + below[1], above[1])
    odd_real = replace_row(below[1] - above[1], below[0])
    odd_imag = replace_row(above[0] - below[0], below[1])
    top = jnp.concatenate([even_real, even_imag], 1)
    bottom = jnp.concatenate([odd_real, odd_imag], 1)
    return table_times(table, jnp.concatenate([top, bottom], 0))


def ref_slot_of(map_ref):
    slot = jnp.int32(0)
    for at in range(1, map_ref.shape[0]):
        slot = jnp.where(map_ref[at] == 0, jnp.int32(at), slot)
    return slot


def first_kernel(map_ref, observed_ref, columns_ref, out_ref, spread_ref, turned_ref):
    depth, rows, width = observed_ref.shape[1:]
    half = width // 2
    groups, _, local_depth = out_ref.shape[:3]
    flat = observed_ref[0].reshape(depth * rows, width)
    table = columns_ref[...]
    spread = dot(flat, table[:, :width]) + dot(flat, table[:, width:])
    spread_ref[...] = spread.reshape(depth, rows, width)
    shift = MID * math.sqrt(width * depth)
    spots = depth_order(depth)
    lane = lax.broadcasted_iota(jnp.int32, (ROWS, half), 1)

    @pl.loop(0, rows // ROWS)
    def _(b):
        at = pl.ds(pl.multiple_of(b * ROWS, ROWS), ROWS)
        real = [spread_ref[z, at, :half] for z in range(depth)]
        imag = [spread_ref[z, at, half:] for z in range(depth)]
        real, imag = depth_transform(real, imag, 1)
        edge = lane == 0
        real[0] = jnp.where(edge, real[0] - shift, real[0])
        for k in range(1, depth // 2):
            n = depth - k
            zero_real, zero_imag = 0.5 * (real[k] + real[n]), 0.5 * (imag[k] - imag[n])
            top_real, top_imag = 0.5 * (imag[k] + imag[n]), 0.5 * (real[n] - real[k])
            real[k], imag[k] = jnp.where(edge, zero_real, real[k]), jnp.where(edge, zero_imag, imag[k])
            real[n], imag[n] = jnp.where(edge, top_real, real[n]), jnp.where(edge, top_imag, imag[n])
        for spot, k in enumerate(spots):
            turned_ref[spot, at, :half] = real[k]
            turned_ref[spot, at, half:] = imag[k]

    code = encode(turned_ref[...], forward_bound(depth, width))
    out_ref[:, 0] = code.reshape(groups, local_depth, rows, width)


def load_plane(in_ref, k):
    groups, _, _, rows, width = in_ref.shape
    return decode(in_ref[:, 0, k].reshape(groups * rows, width))


def edge_mask(shape, group_zero):
    row = lax.broadcasted_iota(jnp.int32, shape, 0)
    lane = lax.broadcasted_iota(jnp.int32, shape, 1)
    return (lane == 0) & (row > 0) & group_zero


def spectrum(table, plane, k, group_zero, depth):
    above, below = rows_forward(table, plane)
    if k == 0:
        shift = MID * math.sqrt(depth * plane.shape[0] * plane.shape[1])
        lane = lax.broadcasted_iota(jnp.int32, above[0].shape, 1)
        here = (lane[:1] == 0) & group_zero
        row = jnp.where(here, above[0][:1] + shift, above[0][:1])
        above = (replace_row(above[0], row), above[1])
    if k < 2:
        mask = edge_mask(above[0].shape, group_zero)
        zero = (0.5 * (above[0] + below[0]), 0.5 * (above[1] - below[1]))
        top = (0.5 * (above[1] + below[1]), 0.5 * (below[0] - above[0]))
        above = tuple(jnp.where(mask, new, old) for new, old in zip(zero, above))
        below = tuple(jnp.where(mask, new, old) for new, old in zip(top, below))
    return above, below


def spectrum_kernel(place_ref, in_ref, rows_ref, out_ref):
    group_zero = place_ref[1] == 0
    groups, _, local_depth, _, width = in_ref.shape
    depth = groups * local_depth
    half = width // 2
    table = rows_ref[...]
    for k in range(local_depth):
        above, below = spectrum(table, load_plane(in_ref, k), k, group_zero, depth)
        count = above[0].shape[0]
        out_ref[k, :count, :half] = above[0]
        out_ref[k, :count, half:] = above[1]
        out_ref[k, count:, :half] = below[0]
        out_ref[k, count:, half:] = below[1]


def root(value):
    return value * lax.rsqrt(jnp.maximum(value, 1e-30))


def cross_of(value, ref):
    real, imag = value
    ref_real, ref_imag = ref
    power = (real * real + imag * imag) * (ref_real * ref_real + ref_imag * ref_imag)
    scale = 1.0 / (root(power) + 1.0)
    return (real * ref_real + imag * ref_imag) * scale, (imag * ref_real - real * ref_imag) * scale


def cross_of_real(value, ref):
    product = value * ref
    return product / (jnp.abs(product) + 1.0)


def cross_plane(value, ref, k, group_zero):
    crossed = cross_of(value, ref)
    if k < 2:
        lane = lax.broadcasted_iota(jnp.int32, (1, value[0].shape[1]), 1)
        here = (lane == 0) & group_zero
        parts = []
        for at in range(2):
            row = jnp.where(here, cross_of_real(value[at][:1], ref[at][:1]), crossed[at][:1])
            parts.append(replace_row(crossed[at], row))
        crossed = tuple(parts)
    return crossed


def cross_kernel(map_ref, place_ref, in_ref, rows_ref, back_ref, mine_ref, other_ref, out_ref):
    groups, _, local_depth, rows, width = in_ref.shape
    slots = map_ref.shape[0] // 2
    holds_ref = ref_slot_of(map_ref) // slots == place_ref[0]
    group_zero = place_ref[1] == 0
    depth = groups * local_depth
    half = width // 2
    length = groups * rows
    count = length // 2
    bound = backward_bound(length)
    table = rows_ref[...]
    for k in range(local_depth):
        above, below = spectrum(table, load_plane(in_ref, k), k, group_zero, depth)
        ref = jnp.where(holds_ref, mine_ref[k], other_ref[k])
        above = cross_plane(above, (ref[:count, :half], ref[:count, half:]), k, group_zero)
        below = cross_plane(below, (ref[count:, :half], ref[count:, half:]), k, group_zero)
        if k < 2:
            mask = edge_mask(above[0].shape, group_zero)
            plus = (above[0] - below[1], above[1] + below[0])
            minus = (above[0] + below[1], below[0] - above[1])
            above = tuple(jnp.where(mask, new, old) for new, old in zip(plus, above))
            below = tuple(jnp.where(mask, new, old) for new, old in zip(minus, below))
        back = rows_inverse(back_ref[...], above, below)
        out_ref[:, 0, k] = encode(back, bound).reshape(groups, rows, width)


def last_kernel(map_ref, in_ref, columns_ref, *rest):
    out_ref, turned_ref, spread_ref = rest[-3:]
    groups, _, local_depth, rows, width = in_ref.shape
    depth = groups * local_depth
    half = width // 2
    table = columns_ref[...]
    spots = depth_order(depth)
    value = decode(in_ref[:, 0])
    turned_ref[...] = value.reshape(depth, rows, width)

    @pl.loop(0, rows // ROWS)
    def _(b):
        at = pl.ds(pl.multiple_of(b * ROWS, ROWS), ROWS)
        real, imag = [None] * depth, [None] * depth
        for spot, k in enumerate(spots):
            real[k] = turned_ref[spot, at, :half]
            imag[k] = turned_ref[spot, at, half:]
        edge = lax.broadcasted_iota(jnp.int32, (ROWS, half), 1) == 0
        for k in range(1, depth // 2):
            n = depth - k
            plus = (real[k] - imag[n], imag[k] + real[n])
            minus = (real[k] + imag[n], real[n] - imag[k])
            real[k], imag[k] = jnp.where(edge, plus[0], real[k]), jnp.where(edge, plus[1], imag[k])
            real[n], imag[n] = jnp.where(edge, minus[0], real[n]), jnp.where(edge, minus[1], imag[n])
        real, imag = depth_transform(real, imag, -1)
        for z in range(depth):
            spread_ref[z, at, :half] = real[z]
            spread_ref[z, at, half:] = imag[z]

    high, low = split(spread_ref[...].reshape(depth * rows, width))
    cells = dot(high, table[:, :width]) + dot(high, table[:, width:]) + dot(low, table[:, :width])
    out_ref[0] = cells.reshape(depth, rows, width)


def pick_tap(psf_ref, view, axis, index):
    value = jnp.zeros(index.shape, F32)
    for j in range(TAPS):
        value = jnp.where(index == j, psf_ref[view, axis, j], value)
    return value


def filter_kernel(place_ref, map_ref, shift_ref, psf_ref, forward_ref, backward_ref, columns_ref):
    size = forward_ref.shape[1]
    width = columns_ref.shape[1]
    depth = size // ROWS
    view = map_ref[place_ref[0] * pl.num_programs(0) + pl.program_id(0)]
    depth_shift = shift_ref[view, 0]
    column_shift = shift_ref[view, 1]
    at_out = lax.broadcasted_iota(jnp.int32, (depth, size), 0)
    at_in = lax.broadcasted_iota(jnp.int32, (depth, size), 1) // ROWS
    row = lax.broadcasted_iota(jnp.int32, (ROWS, size), 0)
    cell = lax.broadcasted_iota(jnp.int32, (ROWS, size), 1) % ROWS
    for out_ref, orient in ((forward_ref, 1), (backward_ref, -1)):
        depth_part = pick_tap(psf_ref, view, 0, orient * (at_in - at_out) + HALF - depth_shift)
        for c in range(3):
            reach = c * ROWS + cell - ROWS - row
            row_part = pick_tap(psf_ref, view, 1, orient * reach + HALF)
            block = depth_part[:, None, :] * row_part[None, :, :]
            out_ref[0, :, c * size : (c + 1) * size] = block.reshape(size, size).astype(BF16)
    source = lax.broadcasted_iota(jnp.int32, (width, width), 0)
    target = lax.broadcasted_iota(jnp.int32, (width, width), 1)
    picked = pick_tap(psf_ref, view, 2, source - target + HALF - column_shift)
    columns_ref[0] = picked.astype(BF16)


def join_kernel(
    views,
    updated,
    *refs,
):
    if updated:
        mine_ref, other_ref, *refs = refs
    (
    estimate_ref,
    below_ref,
    above_ref,
    observed_ref,
    seen_below_ref,
    seen_above_ref,
    forward_ref,
    backward_ref,
    columns_ref,
    out_ref,
    *refs,
    ) = refs
    if updated:
        now_ref, *refs = refs
    else:
        now_ref = estimate_ref
    cells_ref, mixed_ref, blurred_ref, ratio_ref, product_ref = refs
    depth, rows, width = estimate_ref.shape
    size = depth * ROWS
    blocks = rows // ROWS
    slots = forward_ref.shape[0]
    step = pl.program_id(0)

    @pl.when(step == 0)
    def _():
        if updated:
            logs = mine_ref[...] + other_ref[...]
            now_ref[...] = estimate_ref[...] * jnp.exp(logs.reshape(depth, rows, width))
        for rim_ref, start in ((below_ref, 0), (above_ref, blocks + 2)):
            for b in range(2):
                piece = rim_ref[b].astype(F32).reshape(size, width)
                cells_ref[start + b] = piece.astype(BF16)
        for b in range(blocks):
            piece = now_ref[:, b * ROWS : (b + 1) * ROWS].reshape(size, width)
            cells_ref[b + 2] = piece.astype(BF16)
        product_ref[...] = jnp.ones_like(product_ref)

        @pl.loop(0, blocks + 2)
        def _(b):
            window = cells_ref[pl.ds(b, 3)].reshape(3 * size, width)
            mixed = dot(forward_ref[...].reshape(slots * size, 3 * size), window)
            mixed_ref[:, b] = mixed.astype(BF16).reshape(slots, size, width)

    columns = columns_ref[0]
    blurred = dot(mixed_ref[step].reshape((blocks + 2) * size, width), columns)
    blurred_ref[...] = blurred.reshape(blocks + 2, size, width)
    for b in range(blocks + 2):
        if b == 0:
            seen = seen_below_ref[0].astype(F32)
        elif b == blocks + 1:
            seen = seen_above_ref[0].astype(F32)
        else:
            seen = observed_ref[0, :, (b - 1) * ROWS : b * ROWS].astype(F32)
        seen = seen.reshape(size, width)
        ratio = jnp.where(seen > 0.0, seen / blurred_ref[b], 0.0)
        ratio_ref[b] = ratio.astype(BF16)
    ratio = dot_t(ratio_ref[...].reshape((blocks + 2) * size, width), columns)
    ratio_ref[...] = ratio.astype(BF16).reshape(blocks + 2, size, width)
    for b in range(blocks):
        window = ratio_ref[b : b + 3].reshape(3 * size, width)
        product_ref[b] = product_ref[b] * dot(backward_ref[0], window)

    @pl.when(step == slots - 1)
    def _():
        for b in range(blocks):
            logs = jnp.log(product_ref[b]) * (1.0 / views)
            out_ref[:, b * ROWS : (b + 1) * ROWS] = logs.reshape(depth, ROWS, width)


def whole(shape):
    return pl.BlockSpec(shape, lambda *_: (0,) * len(shape))


def cost(flops, moved):
    return pl.CostEstimate(flops=int(flops), bytes_accessed=int(moved), transcendentals=0)


def turn(payload):
    return lax.all_to_all(payload, "gz", split_axis=0, concat_axis=0, tiled=True)


def edges(field):
    extent = field.shape[1]
    low = [field[:, at : at + ROWS] for at in (0, ROWS)]
    high = [field[:, at : at + ROWS] for at in (extent - 2 * ROWS, extent - ROWS)]
    return jnp.stack(low), jnp.stack(high)


def send_rims(low, high):
    count = lax.axis_size("gz")
    below = lax.ppermute(high, "gz", [(i, i + 1) for i in range(count - 1)])
    above = lax.ppermute(low, "gz", [(i + 1, i) for i in range(count - 1)])
    return below, above


def swap_cores(field):
    count = lax.axis_size("view")
    return lax.ppermute(field, "view", [(i, (i + 1) % count) for i in range(count)])


def on_device(observed, initial, psf_taps, view_shifts, view_map):
    slots, depth, rows, width = observed.shape
    views = view_map.shape[0]
    groups = lax.axis_size("gz")
    length = groups * rows
    local_depth = depth // groups
    size = depth * ROWS
    blocks = rows // ROWS
    place = jnp.stack([lax.axis_index("view"), lax.axis_index("gz")]).astype(jnp.int32)

    columns_forward, columns_inverse = column_tables(width, depth, length)
    row_turn, row_back = row_tables(length, depth, width)

    low, high = edges(initial.astype(BF16))
    low = jnp.concatenate([observed[:, :, :ROWS], low], 0)
    high = jnp.concatenate([observed[:, :, rows - ROWS :], high], 0)
    first_rims = send_rims(low, high)

    chunk = slots // 2
    payload_block = (groups, 1, local_depth, rows, width)
    payload_shape = (groups, chunk, local_depth, rows, width)
    payload_bytes = 4 * depth * rows * width * chunk
    volume = depth * rows * width

    def first(start):
        return pl.pallas_call(
            first_kernel,
            grid_spec=pltpu.PrefetchScalarGridSpec(
                num_scalar_prefetch=1,
                grid=(chunk,),
                in_specs=[
                    pl.BlockSpec((1, depth, rows, width), lambda s, m: (lax.rem(s + start + ref_slot_of(m), slots), 0, 0, 0)),
                    whole(columns_forward.shape),
                ],
                out_specs=pl.BlockSpec(payload_block, lambda *a: (0, a[0], 0, 0, 0)),
                scratch_shapes=[pltpu.VMEM((depth, rows, width), F32)] * 2,
            ),
            out_shape=jax.ShapeDtypeStruct(payload_shape, jnp.int16),
            cost_estimate=cost(2 * chunk * volume * 8 * width, payload_bytes),
            name="first",
        )(view_map, observed, columns_forward)

    spectrum_shape = (local_depth, length, width)
    row_flops = 2 * local_depth * length * width * 3 * length

    def reference_spectrum(payload):
        return pl.pallas_call(
            spectrum_kernel,
            grid_spec=pltpu.PrefetchScalarGridSpec(
                num_scalar_prefetch=1,
                grid=(1,),
                in_specs=[
                    pl.BlockSpec(payload_block, lambda *_: (0, 0, 0, 0, 0)),
                    whole(row_turn.shape),
                ],
                out_specs=whole(spectrum_shape),
            ),
            out_shape=jax.ShapeDtypeStruct(spectrum_shape, F32),
            cost_estimate=cost(row_flops, 6 * volume),
            name="spectrum",
        )(place, payload, row_turn)

    def crossed(payload, mine, other):
        return pl.pallas_call(
            cross_kernel,
            grid_spec=pltpu.PrefetchScalarGridSpec(
                num_scalar_prefetch=2,
                grid=(chunk,),
                in_specs=[
                    pl.BlockSpec(payload_block, lambda *a: (0, a[0], 0, 0, 0)),
                    whole(row_turn.shape),
                    whole(row_back.shape),
                    whole(spectrum_shape),
                    whole(spectrum_shape),
                ],
                out_specs=pl.BlockSpec(payload_block, lambda *a: (0, a[0], 0, 0, 0)),
            ),
            out_shape=jax.ShapeDtypeStruct(payload_shape, jnp.int16),
            cost_estimate=cost(2 * row_flops * chunk, payload_bytes + 10 * volume),
            name="cross",
        )(view_map, place, payload, row_turn, row_back, mine, other)

    def last(payload, start, partial):
        specs = [
            pl.BlockSpec(payload_block, lambda *a: (0, a[0], 0, 0, 0)),
            whole(columns_inverse.shape),
        ]
        operands = [view_map, payload, columns_inverse]
        aliases = {}
        if partial is not None:
            specs.append(pl.BlockSpec(memory_space=pl.ANY))
            aliases = {len(operands): 0}
            operands.append(partial)
        return pl.pallas_call(
            last_kernel,
            grid_spec=pltpu.PrefetchScalarGridSpec(
                num_scalar_prefetch=1,
                grid=(chunk,),
                in_specs=specs,
                out_specs=pl.BlockSpec((1, depth, rows, width), lambda s, m: (lax.rem(s + start + ref_slot_of(m), slots), 0, 0, 0)),
                scratch_shapes=[pltpu.VMEM((depth, rows, width), F32)] * 2,
            ),
            out_shape=jax.ShapeDtypeStruct((slots, depth, rows, width), F32),
            input_output_aliases=aliases,
            cost_estimate=cost(2 * chunk * volume * 9 * width, payload_bytes * 1.5),
            name="last",
        )(*operands)

    def filters():
        smem = pl.BlockSpec(memory_space=pltpu.SMEM)
        return pl.pallas_call(
            filter_kernel,
            grid=(slots,),
            in_specs=[smem] * 4,
            out_specs=[
                pl.BlockSpec((1, size, 3 * size), lambda s: (s, 0, 0)),
                pl.BlockSpec((1, size, 3 * size), lambda s: (s, 0, 0)),
                pl.BlockSpec((1, width, width), lambda s: (s, 0, 0)),
            ],
            out_shape=[
                jax.ShapeDtypeStruct((slots, size, 3 * size), BF16),
                jax.ShapeDtypeStruct((slots, size, 3 * size), BF16),
                jax.ShapeDtypeStruct((slots, width, width), BF16),
            ],
            cost_estimate=cost(slots * size * size * 60, slots * size * size * 14),
            name="filters",
        )(place, view_map, view_shifts, psf_taps)

    forward, backward, columns = filters()

    def join(estimate, below, above, logs=None):
        def slot_block(shape):
            return pl.BlockSpec((1,) + shape, lambda s: (s,) + (0,) * len(shape))

        def rim_block(rim):
            at = rim.shape[0] // 2 - 1
            return pl.BlockSpec((2, depth, ROWS, width), lambda s: (at, 0, 0, 0))

        updated = logs is not None
        field = jax.ShapeDtypeStruct((depth, rows, width), F32)
        extra_specs = []
        if updated:
            extra_specs = [whole((depth, rows, width))] * 2
        return pl.pallas_call(
            functools.partial(join_kernel, views, updated),
            grid=(slots,),
            in_specs=extra_specs
            + [
                whole((depth, rows, width)),
                rim_block(below),
                rim_block(above),
                slot_block((depth, rows, width)),
                slot_block((depth, ROWS, width)),
                slot_block((depth, ROWS, width)),
                whole((slots, size, 3 * size)),
                slot_block((size, 3 * size)),
                slot_block((width, width)),
            ],
            out_specs=[whole((depth, rows, width))] * (1 + updated),
            out_shape=[field] * (1 + updated),
            scratch_shapes=[
                pltpu.VMEM((blocks + 4, size, width), BF16),
                pltpu.VMEM((slots, blocks + 2, size, width), BF16),
                pltpu.VMEM((blocks + 2, size, width), F32),
                pltpu.VMEM((blocks + 2, size, width), BF16),
                pltpu.VMEM((blocks, size, width), F32),
            ],
            cost_estimate=cost(2 * slots * size * width * ((blocks + 2) * (3 * size + 2 * width) + blocks * 3 * size), 12e6),
            name="join",
        )(*(logs or ()), estimate, below, above, observed, *first_rims, forward, backward, columns)

    sent_a = turn(first(0))
    payload_b = first(chunk)
    sent_b = turn(payload_b)
    mine = reference_spectrum(sent_a)
    other = swap_cores(mine)
    crossed_a, start = lax.optimization_barrier((crossed(sent_a, mine, other), initial))
    back_a = turn(crossed_a)

    (logs,) = join(start, *first_rims)
    logs, late = lax.optimization_barrier((logs, sent_b))
    total = (logs, swap_cores(logs))
    crossed_b = crossed(late, mine, other)

    def updated_rows(at):
        window = [lax.slice_in_dim(part, at, at + ROWS, axis=1) for part in (initial, *total)]
        return (window[0] * jnp.exp(window[1] + window[2])).astype(BF16)

    low = jnp.stack([updated_rows(at) for at in (0, ROWS)])
    high = jnp.stack([updated_rows(at) for at in (rows - 2 * ROWS, rows - ROWS)])
    rims = send_rims(low, high)
    back_b = turn(crossed_b)
    logs, estimate = join(initial, *rims, logs=total)
    estimate = estimate * jnp.exp(logs + swap_cores(logs))

    surfaces = last(back_a, 0, None)
    surfaces = last(back_b, chunk, surfaces)
    return estimate, surfaces


def solution(mesh):
    placed = (P("view", "parts", "gz", None), P("parts", "gz", None), P(), P(), P())

    return jax.shard_map(
        on_device,
        mesh=mesh,
        in_specs=placed,
        out_specs=(P("parts", "gz", None), P("view", "parts", "gz", None)),
        check_vma=False,
    )
```

profile of v0, /device:TPU:17, one launch (start us, length us, event | category | flops | bytes accessed | tf_op | source)
XLA Modules:
  0.0 185.8 jit_solution(13400473096567638786)
XLA Ops:
  0.6 5.1 %first.2 = s16[8,2,4,32,256]{4,3,2,1,0:T(8,128)(2,1)} custom-call(s32[8]{0:T(128)} %map_ref.13, bf16[4,32,32,256]{3,2,1,0:T(8,128)(2,1)} %refs_5_.1, bf16[256,512]{1,0:T(8,128)(2,1)} %constant.16.clone.columns_ref), custom_call_target="tpu_custom_call" | custom-call | flops 2147483648 | bytes 2097152 | tf_op jit(solution)/shard_map/first/pallas_call | solution.py:511
  5.7 5.6 %all-to-all-start = ((s16[8,2,4,32,256]{4,3,2,1,0:T(8,128)(2,1)}), s16[8,2,4,32,256]{4,3,2,1,0:T(8,128)(2,1)S(1)}, u32[]{:S(2)}, u32[]{:S(2)}) async-start(s16[8,2,4,32,256]{4,3,2,1,0:T(8,128)(2,1)} %first.2), calls=%async_computation | async-start | bytes 2097152 | tf_op jit(solution)/shard_map/all_to_all | solution.py:464
  11.3 5.1 %first.3 = s16[8,2,4,32,256]{4,3,2,1,0:T(8,128)(2,1)} custom-call(s32[8]{0:T(128)} %map_ref.13, bf16[4,32,32,256]{3,2,1,0:T(8,128)(2,1)} %refs_5_.1, bf16[256,512]{1,0:T(8,128)(2,1)} %constant.16.clone.columns_ref), custom_call_target="tpu_custom_call" | custom-call | flops 2147483648 | bytes 2097152 | tf_op jit(solution)/shard_map/first/pallas_call | solution.py:511
  16.4 17.1 %all-to-all-done.in_ref = s16[8,2,4,32,256]{4,3,2,1,0:T(8,128)(2,1)S(1)} async-done(((s16[8,2,4,32,256]{4,3,2,1,0:T(8,128)(2,1)}), s16[8,2,4,32,256]{4,3,2,1,0:T(8,128)(2,1)S(1)}, u32[]{:S(2)}, u32[]{:S(2)}) %all-to-all-start) | async-done | bytes 1048608 | tf_op jit(solution)/shard_map/all_to_all | solution.py:464
  33.5 7.3 %all-to-all-start.1 = ((s16[8,2,4,32,256]{4,3,2,1,0:T(8,128)(2,1)}), s16[8,2,4,32,256]{4,3,2,1,0:T(8,128)(2,1)}, u32[]{:S(2)}, u32[]{:S(2)}) async-start(s16[8,2,4,32,256]{4,3,2,1,0:T(8,128)(2,1)} %first.3), calls=%async_computation.1 | async-start | bytes 2097152 | tf_op jit(solution)/shard_map/all_to_all | solution.py:464
  41.6 1.3 fusion.16
  42.9 3.5 %spectrum.1.mine_ref = f32[4,256,256]{2,1,0:T(8,128)} custom-call(s32[2]{0:T(128)} %pad_add_fusion.place_ref, s16[8,2,4,32,256]{4,3,2,1,0:T(8,128)(2,1)} %copy-done.3, bf16[256,512]{1,0:T(8,128)(2,1)} %constant.18.clone.rows_ref), custom_call_target="tpu_custom_call" | custom-call | flops 402653184 | bytes 1572864 | tf_op jit(solution)/shard_map/spectrum/pallas_call | solution.py:532
  46.3 1.6 collective-permute-start
  48.0 3.1 %collective-permute-start.1 = (bf16[6,32,8,256]{3,2,1,0:T(8,128)(2,1)S(1)}, bf16[6,32,8,256]{3,2,1,0:T(8,128)(2,1)S(1)}, u32[]{:S(2)}, u32[]{:S(2)}) collective-permute-start(bf16[6,32,8,256]{3,2,1,0:T(8,128)(2,1)S(1)} %pad_maximum_fusion), channel_id=1, source_target_pairs={{0,2},{2,4},{4,6},{6,8},{8,10},{10,12},{12,14},{1,3},{3,5},{5,7},{... | collective-permute-start | bytes 2359304 | tf_op jit(solution)/shard_map/ppermute | solution.py:476
  51.3 3.1 %collective-permute-start.2 = (bf16[6,32,8,256]{3,2,1,0:T(8,128)(2,1)S(1)}, bf16[6,32,8,256]{3,2,1,0:T(8,128)(2,1)S(1)}, u32[]{:S(2)}, u32[]{:S(2)}) collective-permute-start(bf16[6,32,8,256]{3,2,1,0:T(8,128)(2,1)S(1)} %pad_maximum_fusion.1), channel_id=1, source_target_pairs={{2,0},{4,2},{6,4},{8,6},{10,8},{12,10},{14,12},{3,1},{5,3},{7,5},{... | collective-permute-start | bytes 2359304 | tf_op jit(solution)/shard_map/ppermute | solution.py:477
  55.6 6.8 %cross.2 = s16[8,2,4,32,256]{4,3,2,1,0:T(8,128)(2,1)} custom-call(s32[8]{0:T(128)} %map_ref.13, s32[2]{0:T(128)} %pad_add_fusion.place_ref, s16[8,2,4,32,256]{4,3,2,1,0:T(8,128)(2,1)} %copy-done.3, bf16[256,512]{1,0:T(8,128)(2,1)} %constant.18.clone.rows_ref, bf16[256,512]{1,0:T(8,128)(2,1)} %constant.19.clone.back_ref, f32[4,256,256]{2,1,0:T(8,128)} %spectrum.1.mine_ref, ...), custom_call_target="tpu_custom_call" | custom-call | flops 1610612736 | bytes 4718592 | tf_op jit(solution)/shard_map/cross/pallas_call | solution.py:549
  62.4 0.7 all-to-all-done.1.in_ref
  63.2 7.4 %all-to-all-start.3 = ((s16[8,2,4,32,256]{4,3,2,1,0:T(8,128)(2,1)}), s16[8,2,4,32,256]{4,3,2,1,0:T(8,128)(2,1)}, u32[]{:S(2)}, u32[]{:S(2)}) async-start(s16[8,2,4,32,256]{4,3,2,1,0:T(8,128)(2,1)} %cross.2), calls=%async_computation.3 | async-start | bytes 2097152 | tf_op jit(solution)/shard_map/all_to_all | solution.py:464
  70.6 4.0 %filters.1 = (bf16[4,256,768]{2,1,0:T(8,128)(2,1)}, bf16[4,256,768]{2,1,0:T(8,128)(2,1)}, bf16[4,256,256]{2,1,0:T(8,128)(2,1)}) custom-call(s32[2]{0:T(128)} %pad_add_fusion.place_ref, s32[8]{0:T(128)} %map_ref.13, s32[8,2]{1,0:T(8,128)} %copy.12.shift_ref, f32[8,3,15]{2,1,0:T(4,128)} %copy.13.psf_ref), custom_call_target="tpu_custom_call" | custom-call | flops 15728640 | bytes 3670016 | tf_op jit(solution)/shard_map/filters/pallas_call | solution.py:596
  74.6 21.4 %collective-permute-done.1.refs_1_.refs_4_.refs_6_ = bf16[6,32,8,256]{3,2,1,0:T(8,128)(2,1)S(1)} collective-permute-done((bf16[6,32,8,256]{3,2,1,0:T(8,128)(2,1)S(1)}, bf16[6,32,8,256]{3,2,1,0:T(8,128)(2,1)S(1)}, u32[]{:S(2)}, u32[]{:S(2)}) %collective-permute-start.1) | collective-permute-done | bytes 786464 | tf_op jit(solution)/shard_map/ppermute | solution.py:476
  96.0 2.4 %collective-permute-done.2.refs_2_.refs_5_.refs_7_ = bf16[6,32,8,256]{3,2,1,0:T(8,128)(2,1)S(1)} collective-permute-done((bf16[6,32,8,256]{3,2,1,0:T(8,128)(2,1)S(1)}, bf16[6,32,8,256]{3,2,1,0:T(8,128)(2,1)S(1)}, u32[]{:S(2)}, u32[]{:S(2)}) %collective-permute-start.2) | collective-permute-done | bytes 786464 | tf_op jit(solution)/shard_map/ppermute | solution.py:477
  98.4 0.9 copy-done.12
  99.3 11.8 %join.2.refs_0_ = f32[32,32,256]{2,1,0:T(8,128)} custom-call(f32[32,32,256]{2,1,0:T(8,128)} %refs_2_.1, bf16[6,32,8,256]{3,2,1,0:T(8,128)(2,1)} %copy-done.11, bf16[6,32,8,256]{3,2,1,0:T(8,128)(2,1)} %copy-done.12, bf16[4,32,32,256]{3,2,1,0:T(8,128)(2,1)} %refs_5_.1, bf16[6,32,8,256]{3,2,1,0:T(8,128)(2,1)} %copy-done.11, bf16[6,32,8,256]{3,2,1,0:T(8,128)(2,1)} %copy-done.12, ...), custom_call_target="tpu_custom_call" | custom-call | flops 5637144576 | bytes 12000000 | tf_op jit(solution)/shard_map/join/pallas_call | solution.py:629
  111.1 1.2 collective-permute-start.3
  112.3 6.8 %cross.3 = s16[8,2,4,32,256]{4,3,2,1,0:T(8,128)(2,1)} custom-call(s32[8]{0:T(128)} %map_ref.13, s32[2]{0:T(128)} %pad_add_fusion.place_ref, s16[8,2,4,32,256]{4,3,2,1,0:T(8,128)(2,1)} %all-to-all-done.1.in_ref, bf16[256,512]{1,0:T(8,128)(2,1)} %constant.18.clone.rows_ref, bf16[256,512]{1,0:T(8,128)(2,1)} %constant.19.clone.back_ref, ...), custom_call_target="tpu_custom_call" | custom-call | flops 1610612736 | bytes 4718592 | tf_op jit(solution)/shard_map/cross/pallas_call | solution.py:549
  119.1 1.0 fusion.14
  120.2 6.1 %all-to-all-start.2 = ((s16[8,2,4,32,256]{4,3,2,1,0:T(8,128)(2,1)}), s16[8,2,4,32,256]{4,3,2,1,0:T(8,128)(2,1)S(1)}, u32[]{:S(2)}, u32[]{:S(2)}) async-start(s16[8,2,4,32,256]{4,3,2,1,0:T(8,128)(2,1)} %cross.3), calls=%async_computation.2 | async-start | bytes 2097152 | tf_op jit(solution)/shard_map/all_to_all | solution.py:464
  126.3 3.1 %collective-permute-start.4 = (bf16[2,32,8,256]{3,2,1,0:T(8,128)(2,1)S(1)}, bf16[2,32,8,256]{3,2,1,0:T(8,128)(2,1)S(1)}, u32[]{:S(2)}, u32[]{:S(2)}) collective-permute-start(bf16[2,32,8,256]{3,2,1,0:T(8,128)(2,1)S(1)} %pad_maximum_fusion.2), channel_id=1, source_target_pairs={{0,2},{2,4},{4,6},{6,8},{8,10},{10,12},{12,14},{1,3},{3,5},{5,7},{... | collective-permute-start | bytes 786440 | tf_op jit(solution)/shard_map/ppermute | solution.py:476
  129.5 3.3 %collective-permute-start.5 = (bf16[2,32,8,256]{3,2,1,0:T(8,128)(2,1)S(1)}, bf16[2,32,8,256]{3,2,1,0:T(8,128)(2,1)S(1)}, u32[]{:S(2)}, u32[]{:S(2)}) collective-permute-start(bf16[2,32,8,256]{3,2,1,0:T(8,128)(2,1)S(1)} %pad_maximum_fusion.3), channel_id=1, source_target_pairs={{2,0},{4,2},{6,4},{8,6},{10,8},{12,10},{14,12},{3,1},{5,3},{7,5},{... | collective-permute-start | bytes 786440 | tf_op jit(solution)/shard_map/ppermute | solution.py:477
  132.7 24.3 %collective-permute-done.4.refs_3_ = bf16[2,32,8,256]{3,2,1,0:T(8,128)(2,1)S(1)} collective-permute-done((bf16[2,32,8,256]{3,2,1,0:T(8,128)(2,1)S(1)}, bf16[2,32,8,256]{3,2,1,0:T(8,128)(2,1)S(1)}, u32[]{:S(2)}, u32[]{:S(2)}) %collective-permute-start.4) | collective-permute-done | bytes 262176 | tf_op jit(solution)/shard_map/ppermute | solution.py:476
  157.0 0.7 copy-done.13
  157.7 0.7 copy-done.14
  158.4 13.1 %join.3 = (f32[32,32,256]{2,1,0:T(8,128)}, f32[32,32,256]{2,1,0:T(8,128)}) custom-call(f32[32,32,256]{2,1,0:T(8,128)} %join.2.refs_0_, f32[32,32,256]{2,1,0:T(8,128)} %copy-done.5, f32[32,32,256]{2,1,0:T(8,128)} %refs_2_.1, bf16[2,32,8,256]{3,2,1,0:T(8,128)(2,1)} %copy-done.13, bf16[2,32,8,256]{3,2,1,0:T(8,128)(2,1)} %copy-done.14, ...), custom_call_target="tpu_custom_call" | custom-call | flops 5637144576 | bytes 12000000 | tf_op jit(solution)/shard_map/join/pallas_call | solution.py:629
  172.0 5.1 %last.2.rest_0_ = f32[4,32,32,256]{3,2,1,0:T(8,128)} custom-call(s32[8]{0:T(128)} %map_ref.13, s16[8,2,4,32,256]{4,3,2,1,0:T(8,128)(2,1)} %all-to-all-done.3.in_ref, bf16[256,512]{1,0:T(8,128)(2,1)} %constant.17.clone.columns_ref), custom_call_target="tpu_custom_call" | custom-call | flops 2415919104 | bytes 3145728 | tf_op jit(solution)/shard_map/last/pallas_call | solution.py:579
  177.1 1.0 copy-done.2
  178.1 5.2 %last.3 = f32[4,32,32,256]{3,2,1,0:T(8,128)} custom-call(s32[8]{0:T(128)} %map_ref.13, s16[8,2,4,32,256]{4,3,2,1,0:T(8,128)(2,1)} %copy-done.2, bf16[256,512]{1,0:T(8,128)(2,1)} %constant.17.clone.columns_ref, f32[4,32,32,256]{3,2,1,0:T(8,128)} %last.2.rest_0_), custom_call_target="tpu_custom_call", output_to_operand_aliasing={{}: (3, {})} | custom-call | flops 2415919104 | bytes 3145728 | tf_op jit(solution)/shard_map/last/pallas_call | solution.py:579
  183.3 2.5 %exponential_multiply_fusion = f32[32,32,256]{2,1,0:T(8,128)} fusion(f32[32,32,256]{2,1,0:T(8,128)S(1)} %copy-done.7, f32[32,32,256]{2,1,0:T(8,128)S(1)} %copy-done.6, f32[32,32,256]{2,1,0:T(8,128)} %collective-permute-done.6), kind=kLoop, calls=%fused_computation | loop fusion | flops 524288 | bytes 4194304 | tf_op jit(solution)/shard_map/mul | solution.py:679
  (42 shorter events, 2.8 us)
Async XLA Ops:
  5.7 27.8 %all-to-all-start = ((s16[8,2,4,32,256]{4,3,2,1,0:T(8,128)(2,1)}), s16[8,2,4,32,256]{4,3,2,1,0:T(8,128)(2,1)S(1)}, u32[]{:S(2)}, u32[]{:S(2)}) async-start(s16[8,2,4,32,256]{4,3,2,1,0:T(8,128)(2,1)} %first.2), calls=%async_computation | async-start | bytes 2097152 | tf_op jit(solution)/shard_map/all_to_all | solution.py:464
  16.4 24.5 %copy-start = (f32[32,32,256]{2,1,0:T(8,128)S(1)}, f32[32,32,256]{2,1,0:T(8,128)}, u32[]{:S(2)}) copy-start(f32[32,32,256]{2,1,0:T(8,128)} %refs_2_.1) | copy-start | bytes 3145732
  33.5 9.3 %copy-start.3 = (s16[8,2,4,32,256]{4,3,2,1,0:T(8,128)(2,1)}, s16[8,2,4,32,256]{4,3,2,1,0:T(8,128)(2,1)S(1)}, u32[]{:S(2)}) copy-start(s16[8,2,4,32,256]{4,3,2,1,0:T(8,128)(2,1)S(1)} %all-to-all-done.in_ref) | copy-start | bytes 3145732
  33.5 29.6 %all-to-all-start.1 = ((s16[8,2,4,32,256]{4,3,2,1,0:T(8,128)(2,1)}), s16[8,2,4,32,256]{4,3,2,1,0:T(8,128)(2,1)}, u32[]{:S(2)}, u32[]{:S(2)}) async-start(s16[8,2,4,32,256]{4,3,2,1,0:T(8,128)(2,1)} %first.3), calls=%async_computation.1 | async-start | bytes 2097152 | tf_op jit(solution)/shard_map/all_to_all | solution.py:464
  46.3 8.0 %copy-start.10 = (s32[8,2]{0,1:T(2,128)S(1)}, s32[8,2]{0,1:T(2,128)}, u32[]{:S(2)}) copy-start(s32[8,2]{0,1:T(2,128)} %param.12) | copy-start | bytes 196
  46.3 8.7 %copy-start.9 = (f32[8,3,15]{2,0,1:T(8,128)S(1)}, f32[8,3,15]{2,0,1:T(8,128)}, u32[]{:S(2)}) copy-start(f32[8,3,15]{2,0,1:T(8,128)} %param.11) | copy-start | bytes 4324
  46.3 9.3 %collective-permute-start = (f32[4,256,256]{2,1,0:T(8,128)}, f32[4,256,256]{2,1,0:T(8,128)}, u32[]{:S(2)}, u32[]{:S(2)}) collective-permute-start(f32[4,256,256]{2,1,0:T(8,128)} %spectrum.1.mine_ref), channel_id=1, source_target_pairs={{0,1},{1,0},{2,3},{3,2},{4,5},{5,4},{6,7},{7,6},{8,9},{9,8},{10,11... | collective-permute-start | bytes 3145736 | tf_op jit(solution)/shard_map/ppermute | solution.py:483
  48.0 48.0 %collective-permute-start.1 = (bf16[6,32,8,256]{3,2,1,0:T(8,128)(2,1)S(1)}, bf16[6,32,8,256]{3,2,1,0:T(8,128)(2,1)S(1)}, u32[]{:S(2)}, u32[]{:S(2)}) collective-permute-start(bf16[6,32,8,256]{3,2,1,0:T(8,128)(2,1)S(1)} %pad_maximum_fusion), channel_id=1, source_target_pairs={{0,2},{2,4},{4,6},{6,8},{8,10},{10,12},{12,14},{1,3},{3,5},{5,7},{... | collective-permute-start | bytes 2359304 | tf_op jit(solution)/shard_map/ppermute | solution.py:476
  51.3 47.1 %collective-permute-start.2 = (bf16[6,32,8,256]{3,2,1,0:T(8,128)(2,1)S(1)}, bf16[6,32,8,256]{3,2,1,0:T(8,128)(2,1)S(1)}, u32[]{:S(2)}, u32[]{:S(2)}) collective-permute-start(bf16[6,32,8,256]{3,2,1,0:T(8,128)(2,1)S(1)} %pad_maximum_fusion.1), channel_id=1, source_target_pairs={{2,0},{4,2},{6,4},{8,6},{10,8},{12,10},{14,12},{3,1},{5,3},{7,5},{... | collective-permute-start | bytes 2359304 | tf_op jit(solution)/shard_map/ppermute | solution.py:477
  63.2 57.0 %all-to-all-start.3 = ((s16[8,2,4,32,256]{4,3,2,1,0:T(8,128)(2,1)}), s16[8,2,4,32,256]{4,3,2,1,0:T(8,128)(2,1)}, u32[]{:S(2)}, u32[]{:S(2)}) async-start(s16[8,2,4,32,256]{4,3,2,1,0:T(8,128)(2,1)} %cross.2), calls=%async_computation.3 | async-start | bytes 2097152 | tf_op jit(solution)/shard_map/all_to_all | solution.py:464
  96.0 2.4 %copy-start.11 = (bf16[6,32,8,256]{3,2,1,0:T(8,128)(2,1)}, bf16[6,32,8,256]{3,2,1,0:T(8,128)(2,1)S(1)}, u32[]{:S(2)}) copy-start(bf16[6,32,8,256]{3,2,1,0:T(8,128)(2,1)S(1)} %collective-permute-done.1.refs_1_.refs_4_.refs_6_) | copy-start | bytes 2359300
  98.4 0.9 copy-start.12
  111.1 8.0 %copy-start.1 = (f32[32,32,256]{2,1,0:T(8,128)S(1)}, f32[32,32,256]{2,1,0:T(8,128)}, u32[]{:S(2)}) copy-start(f32[32,32,256]{2,1,0:T(8,128)} %refs_2_.1) | copy-start | bytes 3145732
  111.1 8.0 %copy-start.4 = (f32[32,32,256]{2,1,0:T(8,128)S(1)}, f32[32,32,256]{2,1,0:T(8,128)}, u32[]{:S(2)}) copy-start(f32[32,32,256]{2,1,0:T(8,128)} %join.2.refs_0_) | copy-start | bytes 3145732
  111.1 8.0 %collective-permute-start.3 = (f32[32,32,256]{2,1,0:T(8,128)}, f32[32,32,256]{2,1,0:T(8,128)S(1)}, u32[]{:S(2)}, u32[]{:S(2)}) collective-permute-start(f32[32,32,256]{2,1,0:T(8,128)} %join.2.refs_0_), channel_id=1, source_target_pairs={{0,1},{1,0},{2,3},{3,2},{4,5},{5,4},{6,7},{7,6},{8,9},{9,8},{10,11... | collective-permute-start | bytes 3145736 | tf_op jit(solution)/shard_map/ppermute | solution.py:483
  119.1 1.0 copy-start.5
  120.1 6.2 %copy-start.8 = (bf16[1,32,8,256]{3,2,1,0:T(8,128)(2,1)S(1)}, bf16[1,32,8,256]{3,2,1,0:T(8,128)(2,1)}, u32[]{:S(2)}) copy-start(bf16[1,32,8,256]{3,2,1,0:T(8,128)(2,1)} %get-tuple-element.23) | copy-start | bytes 393220
  120.2 56.9 %all-to-all-start.2 = ((s16[8,2,4,32,256]{4,3,2,1,0:T(8,128)(2,1)}), s16[8,2,4,32,256]{4,3,2,1,0:T(8,128)(2,1)S(1)}, u32[]{:S(2)}, u32[]{:S(2)}) async-start(s16[8,2,4,32,256]{4,3,2,1,0:T(8,128)(2,1)} %cross.3), calls=%async_computation.2 | async-start | bytes 2097152 | tf_op jit(solution)/shard_map/all_to_all | solution.py:464
  126.3 30.7 %collective-permute-start.4 = (bf16[2,32,8,256]{3,2,1,0:T(8,128)(2,1)S(1)}, bf16[2,32,8,256]{3,2,1,0:T(8,128)(2,1)S(1)}, u32[]{:S(2)}, u32[]{:S(2)}) collective-permute-start(bf16[2,32,8,256]{3,2,1,0:T(8,128)(2,1)S(1)} %pad_maximum_fusion.2), channel_id=1, source_target_pairs={{0,2},{2,4},{4,6},{6,8},{8,10},{10,12},{12,14},{1,3},{3,5},{5,7},{... | collective-permute-start | bytes 786440 | tf_op jit(solution)/shard_map/ppermute | solution.py:476
  129.5 27.6 %collective-permute-start.5 = (bf16[2,32,8,256]{3,2,1,0:T(8,128)(2,1)S(1)}, bf16[2,32,8,256]{3,2,1,0:T(8,128)(2,1)S(1)}, u32[]{:S(2)}, u32[]{:S(2)}) collective-permute-start(bf16[2,32,8,256]{3,2,1,0:T(8,128)(2,1)S(1)} %pad_maximum_fusion.3), channel_id=1, source_target_pairs={{2,0},{4,2},{6,4},{8,6},{10,8},{12,10},{14,12},{3,1},{5,3},{7,5},{... | collective-permute-start | bytes 786440 | tf_op jit(solution)/shard_map/ppermute | solution.py:477
  157.0 0.7 copy-start.13
  157.7 0.7 copy-start.14
  171.5 11.8 %collective-permute-start.6 = (f32[32,32,256]{2,1,0:T(8,128)}, f32[32,32,256]{2,1,0:T(8,128)}, u32[]{:S(2)}, u32[]{:S(2)}) collective-permute-start(f32[32,32,256]{2,1,0:T(8,128)} %get-tuple-element.17), channel_id=1, source_target_pairs={{0,1},{1,0},{2,3},{3,2},{4,5},{5,4},{6,7},{7,6},{8,9},{9,8},{10,11... | collective-permute-start | bytes 3145736 | tf_op jit(solution)/shard_map/ppermute | solution.py:483
  177.1 6.2 %copy-start.6 = (f32[32,32,256]{2,1,0:T(8,128)S(1)}, f32[32,32,256]{2,1,0:T(8,128)}, u32[]{:S(2)}) copy-start(f32[32,32,256]{2,1,0:T(8,128)} %get-tuple-element.17) | copy-start | bytes 3145732
  177.1 6.2 %copy-start.7 = (f32[32,32,256]{2,1,0:T(8,128)S(1)}, f32[32,32,256]{2,1,0:T(8,128)}, u32[]{:S(2)}) copy-start(f32[32,32,256]{2,1,0:T(8,128)} %get-tuple-element.16) | copy-start | bytes 3145732
  177.1 1.0 copy-start.2
where the time goes:
time: 187 us; the launch traced here: 186 us
  Pallas kernels  66.4 us (36%)
  waiting for transfers between devices  66 us (35%)
  starting transfers between devices  42.3 us (23%)
  local copies, waits for them, and re-layouts  5.89 us (3%)
  other arithmetic  4.4 us (2%)
    ppermute x2, waiting for transfers between devices, send_rims(): below = lax.ppermute(high, 'gz', [(i, i + 1) for i in range(count - 1)])  45.7 us
    all_to_all x4, starting transfers between devices, turn(): lax.all_to_all(payload, 'gz', split_axis=0, concat_axis=0, tiled=True)  26.5 us
    pallas_call x2, Pallas kernels, join(): pl.pallas_call(functools.partial(join_kernel, views, updated), grid=(slot...  24.9 us
    all_to_all x4, waiting for transfers between devices, turn(): lax.all_to_all(payload, 'gz', split_axis=0, concat_axis=0, tiled=True)  17.9 us
    pallas_call x2, Pallas kernels, crossed(): pl.pallas_call(cross_kernel, grid_spec=pltpu.PrefetchScalarGridSpec(num_s...  13.5 us
    pallas_call x2, Pallas kernels, last(): pl.pallas_call(last_kernel, grid_spec=pltpu.PrefetchScalarGridSpec(num_sc...  10.4 us
    pallas_call x2, Pallas kernels, first(): pl.pallas_call(first_kernel, grid_spec=pltpu.PrefetchScalarGridSpec(num_s...  10.2 us
    ppermute x2, starting transfers between devices, send_rims(): above = lax.ppermute(low, 'gz', [(i + 1, i) for i in range(count - 1)])  6.35 us
  transfers between devices with their start and end apart: 11, of which 5 were waited for; matrix products, arithmetic and copies ran while one was open for 2% of the time, Pallas kernels for 33%

commit v1 on v0

--- a/solution.py
+++ b/solution.py
@@ -383,9 +383,10 @@
     if updated:
         mine_ref, other_ref, *refs = refs
     (
+    place_ref,
     estimate_ref,
-    below_ref,
-    above_ref,
+    strips_ref,
+    swapped_ref,
     observed_ref,
     seen_below_ref,
     seen_above_ref,
@@ -411,10 +412,12 @@
         if updated:
             logs = mine_ref[...] + other_ref[...]
             now_ref[...] = estimate_ref[...] * jnp.exp(logs.reshape(depth, rows, width))
-        for rim_ref, start in ((below_ref, 0), (above_ref, blocks + 2)):
-            for b in range(2):
-                piece = rim_ref[b].astype(F32).reshape(size, width)
-                cells_ref[start + b] = piece.astype(BF16)
+        first_core = place_ref[0] == 0
+        for side, near, far in ((0, 1, 0), (1, blocks + 2, blocks + 3)):
+            own = strips_ref[side].astype(F32).reshape(size, width)
+            swapped = swapped_ref[side].astype(F32).reshape(size, width)
+            cells_ref[near] = jnp.where(first_core, own, swapped).astype(BF16)
+            cells_ref[far] = jnp.where(first_core, swapped, own).astype(BF16)
         for b in range(blocks):
             piece = now_ref[:, b * ROWS : (b + 1) * ROWS].reshape(size, width)
             cells_ref[b + 2] = piece.astype(BF16)
@@ -464,11 +467,8 @@
     return lax.all_to_all(payload, "gz", split_axis=0, concat_axis=0, tiled=True)
 
 
-def edges(field):
-    extent = field.shape[1]
-    low = [field[:, at : at + ROWS] for at in (0, ROWS)]
-    high = [field[:, at : at + ROWS] for at in (extent - 2 * ROWS, extent - ROWS)]
-    return jnp.stack(low), jnp.stack(high)
+def own_strip(near, far):
+    return jnp.where(lax.axis_index("view") == 0, near, far)
 
 
 def send_rims(low, high):
@@ -481,6 +481,11 @@
 def swap_cores(field):
     count = lax.axis_size("view")
     return lax.ppermute(field, "view", [(i, (i + 1) % count) for i in range(count)])
+
+
+def swap_strips(strips):
+    mine = jnp.stack(strips)
+    return mine, swap_cores(mine)
 
 
 def on_device(observed, initial, psf_taps, view_shifts, view_map):
@@ -496,9 +501,9 @@
     columns_forward, columns_inverse = column_tables(width, depth, length)
     row_turn, row_back = row_tables(length, depth, width)
 
-    low, high = edges(initial.astype(BF16))
-    low = jnp.concatenate([observed[:, :, :ROWS], low], 0)
-    high = jnp.concatenate([observed[:, :, rows - ROWS :], high], 0)
+    strips = [initial[:, at : at + ROWS].astype(BF16) for at in (0, ROWS, rows - 2 * ROWS, rows - ROWS)]
+    low = jnp.concatenate([observed[:, :, :ROWS], own_strip(strips[0], strips[1])[None]], 0)
+    high = jnp.concatenate([observed[:, :, rows - ROWS :], own_strip(strips[3], strips[2])[None]], 0)
     first_rims = send_rims(low, high)
 
     chunk = slots // 2
@@ -613,13 +618,9 @@
 
     forward, backward, columns = filters()
 
-    def join(estimate, below, above, logs=None):
+    def join(estimate, strips, rims, logs=None):
         def slot_block(shape):
             return pl.BlockSpec((1,) + shape, lambda s: (s,) + (0,) * len(shape))
-
-        def rim_block(rim):
-            at = rim.shape[0] // 2 - 1
-            return pl.BlockSpec((2, depth, ROWS, width), lambda s: (at, 0, 0, 0))
 
         updated = logs is not None
         field = jax.ShapeDtypeStruct((depth, rows, width), F32)
@@ -631,9 +632,10 @@
             grid=(slots,),
             in_specs=extra_specs
             + [
+                pl.BlockSpec(memory_space=pltpu.SMEM),
                 whole((depth, rows, width)),
-                rim_block(below),
-                rim_block(above),
+                whole((2, depth, ROWS, width)),
+                whole((2, depth, ROWS, width)),
                 slot_block((depth, rows, width)),
                 slot_block((depth, ROWS, width)),
                 slot_block((depth, ROWS, width)),
@@ -652,31 +654,32 @@
             ],
             cost_estimate=cost(2 * slots * size * width * ((blocks + 2) * (3 * size + 2 * width) + blocks * 3 * size), 12e6),
             name="join",
-        )(*(logs or ()), estimate, below, above, observed, *first_rims, forward, backward, columns)
+        )(*(logs or ()), place, estimate, *strips, observed, *rims, forward, backward, columns)
 
     sent_a = turn(first(0))
     payload_b = first(chunk)
     sent_b = turn(payload_b)
     mine = reference_spectrum(sent_a)
     other = swap_cores(mine)
-    crossed_a, start = lax.optimization_barrier((crossed(sent_a, mine, other), initial))
+    first_rims, crossed_a = lax.optimization_barrier((first_rims, crossed(sent_a, mine, other)))
     back_a = turn(crossed_a)
-
-    (logs,) = join(start, *first_rims)
-    logs, late = lax.optimization_barrier((logs, sent_b))
+    first_strips = swap_strips([rim[slots] for rim in first_rims])
+
+    (logs,) = join(initial, first_strips, first_rims)
     total = (logs, swap_cores(logs))
-    crossed_b = crossed(late, mine, other)
 
     def updated_rows(at):
         window = [lax.slice_in_dim(part, at, at + ROWS, axis=1) for part in (initial, *total)]
         return (window[0] * jnp.exp(window[1] + window[2])).astype(BF16)
 
-    low = jnp.stack([updated_rows(at) for at in (0, ROWS)])
-    high = jnp.stack([updated_rows(at) for at in (rows - 2 * ROWS, rows - ROWS)])
-    rims = send_rims(low, high)
+    strips = [updated_rows(at) for at in (0, ROWS, rows - 2 * ROWS, rows - ROWS)]
+    rims = send_rims(own_strip(strips[0], strips[1]), own_strip(strips[3], strips[2]))
+    crossed_b = crossed(sent_b, mine, other)
+    strips = swap_strips(rims)
     back_b = turn(crossed_b)
-    logs, estimate = join(initial, *rims, logs=total)
-    estimate = estimate * jnp.exp(logs + swap_cores(logs))
+    logs, estimate = join(initial, strips, first_rims, logs=total)
+    swapped = swap_cores(logs)
+    estimate = estimate * jnp.exp(logs + swapped)
 
     surfaces = last(back_a, 0, None)
     surfaces = last(back_b, chunk, surfaces)

time: 187 us -> 170 us (0.909)
  the two profiles are of different devices: /device:TPU:17 before, /device:TPU:0 now
where the time goes in v1:
time: 170 us; the launch traced here: 169 us
  Pallas kernels  66.6 us (39%)
  waiting for transfers between devices  52.8 us (31%)
  starting transfers between devices  37.4 us (22%)
  local copies, waits for them, and re-layouts  6.04 us (4%)
  other arithmetic  5.03 us (3%)
    all_to_all x4, starting transfers between devices, turn(): lax.all_to_all(payload, 'gz', split_axis=0, concat_axis=0, tiled=True)  26.3 us
    all_to_all x4, waiting for transfers between devices, turn(): lax.all_to_all(payload, 'gz', split_axis=0, concat_axis=0, tiled=True)  25.4 us
    pallas_call x2, Pallas kernels, join(): pl.pallas_call(functools.partial(join_kernel, views, updated), grid=(slot...  25.2 us
    ppermute x2, waiting for transfers between devices, send_rims(): below = lax.ppermute(high, 'gz', [(i, i + 1) for i in range(count - 1)])  23.2 us
    pallas_call x2, Pallas kernels, crossed(): pl.pallas_call(cross_kernel, grid_spec=pltpu.PrefetchScalarGridSpec(num_s...  13.5 us
    pallas_call x2, Pallas kernels, last(): pl.pallas_call(last_kernel, grid_spec=pltpu.PrefetchScalarGridSpec(num_sc...  10.2 us
    pallas_call x2, Pallas kernels, first(): pl.pallas_call(first_kernel, grid_spec=pltpu.PrefetchScalarGridSpec(num_s...  10.2 us
    ppermute x2, starting transfers between devices, send_rims(): below = lax.ppermute(high, 'gz', [(i, i + 1) for i in range(count - 1)])  7.89 us
  transfers between devices with their start and end apart: 13, of which 5 were waited for; matrix products, arithmetic and copies ran while one was open for 4% of the time, Pallas kernels for 36%

profile of v1, /device:TPU:0, one launch (start us, length us, event | category | flops | bytes accessed | tf_op | source)
XLA Modules:
  0.0 168.7 jit_solution(6527455022754092505)
XLA Ops:
  0.6 5.1 %first.2 = s16[8,2,4,32,256]{4,3,2,1,0:T(8,128)(2,1)} custom-call(s32[8]{0:T(128)} %map_ref.13, bf16[4,32,32,256]{3,2,1,0:T(8,128)(2,1)} %observed_ref.3, bf16[256,512]{1,0:T(8,128)(2,1)} %constant.18.clone.columns_ref), custom_call_target="tpu_custom_call" | custom-call | flops 2147483648 | bytes 2097152 | tf_op jit(solution)/shard_map/first/pallas_call | solution.py:516
  5.7 7.3 %all-to-all-start = ((s16[8,2,4,32,256]{4,3,2,1,0:T(8,128)(2,1)}), s16[8,2,4,32,256]{4,3,2,1,0:T(8,128)(2,1)S(1)}, u32[]{:S(2)}, u32[]{:S(2)}) async-start(s16[8,2,4,32,256]{4,3,2,1,0:T(8,128)(2,1)} %first.2), calls=%async_computation | async-start | bytes 2097152 | tf_op jit(solution)/shard_map/all_to_all | solution.py:467
  13.0 5.1 %first.3 = s16[8,2,4,32,256]{4,3,2,1,0:T(8,128)(2,1)} custom-call(s32[8]{0:T(128)} %map_ref.13, bf16[4,32,32,256]{3,2,1,0:T(8,128)(2,1)} %observed_ref.3, bf16[256,512]{1,0:T(8,128)(2,1)} %constant.18.clone.columns_ref), custom_call_target="tpu_custom_call" | custom-call | flops 2147483648 | bytes 2097152 | tf_op jit(solution)/shard_map/first/pallas_call | solution.py:516
  18.1 20.7 %all-to-all-done.in_ref = s16[8,2,4,32,256]{4,3,2,1,0:T(8,128)(2,1)S(1)} async-done(((s16[8,2,4,32,256]{4,3,2,1,0:T(8,128)(2,1)}), s16[8,2,4,32,256]{4,3,2,1,0:T(8,128)(2,1)S(1)}, u32[]{:S(2)}, u32[]{:S(2)}) %all-to-all-start) | async-done | bytes 1048608 | tf_op jit(solution)/shard_map/all_to_all | solution.py:467
  38.8 3.6 %all-to-all-start.1 = ((s16[8,2,4,32,256]{4,3,2,1,0:T(8,128)(2,1)}), s16[8,2,4,32,256]{4,3,2,1,0:T(8,128)(2,1)S(1)}, u32[]{:S(2)}, u32[]{:S(2)}) async-start(s16[8,2,4,32,256]{4,3,2,1,0:T(8,128)(2,1)} %first.3), calls=%async_computation.1 | async-start | bytes 2097152 | tf_op jit(solution)/shard_map/all_to_all | solution.py:467
  42.9 3.4 %spectrum.1.mine_ref = f32[4,256,256]{2,1,0:T(8,128)} custom-call(s32[2]{0:T(128)} %pad_add_fusion.place_ref.refs_0_.refs_2_, s16[8,2,4,32,256]{4,3,2,1,0:T(8,128)(2,1)} %copy-done.1, bf16[256,512]{1,0:T(8,128)(2,1)} %constant.20.clone.rows_ref), custom_call_target="tpu_custom_call" | custom-call | flops 402653184 | bytes 1572864 | tf_op jit(solution)/shard_map/spectrum/pallas_call | solution.py:537
  46.4 1.3 fusion.18
  47.8 4.0 %collective-permute-start = (bf16[5,32,8,256]{3,2,1,0:T(8,128)(2,1)S(1)}, bf16[5,32,8,256]{3,2,1,0:T(8,128)(2,1)S(1)}, u32[]{:S(2)}, u32[]{:S(2)}) collective-permute-start(bf16[5,32,8,256]{3,2,1,0:T(8,128)(2,1)S(1)} %pad_maximum_fusion), channel_id=1, source_target_pairs={{0,2},{2,4},{4,6},{6,8},{8,10},{10,12},{12,14},{1,3},{3,5},{5,7},{... | collective-permute-start | bytes 1966088 | tf_op jit(solution)/shard_map/ppermute | solution.py:476
  51.8 1.3 collective-permute-start.1
  53.1 6.8 %cross.2 = s16[8,2,4,32,256]{4,3,2,1,0:T(8,128)(2,1)} custom-call(s32[8]{0:T(128)} %map_ref.13, s32[2]{0:T(128)} %pad_add_fusion.place_ref.refs_0_.refs_2_, s16[8,2,4,32,256]{4,3,2,1,0:T(8,128)(2,1)} %copy-done.1, bf16[256,512]{1,0:T(8,128)(2,1)} %constant.20.clone.rows_ref, bf16[256,512]{1,0:T(8,128)(2,1)} %constant.21.clone.back_ref, ...), custom_call_target="tpu_custom_call" | custom-call | flops 1610612736 | bytes 4718592 | tf_op jit(solution)/shard_map/cross/pallas_call | solution.py:554
  59.9 23.2 %collective-permute-done.refs_5_.refs_7_ = bf16[5,32,8,256]{3,2,1,0:T(8,128)(2,1)S(1)} collective-permute-done((bf16[5,32,8,256]{3,2,1,0:T(8,128)(2,1)S(1)}, bf16[5,32,8,256]{3,2,1,0:T(8,128)(2,1)S(1)}, u32[]{:S(2)}, u32[]{:S(2)}) %collective-permute-start) | collective-permute-done | bytes 655392 | tf_op jit(solution)/shard_map/ppermute | solution.py:476
  83.2 1.1 slice.59
  84.4 0.6 copy.13.psf_ref
  85.0 0.7 copy.12.shift_ref
  85.7 4.0 %filters.1 = (bf16[4,256,768]{2,1,0:T(8,128)(2,1)}, bf16[4,256,768]{2,1,0:T(8,128)(2,1)}, bf16[4,256,256]{2,1,0:T(8,128)(2,1)}) custom-call(s32[2]{0:T(128)} %pad_add_fusion.place_ref.refs_0_.refs_2_, s32[8]{0:T(128)} %map_ref.13, s32[8,2]{1,0:T(8,128)} %copy.12.shift_ref, f32[8,3,15]{2,1,0:T(4,128)} %copy.13.psf_ref), custom_call_target="tpu_custom_call" | custom-call | flops 15728640 | bytes 3670016 | tf_op jit(solution)/shard_map/filters/pallas_call | solution.py:601
  89.7 8.7 %all-to-all-start.3 = ((s16[8,2,4,32,256]{4,3,2,1,0:T(8,128)(2,1)}), s16[8,2,4,32,256]{4,3,2,1,0:T(8,128)(2,1)S(1)}, u32[]{:S(2)}, u32[]{:S(2)}) async-start(s16[8,2,4,32,256]{4,3,2,1,0:T(8,128)(2,1)} %cross.2), calls=%async_computation.3 | async-start | bytes 2097152 | tf_op jit(solution)/shard_map/all_to_all | solution.py:467
  98.5 0.7 copy-done.14
  99.2 12.0 %join.2.refs_0_ = f32[32,32,256]{2,1,0:T(8,128)} custom-call(s32[2]{0:T(128)} %pad_add_fusion.place_ref.refs_0_.refs_2_, f32[32,32,256]{2,1,0:T(8,128)} %refs_3_.1, bf16[2,32,8,256]{3,2,1,0:T(8,128)(2,1)} %copy-done.9, bf16[2,32,8,256]{3,2,1,0:T(8,128)(2,1)} %copy-done.14, bf16[4,32,32,256]{3,2,1,0:T(8,128)(2,1)} %observed_ref.3, ...), custom_call_target="tpu_custom_call" | custom-call | flops 5637144576 | bytes 12000000 | tf_op jit(solution)/shard_map/join/pallas_call | solution.py:630
  111.5 2.7 %collective-permute-done.4.refs_1_ = f32[32,32,256]{2,1,0:T(8,128)S(1)} collective-permute-done((f32[32,32,256]{2,1,0:T(8,128)}, f32[32,32,256]{2,1,0:T(8,128)S(1)}, u32[]{:S(2)}, u32[]{:S(2)}) %collective-permute-start.4) | collective-permute-done | bytes 1048608 | tf_op jit(solution)/shard_map/ppermute | solution.py:483
  114.1 1.8 %fusion.16 = (bf16[32,8,256]{2,1,0:T(8,128)(2,1)S(1)}, bf16[32,8,256]{2,1,0:T(8,128)(2,1)S(1)}) fusion(f32[32,32,256]{2,1,0:T(8,128)S(1)} %collective-permute-done.4.refs_1_, f32[32,32,256]{2,1,0:T(8,128)} %join.2.refs_0_, f32[32,32,256]{2,1,0:T(8,128)S(1)} %copy-done.3, pred[]{:T(512)S(6)} %eq.2), kind=kLoop, calls=%fused_computation.29 | loop fusion | flops 917504 | bytes 3407873 | tf_op jit(solution)/shard_map/jit(_where)/select_n | solution.py:471
  115.9 3.9 %collective-permute-start.5 = (bf16[32,8,256]{2,1,0:T(8,128)(2,1)S(1)}, bf16[32,8,256]{2,1,0:T(8,128)(2,1)S(1)}, u32[]{:S(2)}, u32[]{:S(2)}) collective-permute-start(bf16[32,8,256]{2,1,0:T(8,128)(2,1)S(1)} %get-tuple-element.18), channel_id=1, source_target_pairs={{0,2},{2,4},{4,6},{6,8},{8,10},{10,12},{12,14},{1,3},{3,5},{5,7},{... | collective-permute-start | bytes 393224 | tf_op jit(solution)/shard_map/ppermute | solution.py:476
  119.9 1.3 collective-permute-start.6
  121.2 6.8 %cross.3 = s16[8,2,4,32,256]{4,3,2,1,0:T(8,128)(2,1)} custom-call(s32[8]{0:T(128)} %map_ref.13, s32[2]{0:T(128)} %pad_add_fusion.place_ref.refs_0_.refs_2_, s16[8,2,4,32,256]{4,3,2,1,0:T(8,128)(2,1)} %copy-done.4, bf16[256,512]{1,0:T(8,128)(2,1)} %constant.20.clone.rows_ref, bf16[256,512]{1,0:T(8,128)(2,1)} %constant.21.clone.back_ref, ...), custom_call_target="tpu_custom_call" | custom-call | flops 1610612736 | bytes 4718592 | tf_op jit(solution)/shard_map/cross/pallas_call | solution.py:554
  127.9 6.6 %all-to-all-start.2 = ((s16[8,2,4,32,256]{4,3,2,1,0:T(8,128)(2,1)}), s16[8,2,4,32,256]{4,3,2,1,0:T(8,128)(2,1)S(1)}, u32[]{:S(2)}, u32[]{:S(2)}) async-start(s16[8,2,4,32,256]{4,3,2,1,0:T(8,128)(2,1)} %cross.3), calls=%async_computation.2 | async-start | bytes 2097152 | tf_op jit(solution)/shard_map/all_to_all | solution.py:467
  134.7 1.5 collective-permute-done.7.refs_5_
  136.2 0.7 copy-done.15
  136.9 13.2 %join.3 = (f32[32,32,256]{2,1,0:T(8,128)}, f32[32,32,256]{2,1,0:T(8,128)}) custom-call(f32[32,32,256]{2,1,0:T(8,128)} %join.2.refs_0_, f32[32,32,256]{2,1,0:T(8,128)} %copy-done.6, s32[2]{0:T(128)} %pad_add_fusion.place_ref.refs_0_.refs_2_, f32[32,32,256]{2,1,0:T(8,128)} %refs_3_.1, bf16[2,32,8,256]{3,2,1,0:T(8,128)(2,1)} %copy-done.10, ...), custom_call_target="tpu_custom_call" | custom-call | flops 5637144576 | bytes 12000000 | tf_op jit(solution)/shard_map/join/pallas_call | solution.py:630
  150.3 5.1 %last.2.rest_0_ = f32[4,32,32,256]{3,2,1,0:T(8,128)} custom-call(s32[8]{0:T(128)} %map_ref.13, s16[8,2,4,32,256]{4,3,2,1,0:T(8,128)(2,1)} %copy-done.5, bf16[256,512]{1,0:T(8,128)(2,1)} %constant.19.clone.columns_ref), custom_call_target="tpu_custom_call" | custom-call | flops 2415919104 | bytes 3145728 | tf_op jit(solution)/shard_map/last/pallas_call | solution.py:584
  155.4 4.7 %all-to-all-done.2.in_ref = s16[8,2,4,32,256]{4,3,2,1,0:T(8,128)(2,1)S(1)} async-done(((s16[8,2,4,32,256]{4,3,2,1,0:T(8,128)(2,1)}), s16[8,2,4,32,256]{4,3,2,1,0:T(8,128)(2,1)S(1)}, u32[]{:S(2)}, u32[]{:S(2)}) %all-to-all-start.2) | async-done | bytes 1048608 | tf_op jit(solution)/shard_map/all_to_all | solution.py:467
  160.2 1.0 copy-done
  161.1 5.1 %last.3 = f32[4,32,32,256]{3,2,1,0:T(8,128)} custom-call(s32[8]{0:T(128)} %map_ref.13, s16[8,2,4,32,256]{4,3,2,1,0:T(8,128)(2,1)} %copy-done, bf16[256,512]{1,0:T(8,128)(2,1)} %constant.19.clone.columns_ref, f32[4,32,32,256]{3,2,1,0:T(8,128)} %last.2.rest_0_), custom_call_target="tpu_custom_call", output_to_operand_aliasing={{}: (3, {})} | custom-call | flops 2415919104 | bytes 3145728 | tf_op jit(solution)/shard_map/last/pallas_call | solution.py:584
  166.3 2.5 %exponential_multiply_fusion = f32[32,32,256]{2,1,0:T(8,128)} fusion(f32[32,32,256]{2,1,0:T(8,128)S(1)} %copy-done.8, f32[32,32,256]{2,1,0:T(8,128)S(1)} %copy-done.7, f32[32,32,256]{2,1,0:T(8,128)} %collective-permute-done.8), kind=kLoop, calls=%fused_computation | loop fusion | flops 524288 | bytes 4194304 | tf_op jit(solution)/shard_map/mul | solution.py:682
  (49 shorter events, 1.5 us)
Async XLA Ops:
  5.7 33.1 %all-to-all-start = ((s16[8,2,4,32,256]{4,3,2,1,0:T(8,128)(2,1)}), s16[8,2,4,32,256]{4,3,2,1,0:T(8,128)(2,1)S(1)}, u32[]{:S(2)}, u32[]{:S(2)}) async-start(s16[8,2,4,32,256]{4,3,2,1,0:T(8,128)(2,1)} %first.2), calls=%async_computation | async-start | bytes 2097152 | tf_op jit(solution)/shard_map/all_to_all | solution.py:467
  18.1 28.3 %copy-start.2 = (f32[32,32,256]{2,1,0:T(8,128)S(1)}, f32[32,32,256]{2,1,0:T(8,128)}, u32[]{:S(2)}) copy-start(f32[32,32,256]{2,1,0:T(8,128)} %refs_3_.1) | copy-start | bytes 3145732
  38.8 4.2 %copy-start.1 = (s16[8,2,4,32,256]{4,3,2,1,0:T(8,128)(2,1)}, s16[8,2,4,32,256]{4,3,2,1,0:T(8,128)(2,1)S(1)}, u32[]{:S(2)}) copy-start(s16[8,2,4,32,256]{4,3,2,1,0:T(8,128)(2,1)S(1)} %all-to-all-done.in_ref) | copy-start | bytes 3145732
  38.8 50.9 %all-to-all-start.1 = ((s16[8,2,4,32,256]{4,3,2,1,0:T(8,128)(2,1)}), s16[8,2,4,32,256]{4,3,2,1,0:T(8,128)(2,1)S(1)}, u32[]{:S(2)}, u32[]{:S(2)}) async-start(s16[8,2,4,32,256]{4,3,2,1,0:T(8,128)(2,1)} %first.3), calls=%async_computation.1 | async-start | bytes 2097152 | tf_op jit(solution)/shard_map/all_to_all | solution.py:467
  46.4 6.8 %collective-permute-start.2 = (f32[4,256,256]{2,1,0:T(8,128)}, f32[4,256,256]{2,1,0:T(8,128)}, u32[]{:S(2)}, u32[]{:S(2)}) collective-permute-start(f32[4,256,256]{2,1,0:T(8,128)} %spectrum.1.mine_ref), channel_id=1, source_target_pairs={{0,1},{1,0},{2,3},{3,2},{4,5},{5,4},{6,7},{7,6},{8,9},{9,8},{10,11... | collective-permute-start | bytes 3145736 | tf_op jit(solution)/shard_map/ppermute | solution.py:483
  47.8 35.4 %collective-permute-start = (bf16[5,32,8,256]{3,2,1,0:T(8,128)(2,1)S(1)}, bf16[5,32,8,256]{3,2,1,0:T(8,128)(2,1)S(1)}, u32[]{:S(2)}, u32[]{:S(2)}) collective-permute-start(bf16[5,32,8,256]{3,2,1,0:T(8,128)(2,1)S(1)} %pad_maximum_fusion), channel_id=1, source_target_pairs={{0,2},{2,4},{4,6},{6,8},{8,10},{10,12},{12,14},{1,3},{3,5},{5,7},{... | collective-permute-start | bytes 1966088 | tf_op jit(solution)/shard_map/ppermute | solution.py:476
  51.8 32.6 %copy-start.12 = (f32[8,3,15]{2,0,1:T(8,128)S(1)}, f32[8,3,15]{2,0,1:T(8,128)}, u32[]{:S(2)}) copy-start(f32[8,3,15]{2,0,1:T(8,128)} %param.11) | copy-start | bytes 4324
  51.8 33.2 %copy-start.13 = (s32[8,2]{0,1:T(2,128)S(1)}, s32[8,2]{0,1:T(2,128)}, u32[]{:S(2)}) copy-start(s32[8,2]{0,1:T(2,128)} %param.12) | copy-start | bytes 196
  51.8 31.3 %collective-permute-start.1 = (bf16[5,32,8,256]{3,2,1,0:T(8,128)(2,1)S(1)}, bf16[5,32,8,256]{3,2,1,0:T(8,128)(2,1)}, u32[]{:S(2)}, u32[]{:S(2)}) collective-permute-start(bf16[5,32,8,256]{3,2,1,0:T(8,128)(2,1)S(1)} %pad_maximum_fusion.1), channel_id=1, source_target_pairs={{2,0},{4,2},{6,4},{8,6},{10,8},{12,10},{14,12},{3,1},{5,3},{7,5},{... | collective-permute-start | bytes 1966088 | tf_op jit(solution)/shard_map/ppermute | solution.py:477
  83.2 15.3 %copy-start.11 = (bf16[5,32,8,256]{3,2,1,0:T(8,128)(2,1)}, bf16[5,32,8,256]{3,2,1,0:T(8,128)(2,1)S(1)}, u32[]{:S(2)}) copy-start(bf16[5,32,8,256]{3,2,1,0:T(8,128)(2,1)S(1)} %collective-permute-done.refs_5_.refs_7_) | copy-start | bytes 1966084
  84.3 14.9 %copy-start.9 = (bf16[2,32,8,256]{3,2,1,0:T(8,128)(2,1)}, bf16[2,32,8,256]{3,2,1,0:T(8,128)(2,1)S(1)}, u32[]{:S(2)}) copy-start(bf16[2,32,8,256]{3,2,1,0:T(8,128)(2,1)S(1)} %pad_maximum_fusion.2.refs_2_) | copy-start | bytes 786436
  84.3 14.2 %collective-permute-start.3 = (bf16[2,32,8,256]{3,2,1,0:T(8,128)(2,1)S(1)}, bf16[2,32,8,256]{3,2,1,0:T(8,128)(2,1)S(1)}, u32[]{:S(2)}, u32[]{:S(2)}) collective-permute-start(bf16[2,32,8,256]{3,2,1,0:T(8,128)(2,1)S(1)} %pad_maximum_fusion.2.refs_2_), channel_id=1, source_target_pairs={{0,1},{1,0},{2,3},{3,2},{4,5},{5,4},{6,7},{7,6},{8,9},{9,8},{10,11... | collective-permute-start | bytes 786440 | tf_op jit(solution)/shard_map/ppermute | solution.py:483
  89.7 21.5 %copy-start.4 = (s16[8,2,4,32,256]{4,3,2,1,0:T(8,128)(2,1)}, s16[8,2,4,32,256]{4,3,2,1,0:T(8,128)(2,1)S(1)}, u32[]{:S(2)}) copy-start(s16[8,2,4,32,256]{4,3,2,1,0:T(8,128)(2,1)S(1)} %all-to-all-done.1.in_ref) | copy-start | bytes 3145732
  89.7 38.2 %all-to-all-start.3 = ((s16[8,2,4,32,256]{4,3,2,1,0:T(8,128)(2,1)}), s16[8,2,4,32,256]{4,3,2,1,0:T(8,128)(2,1)S(1)}, u32[]{:S(2)}, u32[]{:S(2)}) async-start(s16[8,2,4,32,256]{4,3,2,1,0:T(8,128)(2,1)} %cross.2), calls=%async_computation.3 | async-start | bytes 2097152 | tf_op jit(solution)/shard_map/all_to_all | solution.py:467
  98.5 0.7 copy-start.14
  99.2 15.0 %copy-start.3 = (f32[32,32,256]{2,1,0:T(8,128)S(1)}, f32[32,32,256]{2,1,0:T(8,128)}, u32[]{:S(2)}) copy-start(f32[32,32,256]{2,1,0:T(8,128)} %refs_3_.1) | copy-start | bytes 3145732
  111.2 2.9 %collective-permute-start.4 = (f32[32,32,256]{2,1,0:T(8,128)}, f32[32,32,256]{2,1,0:T(8,128)S(1)}, u32[]{:S(2)}, u32[]{:S(2)}) collective-permute-start(f32[32,32,256]{2,1,0:T(8,128)} %join.2.refs_0_), channel_id=1, source_target_pairs={{0,1},{1,0},{2,3},{3,2},{4,5},{5,4},{6,7},{7,6},{8,9},{9,8},{10,11... | collective-permute-start | bytes 3145736 | tf_op jit(solution)/shard_map/ppermute | solution.py:483
  114.1 1.8 %copy-start.6 = (f32[32,32,256]{2,1,0:T(8,128)}, f32[32,32,256]{2,1,0:T(8,128)S(1)}, u32[]{:S(2)}) copy-start(f32[32,32,256]{2,1,0:T(8,128)S(1)} %collective-permute-done.4.refs_1_) | copy-start | bytes 3145732
  115.9 18.6 %collective-permute-start.5 = (bf16[32,8,256]{2,1,0:T(8,128)(2,1)S(1)}, bf16[32,8,256]{2,1,0:T(8,128)(2,1)S(1)}, u32[]{:S(2)}, u32[]{:S(2)}) collective-permute-start(bf16[32,8,256]{2,1,0:T(8,128)(2,1)S(1)} %get-tuple-element.18), channel_id=1, source_target_pairs={{0,2},{2,4},{4,6},{6,8},{8,10},{10,12},{12,14},{1,3},{3,5},{5,7},{... | collective-permute-start | bytes 393224 | tf_op jit(solution)/shard_map/ppermute | solution.py:476
  119.9 14.7 %collective-permute-start.6 = (bf16[32,8,256]{2,1,0:T(8,128)(2,1)S(1)}, bf16[32,8,256]{2,1,0:T(8,128)(2,1)S(1)}, u32[]{:S(2)}, u32[]{:S(2)}) collective-permute-start(bf16[32,8,256]{2,1,0:T(8,128)(2,1)S(1)} %get-tuple-element.19), channel_id=1, source_target_pairs={{2,0},{4,2},{6,4},{8,6},{10,8},{12,10},{14,12},{3,1},{5,3},{7,5},{... | collective-permute-start | bytes 393224 | tf_op jit(solution)/shard_map/ppermute | solution.py:477
  127.9 22.2 %copy-start.5 = (s16[8,2,4,32,256]{4,3,2,1,0:T(8,128)(2,1)}, s16[8,2,4,32,256]{4,3,2,1,0:T(8,128)(2,1)S(1)}, u32[]{:S(2)}) copy-start(s16[8,2,4,32,256]{4,3,2,1,0:T(8,128)(2,1)S(1)} %all-to-all-done.3.in_ref) | copy-start | bytes 3145732
  127.9 32.2 %all-to-all-start.2 = ((s16[8,2,4,32,256]{4,3,2,1,0:T(8,128)(2,1)}), s16[8,2,4,32,256]{4,3,2,1,0:T(8,128)(2,1)S(1)}, u32[]{:S(2)}, u32[]{:S(2)}) async-start(s16[8,2,4,32,256]{4,3,2,1,0:T(8,128)(2,1)} %cross.3), calls=%async_computation.2 | async-start | bytes 2097152 | tf_op jit(solution)/shard_map/all_to_all | solution.py:467
  134.6 1.6 copy-start.10
  134.6 1.6 collective-permute-start.7
  136.2 0.7 copy-start.15
  150.1 16.1 %collective-permute-start.8 = (f32[32,32,256]{2,1,0:T(8,128)}, f32[32,32,256]{2,1,0:T(8,128)}, u32[]{:S(2)}, u32[]{:S(2)}) collective-permute-start(f32[32,32,256]{2,1,0:T(8,128)} %get-tuple-element.16), channel_id=1, source_target_pairs={{0,1},{1,0},{2,3},{3,2},{4,5},{5,4},{6,7},{7,6},{8,9},{9,8},{10,11... | collective-permute-start | bytes 3145736 | tf_op jit(solution)/shard_map/ppermute | solution.py:483
  155.4 10.8 %copy-start.7 = (f32[32,32,256]{2,1,0:T(8,128)S(1)}, f32[32,32,256]{2,1,0:T(8,128)}, u32[]{:S(2)}) copy-start(f32[32,32,256]{2,1,0:T(8,128)} %get-tuple-element.16) | copy-start | bytes 3145732
  155.4 10.8 %copy-start.8 = (f32[32,32,256]{2,1,0:T(8,128)S(1)}, f32[32,32,256]{2,1,0:T(8,128)}, u32[]{:S(2)}) copy-start(f32[32,32,256]{2,1,0:T(8,128)} %get-tuple-element.15) | copy-start | bytes 3145732
  160.2 1.0 copy-start

commit v2 on v1

--- a/solution.py
+++ b/solution.py
@@ -526,6 +526,7 @@
                 scratch_shapes=[pltpu.VMEM((depth, rows, width), F32)] * 2,
             ),
             out_shape=jax.ShapeDtypeStruct(payload_shape, jnp.int16),
+            compiler_params=pltpu.CompilerParams(vmem_limit_bytes=28 * 1024 * 1024),
             cost_estimate=cost(2 * chunk * volume * 8 * width, payload_bytes),
             name="first",
         )(view_map, observed, columns_forward)
@@ -546,6 +547,7 @@
                 out_specs=whole(spectrum_shape),
             ),
             out_shape=jax.ShapeDtypeStruct(spectrum_shape, F32),
+            compiler_params=pltpu.CompilerParams(vmem_limit_bytes=28 * 1024 * 1024),
             cost_estimate=cost(row_flops, 6 * volume),
             name="spectrum",
         )(place, payload, row_turn)
@@ -566,6 +568,7 @@
                 out_specs=pl.BlockSpec(payload_block, lambda *a: (0, a[0], 0, 0, 0)),
             ),
             out_shape=jax.ShapeDtypeStruct(payload_shape, jnp.int16),
+            compiler_params=pltpu.CompilerParams(vmem_limit_bytes=28 * 1024 * 1024),
             cost_estimate=cost(2 * row_flops * chunk, payload_bytes + 10 * volume),
             name="cross",
         )(view_map, place, payload, row_turn, row_back, mine, other)
@@ -592,6 +595,7 @@
             ),
             out_shape=jax.ShapeDtypeStruct((slots, depth, rows, width), F32),
             input_output_aliases=aliases,
+            compiler_params=pltpu.CompilerParams(vmem_limit_bytes=28 * 1024 * 1024),
             cost_estimate=cost(2 * chunk * volume * 9 * width, payload_bytes * 1.5),
             name="last",
         )(*operands)
@@ -612,6 +616,7 @@
                 jax.ShapeDtypeStruct((slots, size, 3 * size), BF16),
                 jax.ShapeDtypeStruct((slots, width, width), BF16),
             ],
+            compiler_params=pltpu.CompilerParams(vmem_limit_bytes=28 * 1024 * 1024),
             cost_estimate=cost(slots * size * size * 60, slots * size * size * 14),
             name="filters",
         )(place, view_map, view_shifts, psf_taps)
@@ -652,6 +657,7 @@
                 pltpu.VMEM((blocks + 2, size, width), BF16),
                 pltpu.VMEM((blocks, size, width), F32),
             ],
+            compiler_params=pltpu.CompilerParams(vmem_limit_bytes=28 * 1024 * 1024),
             cost_estimate=cost(2 * slots * size * width * ((blocks + 2) * (3 * size + 2 * width) + blocks * 3 * size), 12e6),
             name="join",
         )(*(logs or ()), place, estimate, *strips, observed, *rims, forward, backward, columns)

time: 170 us -> 177 us (1.041)
  local copies, waits for them, and re-layouts: 6.04 us -> 31.5 us
  Pallas kernels: 66.6 us -> 48.5 us
    unnamed x34 -> x88, local copies, waits for them, and re-layouts: 3.67 us -> 31.4 us
    pallas_call x2, Pallas kernels: 25.2 us -> 19.3 us  [join(): pl.pallas_call(functools.partial(join_kernel, views, updated), grid=(slot...]
    all_to_all x4, waiting for transfers between devices: 25.4 us -> 20.3 us  [turn(): lax.all_to_all(payload, 'gz', split_axis=0, concat_axis=0, tiled=True)]
    pallas_call x2, Pallas kernels: 13.5 us -> 9.18 us  [crossed(): pl.pallas_call(cross_kernel, grid_spec=pltpu.PrefetchScalarGridSpec(num_s...]
    ppermute x2, waiting for transfers between devices: 23.2 us -> 26.8 us  [send_rims(): below = lax.ppermute(high, 'gz', [(i, i + 1) for i in range(count - 1)])]
    pallas_call x2, Pallas kernels: 10.2 us -> 7.62 us  [first(): pl.pallas_call(first_kernel, grid_spec=pltpu.PrefetchScalarGridSpec(num_s...]
    pallas_call x2, Pallas kernels: 10.2 us -> 7.92 us  [last(): pl.pallas_call(last_kernel, grid_spec=pltpu.PrefetchScalarGridSpec(num_sc...]
    pallas_call x1, Pallas kernels: 3.43 us -> 1.21 us  [reference_spectrum(): pl.pallas_call(spectrum_kernel, grid_spec=pltpu.PrefetchScalarGridSpec(nu...]
  transfers between devices with their start and end apart: 13 -> 13, of which waited for: 5 -> 4; matrix products, arithmetic and copies ran while one was open for 4% -> 2% of each run, Pallas kernels for 36% -> 25%
where the time goes in v2:
time: 177 us; the launch traced here: 176 us
  waiting for transfers between devices  51.1 us (29%)
  Pallas kernels  48.5 us (27%)
  starting transfers between devices  38.7 us (22%)
  local copies, waits for them, and re-layouts  31.5 us (18%)
  other arithmetic  5.36 us (3%)
    unnamed x88, local copies, waits for them, and re-layouts  31.4 us
    all_to_all x4, starting transfers between devices, turn(): lax.all_to_all(payload, 'gz', split_axis=0, concat_axis=0, tiled=True)  27.2 us
    ppermute x2, waiting for transfers between devices, send_rims(): below = lax.ppermute(high, 'gz', [(i, i + 1) for i in range(count - 1)])  26.8 us
    all_to_all x4, waiting for transfers between devices, turn(): lax.all_to_all(payload, 'gz', split_axis=0, concat_axis=0, tiled=True)  20.3 us
    pallas_call x2, Pallas kernels, join(): pl.pallas_call(functools.partial(join_kernel, views, updated), grid=(slot...  19.3 us
    pallas_call x2, Pallas kernels, crossed(): pl.pallas_call(cross_kernel, grid_spec=pltpu.PrefetchScalarGridSpec(num_s...  9.18 us
    ppermute x2, starting transfers between devices, send_rims(): below = lax.ppermute(high, 'gz', [(i, i + 1) for i in range(count - 1)])  8.4 us
    pallas_call x2, Pallas kernels, last(): pl.pallas_call(last_kernel, grid_spec=pltpu.PrefetchScalarGridSpec(num_sc...  7.92 us
  transfers between devices with their start and end apart: 13, of which 4 were waited for; matrix products, arithmetic and copies ran while one was open for 2% of the time, Pallas kernels for 25%

profile of v2, /device:TPU:0, one launch (start us, length us, event | category | flops | bytes accessed | tf_op | source)
XLA Modules:
  0.0 176.3 jit_solution(124973244877108082)
XLA Ops:
  0.6 1.6 copy-done.11
  3.8 3.8 %first.2 = s16[8,2,4,32,256]{4,3,2,1,0:T(8,128)(2,1)} custom-call(s32[8]{0:T(128)S(1)} %copy-done.24, bf16[4,32,32,256]{3,2,1,0:T(8,128)(2,1)S(1)} %copy-done.11, bf16[256,512]{1,0:T(8,128)(2,1)S(1)} %copy-done.30), custom_call_target="tpu_custom_call" | custom-call | flops 2147483648 | bytes 2097152 | tf_op jit(solution)/shard_map/first/pallas_call | solution.py:516
  7.6 7.4 %all-to-all-start = ((s16[8,2,4,32,256]{4,3,2,1,0:T(8,128)(2,1)}), s16[8,2,4,32,256]{4,3,2,1,0:T(8,128)(2,1)S(1)}, u32[]{:S(2)}, u32[]{:S(2)}) async-start(s16[8,2,4,32,256]{4,3,2,1,0:T(8,128)(2,1)} %first.2), calls=%async_computation | async-start | bytes 2097152 | tf_op jit(solution)/shard_map/all_to_all | solution.py:467
  15.1 1.6 copy-done.12
  16.7 3.8 %first.3 = s16[8,2,4,32,256]{4,3,2,1,0:T(8,128)(2,1)} custom-call(s32[8]{0:T(128)S(1)} %copy-done.25, bf16[4,32,32,256]{3,2,1,0:T(8,128)(2,1)S(1)} %copy-done.12, bf16[256,512]{1,0:T(8,128)(2,1)S(1)} %copy-done.31), custom_call_target="tpu_custom_call" | custom-call | flops 2147483648 | bytes 2097152 | tf_op jit(solution)/shard_map/first/pallas_call | solution.py:516
  20.5 20.3 %all-to-all-done.in_ref = s16[8,2,4,32,256]{4,3,2,1,0:T(8,128)(2,1)S(1)} async-done(((s16[8,2,4,32,256]{4,3,2,1,0:T(8,128)(2,1)}), s16[8,2,4,32,256]{4,3,2,1,0:T(8,128)(2,1)S(1)}, u32[]{:S(2)}, u32[]{:S(2)}) %all-to-all-start) | async-done | bytes 1048608 | tf_op jit(solution)/shard_map/all_to_all | solution.py:467
  40.8 4.2 %all-to-all-start.1 = ((s16[8,2,4,32,256]{4,3,2,1,0:T(8,128)(2,1)}), s16[8,2,4,32,256]{4,3,2,1,0:T(8,128)(2,1)}, u32[]{:S(2)}, u32[]{:S(2)}) async-start(s16[8,2,4,32,256]{4,3,2,1,0:T(8,128)(2,1)} %first.3), calls=%async_computation.1 | async-start | bytes 2097152 | tf_op jit(solution)/shard_map/all_to_all | solution.py:467
  45.2 1.2 spectrum.1.mine_ref
  46.9 3.8 %collective-permute-start = (bf16[5,32,8,256]{3,2,1,0:T(8,128)(2,1)S(1)}, bf16[5,32,8,256]{3,2,1,0:T(8,128)(2,1)S(1)}, u32[]{:S(2)}, u32[]{:S(2)}) collective-permute-start(bf16[5,32,8,256]{3,2,1,0:T(8,128)(2,1)S(1)} %pad_maximum_fusion), channel_id=1, source_target_pairs={{0,2},{2,4},{4,6},{6,8},{8,10},{10,12},{12,14},{1,3},{3,5},{5,7},{... | collective-permute-start | bytes 1966088 | tf_op jit(solution)/shard_map/ppermute | solution.py:476
  50.8 1.3 collective-permute-start.1
  52.2 4.1 %cross.2 = s16[8,2,4,32,256]{4,3,2,1,0:T(8,128)(2,1)S(1)} custom-call(s32[8]{0:T(128)S(1)} %copy-done.25, s32[2]{0:T(128)S(1)} %pad_add_fusion.place_ref.refs_0_.refs_2_, s16[8,2,4,32,256]{4,3,2,1,0:T(8,128)(2,1)S(1)} %all-to-all-done.in_ref, bf16[256,512]{1,0:T(8,128)(2,1)S(1)} %copy-done.17, bf16[256,512]{1,0:T(8,128)(2,1)S(1)} %copy-done.28, ...), custom_call_target="tpu_custom_call" | custom-call | flops 1610612736 | bytes 4718592 | tf_op jit(solution)/shard_map/cross/pallas_call | solution.py:556
  57.3 26.8 %collective-permute-done.refs_5_.refs_7_ = bf16[5,32,8,256]{3,2,1,0:T(8,128)(2,1)S(1)} collective-permute-done((bf16[5,32,8,256]{3,2,1,0:T(8,128)(2,1)S(1)}, bf16[5,32,8,256]{3,2,1,0:T(8,128)(2,1)S(1)}, u32[]{:S(2)}, u32[]{:S(2)}) %collective-permute-start) | collective-permute-done | bytes 655392 | tf_op jit(solution)/shard_map/ppermute | solution.py:476
  86.7 3.3 %filters.1 = (bf16[4,256,768]{2,1,0:T(8,128)(2,1)S(1)}, bf16[4,256,768]{2,1,0:T(8,128)(2,1)S(1)}, bf16[4,256,256]{2,1,0:T(8,128)(2,1)S(1)}) custom-call(s32[2]{0:T(128)S(1)} %pad_add_fusion.place_ref.refs_0_.refs_2_, s32[8]{0:T(128)S(1)} %copy-done.25, s32[8,2]{1,0:T(8,128)S(1)} %copy.12.shift_ref, f32[8,3,15]{2,1,0:T(4,128)S(1)} %copy.13.psf_ref), custom_call_target="tpu_custom_call" | custom-call | flops 15728640 | bytes 3670016 | tf_op jit(solution)/shard_map/filters/pallas_call | solution.py:605
  93.1 8.8 %all-to-all-start.3 = ((s16[8,2,4,32,256]{4,3,2,1,0:T(8,128)(2,1)}), s16[8,2,4,32,256]{4,3,2,1,0:T(8,128)(2,1)S(1)}, u32[]{:S(2)}, u32[]{:S(2)}) async-start(s16[8,2,4,32,256]{4,3,2,1,0:T(8,128)(2,1)} %copy-done.3), calls=%async_computation.3 | async-start | bytes 2097152 | tf_op jit(solution)/shard_map/all_to_all | solution.py:467
  102.0 1.6 copy-done.14
  105.7 1.4 copy-done.33
  107.1 1.4 copy-done.36
  109.6 9.3 %join.2.refs_0_ = f32[32,32,256]{2,1,0:T(8,128)S(1)} custom-call(s32[2]{0:T(128)S(1)} %pad_add_fusion.place_ref.refs_0_.refs_2_, f32[32,32,256]{2,1,0:T(8,128)S(1)} %copy-done, bf16[2,32,8,256]{3,2,1,0:T(8,128)(2,1)} %pad_maximum_fusion.2.refs_2_, bf16[2,32,8,256]{3,2,1,0:T(8,128)(2,1)} %collective-permute-done.3.refs_3_, ...), custom_call_target="tpu_custom_call" | custom-call | flops 5637144576 | bytes 12000000 | tf_op jit(solution)/shard_map/join/pallas_call | solution.py:635
  119.2 2.5 %collective-permute-done.4.refs_1_ = f32[32,32,256]{2,1,0:T(8,128)S(1)} collective-permute-done((f32[32,32,256]{2,1,0:T(8,128)S(1)}, f32[32,32,256]{2,1,0:T(8,128)S(1)}, u32[]{:S(2)}, u32[]{:S(2)}) %collective-permute-start.4) | collective-permute-done | bytes 1048608 | tf_op jit(solution)/shard_map/ppermute | solution.py:483
  123.5 4.6 %collective-permute-start.5 = (bf16[32,8,256]{2,1,0:T(8,128)(2,1)}, bf16[32,8,256]{2,1,0:T(8,128)(2,1)}, u32[]{:S(2)}, u32[]{:S(2)}) collective-permute-start(bf16[32,8,256]{2,1,0:T(8,128)(2,1)} %get-tuple-element.18), channel_id=1, source_target_pairs={{0,2},{2,4},{4,6},{6,8},{8,10},{10,12},{12,14},{1,3},{3,5},{5,7},{... | collective-permute-start | bytes 393224 | tf_op jit(solution)/shard_map/ppermute | solution.py:476
  128.0 1.3 collective-permute-start.6
  129.4 5.0 %cross.3 = s16[8,2,4,32,256]{4,3,2,1,0:T(8,128)(2,1)S(1)} custom-call(s32[8]{0:T(128)S(1)} %copy-done.25, s32[2]{0:T(128)S(1)} %pad_add_fusion.place_ref.refs_0_.refs_2_, s16[8,2,4,32,256]{4,3,2,1,0:T(8,128)(2,1)} %all-to-all-done.1.in_ref, bf16[256,512]{1,0:T(8,128)(2,1)S(1)} %copy-done.17, bf16[256,512]{1,0:T(8,128)(2,1)S(1)} %copy-done.29, ...), custom_call_target="tpu_custom_call" | custom-call | flops 1610612736 | bytes 4718592 | tf_op jit(solution)/shard_map/cross/pallas_call | solution.py:556
  136.4 6.7 %all-to-all-start.2 = ((s16[8,2,4,32,256]{4,3,2,1,0:T(8,128)(2,1)}), s16[8,2,4,32,256]{4,3,2,1,0:T(8,128)(2,1)S(1)}, u32[]{:S(2)}, u32[]{:S(2)}) async-start(s16[8,2,4,32,256]{4,3,2,1,0:T(8,128)(2,1)} %copy-done.8), calls=%async_computation.2 | async-start | bytes 2097152 | tf_op jit(solution)/shard_map/all_to_all | solution.py:467
  144.3 1.5 collective-permute-done.7.refs_5_
  145.8 1.2 copy-done.7
  147.0 1.6 copy-done.15
  150.8 1.4 copy-done.34
  152.2 1.4 copy-done.37
  154.7 10.0 %join.3 = (f32[32,32,256]{2,1,0:T(8,128)}, f32[32,32,256]{2,1,0:T(8,128)S(1)}) custom-call(f32[32,32,256]{2,1,0:T(8,128)S(1)} %copy-done.5, f32[32,32,256]{2,1,0:T(8,128)S(1)} %copy-done.7, s32[2]{0:T(128)S(1)} %pad_add_fusion.place_ref.refs_0_.refs_2_, f32[32,32,256]{2,1,0:T(8,128)S(1)} %copy-done, bf16[2,32,8,256]{3,2,1,0:T(8,128)(2,1)S(1)} %pad_maximum_fusion.3.refs_4_, ...), custom_call_target="tpu_custom_call" | custom-call | flops 5637144576 | bytes 12000000 | tf_op jit(solution)/shard_map/join/pallas_call | solution.py:635
  165.9 4.0 %last.2.rest_0_ = f32[4,32,32,256]{3,2,1,0:T(8,128)} custom-call(s32[8]{0:T(128)S(1)} %copy-done.25, s16[8,2,4,32,256]{4,3,2,1,0:T(8,128)(2,1)S(1)} %copy-done.2, bf16[256,512]{1,0:T(8,128)(2,1)S(1)} %copy-done.16), custom_call_target="tpu_custom_call" | custom-call | flops 2415919104 | bytes 3145728 | tf_op jit(solution)/shard_map/last/pallas_call | solution.py:587
  169.8 4.0 %last.3 = f32[4,32,32,256]{3,2,1,0:T(8,128)} custom-call(s32[8]{0:T(128)S(1)} %copy-done.25, s16[8,2,4,32,256]{4,3,2,1,0:T(8,128)(2,1)S(1)} %all-to-all-done.2.in_ref, bf16[256,512]{1,0:T(8,128)(2,1)S(1)} %copy-done.16, f32[4,32,32,256]{3,2,1,0:T(8,128)} %last.2.rest_0_), custom_call_target="tpu_custom_call", output_to_operand_aliasing={{}: (3, {})} | custom-call | flops 2415919104 | bytes 3145728 | tf_op jit(solution)/shard_map/last/pallas_call | solution.py:587
  173.8 2.5 %exponential_multiply_fusion = f32[32,32,256]{2,1,0:T(8,128)} fusion(f32[32,32,256]{2,1,0:T(8,128)S(1)} %copy-done.10, f32[32,32,256]{2,1,0:T(8,128)} %get-tuple-element.16, f32[32,32,256]{2,1,0:T(8,128)S(1)} %collective-permute-done.8), kind=kLoop, calls=%fused_computation | loop fusion | flops 524288 | bytes 4194304 | tf_op jit(solution)/shard_map/mul | solution.py:688
  (103 shorter events, 21.8 us)
Async XLA Ops:
  0.6 1.6 copy-start.11
  7.6 7.4 %copy-start.25 = (s32[8]{0:T(128)S(1)}, s32[8]{0:T(128)}, u32[]{:S(2)}) copy-start(s32[8]{0:T(128)} %map_ref.13) | copy-start | bytes 100
  7.6 7.5 %copy-start.31 = (bf16[256,512]{1,0:T(8,128)(2,1)S(1)}, bf16[256,512]{1,0:T(8,128)(2,1)}, u32[]{:S(2)}) copy-start(bf16[256,512]{1,0:T(8,128)(2,1)} %constant.18.clone.columns_ref) | copy-start | bytes 786436
  7.6 33.2 %all-to-all-start = ((s16[8,2,4,32,256]{4,3,2,1,0:T(8,128)(2,1)}), s16[8,2,4,32,256]{4,3,2,1,0:T(8,128)(2,1)S(1)}, u32[]{:S(2)}, u32[]{:S(2)}) async-start(s16[8,2,4,32,256]{4,3,2,1,0:T(8,128)(2,1)} %first.2), calls=%async_computation | async-start | bytes 2097152 | tf_op jit(solution)/shard_map/all_to_all | solution.py:467
  15.1 1.6 copy-start.12
  20.5 24.7 %copy-start.17 = (bf16[256,512]{1,0:T(8,128)(2,1)S(1)}, bf16[256,512]{1,0:T(8,128)(2,1)}, u32[]{:S(2)}) copy-start(bf16[256,512]{1,0:T(8,128)(2,1)} %constant.20.clone.rows_ref) | copy-start | bytes 786436
  20.5 26.0 %copy-start = (f32[32,32,256]{2,1,0:T(8,128)S(1)}, f32[32,32,256]{2,1,0:T(8,128)}, u32[]{:S(2)}) copy-start(f32[32,32,256]{2,1,0:T(8,128)} %refs_3_.1) | copy-start | bytes 3145732
  40.8 52.3 %all-to-all-start.1 = ((s16[8,2,4,32,256]{4,3,2,1,0:T(8,128)(2,1)}), s16[8,2,4,32,256]{4,3,2,1,0:T(8,128)(2,1)}, u32[]{:S(2)}, u32[]{:S(2)}) async-start(s16[8,2,4,32,256]{4,3,2,1,0:T(8,128)(2,1)} %first.3), calls=%async_computation.1 | async-start | bytes 2097152 | tf_op jit(solution)/shard_map/all_to_all | solution.py:467
  45.2 1.6 copy-start.13
  46.4 5.8 %collective-permute-start.2 = (f32[4,256,256]{2,1,0:T(8,128)S(1)}, f32[4,256,256]{2,1,0:T(8,128)S(1)}, u32[]{:S(2)}, u32[]{:S(2)}) collective-permute-start(f32[4,256,256]{2,1,0:T(8,128)S(1)} %spectrum.1.mine_ref), channel_id=1, source_target_pairs={{0,1},{1,0},{2,3},{3,2},{4,5},{5,4},{6,7},{7,6},{8,9},{9,8},{10,11... | collective-permute-start | bytes 3145736 | tf_op jit(solution)/shard_map/ppermute | solution.py:483
  46.8 5.4 %copy-start.28 = (bf16[256,512]{1,0:T(8,128)(2,1)S(1)}, bf16[256,512]{1,0:T(8,128)(2,1)}, u32[]{:S(2)}) copy-start(bf16[256,512]{1,0:T(8,128)(2,1)} %constant.21.clone.back_ref) | copy-start | bytes 786436
  46.9 37.2 %collective-permute-start = (bf16[5,32,8,256]{3,2,1,0:T(8,128)(2,1)S(1)}, bf16[5,32,8,256]{3,2,1,0:T(8,128)(2,1)S(1)}, u32[]{:S(2)}, u32[]{:S(2)}) collective-permute-start(bf16[5,32,8,256]{3,2,1,0:T(8,128)(2,1)S(1)} %pad_maximum_fusion), channel_id=1, source_target_pairs={{0,2},{2,4},{4,6},{6,8},{8,10},{10,12},{12,14},{1,3},{3,5},{5,7},{... | collective-permute-start | bytes 1966088 | tf_op jit(solution)/shard_map/ppermute | solution.py:476
  50.8 35.8 %copy-start.41 = (f32[8,3,15]{2,0,1:T(8,128)S(1)}, f32[8,3,15]{2,0,1:T(8,128)}, u32[]{:S(2)}) copy-start(f32[8,3,15]{2,0,1:T(8,128)} %param.11) | copy-start | bytes 4324
  50.8 35.8 %copy-start.42 = (s32[8,2]{0,1:T(2,128)S(1)}, s32[8,2]{0,1:T(2,128)}, u32[]{:S(2)}) copy-start(s32[8,2]{0,1:T(2,128)} %param.12) | copy-start | bytes 196
  50.8 33.3 %collective-permute-start.1 = (bf16[5,32,8,256]{3,2,1,0:T(8,128)(2,1)S(1)}, bf16[5,32,8,256]{3,2,1,0:T(8,128)(2,1)S(1)}, u32[]{:S(2)}, u32[]{:S(2)}) collective-permute-start(bf16[5,32,8,256]{3,2,1,0:T(8,128)(2,1)S(1)} %pad_maximum_fusion.1), channel_id=1, source_target_pairs={{2,0},{4,2},{6,4},{8,6},{10,8},{12,10},{14,12},{3,1},{5,3},{7,5},{... | collective-permute-start | bytes 1966088 | tf_op jit(solution)/shard_map/ppermute | solution.py:477
  52.2 4.1 %copy-start.26 = (f32[4,256,256]{2,1,0:T(8,128)}, f32[4,256,256]{2,1,0:T(8,128)S(1)}, u32[]{:S(2)}) copy-start(f32[4,256,256]{2,1,0:T(8,128)S(1)} %collective-permute-done.2.other_ref) | copy-start | bytes 3145732
  86.6 15.4 %collective-permute-start.3 = (bf16[2,32,8,256]{3,2,1,0:T(8,128)(2,1)}, bf16[2,32,8,256]{3,2,1,0:T(8,128)(2,1)}, u32[]{:S(2)}, u32[]{:S(2)}) collective-permute-start(bf16[2,32,8,256]{3,2,1,0:T(8,128)(2,1)} %pad_maximum_fusion.2.refs_2_), channel_id=1, source_target_pairs={{0,1},{1,0},{2,3},{3,2},{4,5},{5,4},{6,7},{7,6},{8,9},{9,8},{10,11... | collective-permute-start | bytes 786440 | tf_op jit(solution)/shard_map/ppermute | solution.py:483
  93.1 42.3 %all-to-all-start.3 = ((s16[8,2,4,32,256]{4,3,2,1,0:T(8,128)(2,1)}), s16[8,2,4,32,256]{4,3,2,1,0:T(8,128)(2,1)S(1)}, u32[]{:S(2)}, u32[]{:S(2)}) async-start(s16[8,2,4,32,256]{4,3,2,1,0:T(8,128)(2,1)} %copy-done.3), calls=%async_computation.3 | async-start | bytes 2097152 | tf_op jit(solution)/shard_map/all_to_all | solution.py:467
  101.9 1.6 copy-start.14
  118.9 10.5 %copy-start.4 = (f32[32,32,256]{2,1,0:T(8,128)}, f32[32,32,256]{2,1,0:T(8,128)S(1)}, u32[]{:S(2)}) copy-start(f32[32,32,256]{2,1,0:T(8,128)S(1)} %join.2.refs_0_) | copy-start | bytes 3145732
  118.9 10.5 %copy-start.27 = (f32[4,256,256]{2,1,0:T(8,128)S(1)}, f32[4,256,256]{2,1,0:T(8,128)}, u32[]{:S(2)}) copy-start(f32[4,256,256]{2,1,0:T(8,128)} %copy-done.26) | copy-start | bytes 3145732
  118.9 10.5 %copy-start.29 = (bf16[256,512]{1,0:T(8,128)(2,1)S(1)}, bf16[256,512]{1,0:T(8,128)(2,1)}, u32[]{:S(2)}) copy-start(bf16[256,512]{1,0:T(8,128)(2,1)} %constant.21.clone.back_ref) | copy-start | bytes 786436
  118.9 2.7 %collective-permute-start.4 = (f32[32,32,256]{2,1,0:T(8,128)S(1)}, f32[32,32,256]{2,1,0:T(8,128)S(1)}, u32[]{:S(2)}, u32[]{:S(2)}) collective-permute-start(f32[32,32,256]{2,1,0:T(8,128)S(1)} %join.2.refs_0_), channel_id=1, source_target_pairs={{0,1},{1,0},{2,3},{3,2},{4,5},{5,4},{6,7},{7,6},{8,9},{9,8},{10,11... | collective-permute-start | bytes 3145736 | tf_op jit(solution)/shard_map/ppermute | solution.py:483
  123.5 19.7 %collective-permute-start.5 = (bf16[32,8,256]{2,1,0:T(8,128)(2,1)}, bf16[32,8,256]{2,1,0:T(8,128)(2,1)}, u32[]{:S(2)}, u32[]{:S(2)}) collective-permute-start(bf16[32,8,256]{2,1,0:T(8,128)(2,1)} %get-tuple-element.18), channel_id=1, source_target_pairs={{0,2},{2,4},{4,6},{6,8},{8,10},{10,12},{12,14},{1,3},{3,5},{5,7},{... | collective-permute-start | bytes 393224 | tf_op jit(solution)/shard_map/ppermute | solution.py:476
  128.0 15.1 %collective-permute-start.6 = (bf16[32,8,256]{2,1,0:T(8,128)(2,1)S(1)}, bf16[32,8,256]{2,1,0:T(8,128)(2,1)}, u32[]{:S(2)}, u32[]{:S(2)}) collective-permute-start(bf16[32,8,256]{2,1,0:T(8,128)(2,1)S(1)} %get-tuple-element.19), channel_id=1, source_target_pairs={{2,0},{4,2},{6,4},{8,6},{10,8},{12,10},{14,12},{3,1},{5,3},{7,5},{... | collective-permute-start | bytes 393224 | tf_op jit(solution)/shard_map/ppermute | solution.py:477
  136.4 9.4 %copy-start.5 = (f32[32,32,256]{2,1,0:T(8,128)S(1)}, f32[32,32,256]{2,1,0:T(8,128)}, u32[]{:S(2)}) copy-start(f32[32,32,256]{2,1,0:T(8,128)} %copy-done.4) | copy-start | bytes 3145732
  136.4 33.5 %all-to-all-start.2 = ((s16[8,2,4,32,256]{4,3,2,1,0:T(8,128)(2,1)}), s16[8,2,4,32,256]{4,3,2,1,0:T(8,128)(2,1)S(1)}, u32[]{:S(2)}, u32[]{:S(2)}) async-start(s16[8,2,4,32,256]{4,3,2,1,0:T(8,128)(2,1)} %copy-done.8), calls=%async_computation.2 | async-start | bytes 2097152 | tf_op jit(solution)/shard_map/all_to_all | solution.py:467
  143.1 22.7 %copy-start.16 = (bf16[256,512]{1,0:T(8,128)(2,1)S(1)}, bf16[256,512]{1,0:T(8,128)(2,1)}, u32[]{:S(2)}) copy-start(bf16[256,512]{1,0:T(8,128)(2,1)} %constant.19.clone.columns_ref) | copy-start | bytes 786436
  144.2 21.7 %copy-start.2 = (s16[8,2,4,32,256]{4,3,2,1,0:T(8,128)(2,1)S(1)}, s16[8,2,4,32,256]{4,3,2,1,0:T(8,128)(2,1)}, u32[]{:S(2)}) copy-start(s16[8,2,4,32,256]{4,3,2,1,0:T(8,128)(2,1)} %copy-done.1) | copy-start | bytes 3145732
  144.2 1.6 collective-permute-start.7
  165.7 8.1 %collective-permute-start.8 = (f32[32,32,256]{2,1,0:T(8,128)}, f32[32,32,256]{2,1,0:T(8,128)S(1)}, u32[]{:S(2)}, u32[]{:S(2)}) collective-permute-start(f32[32,32,256]{2,1,0:T(8,128)} %get-tuple-element.16), channel_id=1, source_target_pairs={{0,1},{1,0},{2,3},{3,2},{4,5},{5,4},{6,7},{7,6},{8,9},{9,8},{10,11... | collective-permute-start | bytes 3145736 | tf_op jit(solution)/shard_map/ppermute | solution.py:483
  169.8 4.0 %copy-start.10 = (f32[32,32,256]{2,1,0:T(8,128)S(1)}, f32[32,32,256]{2,1,0:T(8,128)}, u32[]{:S(2)}) copy-start(f32[32,32,256]{2,1,0:T(8,128)} %copy-done.9) | copy-start | bytes 3145732
  (24 other events, 26.3 us)

commit v3 on v1

--- a/solution.py
+++ b/solution.py
@@ -547,6 +547,7 @@
             ),
             out_shape=jax.ShapeDtypeStruct(spectrum_shape, F32),
             cost_estimate=cost(row_flops, 6 * volume),
+            compiler_params=pltpu.CompilerParams(vmem_limit_bytes=16 * 1024 * 1024),
             name="spectrum",
         )(place, payload, row_turn)
 
@@ -567,6 +568,7 @@
             ),
             out_shape=jax.ShapeDtypeStruct(payload_shape, jnp.int16),
             cost_estimate=cost(2 * row_flops * chunk, payload_bytes + 10 * volume),
+            compiler_params=pltpu.CompilerParams(vmem_limit_bytes=16 * 1024 * 1024),
             name="cross",
         )(view_map, place, payload, row_turn, row_back, mine, other)
 
@@ -593,6 +595,7 @@
             out_shape=jax.ShapeDtypeStruct((slots, depth, rows, width), F32),
             input_output_aliases=aliases,
             cost_estimate=cost(2 * chunk * volume * 9 * width, payload_bytes * 1.5),
+            compiler_params=pltpu.CompilerParams(vmem_limit_bytes=16 * 1024 * 1024),
             name="last",
         )(*operands)
 
@@ -656,12 +659,13 @@
             name="join",
         )(*(logs or ()), place, estimate, *strips, observed, *rims, forward, backward, columns)
 
-    sent_a = turn(first(0))
+    payload_a = first(0)
+    sent_a = turn(payload_a)
     payload_b = first(chunk)
     sent_b = turn(payload_b)
     mine = reference_spectrum(sent_a)
     other = swap_cores(mine)
-    first_rims, crossed_a = lax.optimization_barrier((first_rims, crossed(sent_a, mine, other)))
+    crossed_a = crossed(sent_a, mine, other)
     back_a = turn(crossed_a)
     first_strips = swap_strips([rim[slots] for rim in first_rims])
 

time: 170 us -> 180 us (1.059)
  waiting for transfers between devices: 52.8 us -> 67.1 us
  Pallas kernels: 66.6 us -> 59.5 us
    ppermute x2, waiting for transfers between devices: 23.2 us -> 34.6 us  [send_rims(): below = lax.ppermute(high, 'gz', [(i, i + 1) for i in range(count - 1)])]
    ppermute x2, waiting for transfers between devices: 0.01 us -> 2.92 us  [send_rims(): above = lax.ppermute(low, 'gz', [(i + 1, i) for i in range(count - 1)])]
    pallas_call x2, Pallas kernels: 13.5 us -> 10.9 us  [crossed(): pl.pallas_call(cross_kernel, grid_spec=pltpu.PrefetchScalarGridSpec(num_s...]
    pallas_call x2, Pallas kernels: 10.2 us -> 7.92 us  [last(): pl.pallas_call(last_kernel, grid_spec=pltpu.PrefetchScalarGridSpec(num_sc...]
    pallas_call x1, Pallas kernels: 3.43 us -> 1.21 us  [reference_spectrum(): pl.pallas_call(spectrum_kernel, grid_spec=pltpu.PrefetchScalarGridSpec(nu...]
    unnamed x34 -> x38, local copies, waits for them, and re-layouts: 3.67 us -> 5.54 us
  transfers between devices with their start and end apart: 13 -> 13, of which waited for: 5 -> 7; matrix products, arithmetic and copies ran while one was open for 4% -> 5% of each run, Pallas kernels for 36% -> 28%
where the time goes in v3:
time: 180 us; the launch traced here: 179 us
  waiting for transfers between devices  67.1 us (37%)
  Pallas kernels  59.5 us (33%)
  starting transfers between devices  37.6 us (21%)
  local copies, waits for them, and re-layouts  6.84 us (4%)
  other arithmetic  6.83 us (4%)
    ppermute x2, waiting for transfers between devices, send_rims(): below = lax.ppermute(high, 'gz', [(i, i + 1) for i in range(count - 1)])  34.6 us
    all_to_all x4, starting transfers between devices, turn(): lax.all_to_all(payload, 'gz', split_axis=0, concat_axis=0, tiled=True)  26.7 us
    pallas_call x2, Pallas kernels, join(): pl.pallas_call(functools.partial(join_kernel, views, updated), grid=(slot...  25.3 us
    all_to_all x4, waiting for transfers between devices, turn(): lax.all_to_all(payload, 'gz', split_axis=0, concat_axis=0, tiled=True)  24.1 us
    pallas_call x2, Pallas kernels, crossed(): pl.pallas_call(cross_kernel, grid_spec=pltpu.PrefetchScalarGridSpec(num_s...  10.9 us
    pallas_call x2, Pallas kernels, first(): pl.pallas_call(first_kernel, grid_spec=pltpu.PrefetchScalarGridSpec(num_s...  10.2 us
    pallas_call x2, Pallas kernels, last(): pl.pallas_call(last_kernel, grid_spec=pltpu.PrefetchScalarGridSpec(num_sc...  7.92 us
    ppermute x2, starting transfers between devices, send_rims(): below = lax.ppermute(high, 'gz', [(i, i + 1) for i in range(count - 1)])  7.89 us
  transfers between devices with their start and end apart: 13, of which 7 were waited for; matrix products, arithmetic and copies ran while one was open for 5% of the time, Pallas kernels for 28%

profile of v3, /device:TPU:0, one launch (start us, length us, event | category | flops | bytes accessed | tf_op | source)
XLA Modules:
  0.0 178.8 jit_solution(9320228317687112889)
XLA Ops:
  0.6 5.1 %first.3 = s16[8,2,4,32,256]{4,3,2,1,0:T(8,128)(2,1)} custom-call(s32[8]{0:T(128)} %map_ref.13, bf16[4,32,32,256]{3,2,1,0:T(8,128)(2,1)} %observed_ref.3, bf16[256,512]{1,0:T(8,128)(2,1)} %constant.18.clone.columns_ref), custom_call_target="tpu_custom_call" | custom-call | flops 2147483648 | bytes 2097152 | tf_op jit(solution)/shard_map/first/pallas_call | solution.py:516
  5.7 7.3 %all-to-all-start.1 = ((s16[8,2,4,32,256]{4,3,2,1,0:T(8,128)(2,1)}), s16[8,2,4,32,256]{4,3,2,1,0:T(8,128)(2,1)S(1)}, u32[]{:S(2)}, u32[]{:S(2)}) async-start(s16[8,2,4,32,256]{4,3,2,1,0:T(8,128)(2,1)} %first.3), calls=%async_computation.1 | async-start | bytes 2097152 | tf_op jit(solution)/shard_map/all_to_all | solution.py:467
  13.0 5.1 %first.2 = s16[8,2,4,32,256]{4,3,2,1,0:T(8,128)(2,1)} custom-call(s32[8]{0:T(128)} %map_ref.13, bf16[4,32,32,256]{3,2,1,0:T(8,128)(2,1)} %observed_ref.3, bf16[256,512]{1,0:T(8,128)(2,1)} %constant.18.clone.columns_ref), custom_call_target="tpu_custom_call" | custom-call | flops 2147483648 | bytes 2097152 | tf_op jit(solution)/shard_map/first/pallas_call | solution.py:516
  18.1 20.7 %all-to-all-done.1.in_ref = s16[8,2,4,32,256]{4,3,2,1,0:T(8,128)(2,1)S(1)} async-done(((s16[8,2,4,32,256]{4,3,2,1,0:T(8,128)(2,1)}), s16[8,2,4,32,256]{4,3,2,1,0:T(8,128)(2,1)S(1)}, u32[]{:S(2)}, u32[]{:S(2)}) %all-to-all-start.1) | async-done | bytes 1048608 | tf_op jit(solution)/shard_map/all_to_all | solution.py:467
  38.8 3.6 %all-to-all-start = ((s16[8,2,4,32,256]{4,3,2,1,0:T(8,128)(2,1)}), s16[8,2,4,32,256]{4,3,2,1,0:T(8,128)(2,1)S(1)}, u32[]{:S(2)}, u32[]{:S(2)}) async-start(s16[8,2,4,32,256]{4,3,2,1,0:T(8,128)(2,1)} %first.2), calls=%async_computation | async-start | bytes 2097152 | tf_op jit(solution)/shard_map/all_to_all | solution.py:467
  42.5 1.3 fusion.18
  43.8 1.2 spectrum.1.mine_ref
  45.2 4.0 %collective-permute-start = (bf16[5,32,8,256]{3,2,1,0:T(8,128)(2,1)S(1)}, bf16[5,32,8,256]{3,2,1,0:T(8,128)(2,1)S(1)}, u32[]{:S(2)}, u32[]{:S(2)}) collective-permute-start(bf16[5,32,8,256]{3,2,1,0:T(8,128)(2,1)S(1)} %pad_maximum_fusion), channel_id=1, source_target_pairs={{0,2},{2,4},{4,6},{6,8},{8,10},{10,12},{12,14},{1,3},{3,5},{5,7},{... | collective-permute-start | bytes 1966088 | tf_op jit(solution)/shard_map/ppermute | solution.py:476
  49.3 1.3 collective-permute-start.1
  50.6 31.7 %collective-permute-done.refs_5_.refs_7_ = bf16[5,32,8,256]{3,2,1,0:T(8,128)(2,1)S(1)} collective-permute-done((bf16[5,32,8,256]{3,2,1,0:T(8,128)(2,1)S(1)}, bf16[5,32,8,256]{3,2,1,0:T(8,128)(2,1)S(1)}, u32[]{:S(2)}, u32[]{:S(2)}) %collective-permute-start) | collective-permute-done | bytes 655392 | tf_op jit(solution)/shard_map/ppermute | solution.py:476
  84.8 4.0 %filters.1 = (bf16[4,256,768]{2,1,0:T(8,128)(2,1)}, bf16[4,256,768]{2,1,0:T(8,128)(2,1)}, bf16[4,256,256]{2,1,0:T(8,128)(2,1)}) custom-call(s32[2]{0:T(128)} %copy-done.7, s32[8]{0:T(128)} %map_ref.13, s32[8,2]{1,0:T(8,128)} %copy.12.shift_ref, f32[8,3,15]{2,1,0:T(4,128)} %copy.13.psf_ref), custom_call_target="tpu_custom_call" | custom-call | flops 15728640 | bytes 3670016 | tf_op jit(solution)/shard_map/filters/pallas_call | solution.py:604
  88.9 0.9 copy-done.10
  89.8 5.5 %cross.3 = s16[8,2,4,32,256]{4,3,2,1,0:T(8,128)(2,1)S(1)} custom-call(s32[8]{0:T(128)S(1)} %copy-done.6, s32[2]{0:T(128)S(1)} %copy-done.8, s16[8,2,4,32,256]{4,3,2,1,0:T(8,128)(2,1)S(1)} %all-to-all-done.1.in_ref, bf16[256,512]{1,0:T(8,128)(2,1)S(1)} %copy-done.5, bf16[256,512]{1,0:T(8,128)(2,1)S(1)} %copy-done.10, f32[4,256,256]{2,1,0:T(8,128)S(1)} %spectrum.1.mine_ref, ...), custom_call_target="tpu_custom_call" | custom-call | flops 1610612736 | bytes 4718592 | tf_op jit(solution)/shard_map/cross/pallas_call | solution.py:555
  95.3 1.0 copy-done.2
  96.2 8.6 %all-to-all-start.3 = ((s16[8,2,4,32,256]{4,3,2,1,0:T(8,128)(2,1)}), s16[8,2,4,32,256]{4,3,2,1,0:T(8,128)(2,1)S(1)}, u32[]{:S(2)}, u32[]{:S(2)}) async-start(s16[8,2,4,32,256]{4,3,2,1,0:T(8,128)(2,1)} %copy-done.2), calls=%async_computation.3 | async-start | bytes 2097152 | tf_op jit(solution)/shard_map/all_to_all | solution.py:467
  104.8 12.0 %join.2.refs_0_ = f32[32,32,256]{2,1,0:T(8,128)} custom-call(s32[2]{0:T(128)} %copy-done.7, f32[32,32,256]{2,1,0:T(8,128)} %refs_3_.1, bf16[2,32,8,256]{3,2,1,0:T(8,128)(2,1)} %pad_maximum_fusion.2.refs_2_, bf16[2,32,8,256]{3,2,1,0:T(8,128)(2,1)} %collective-permute-done.2.refs_3_, bf16[4,32,32,256]{3,2,1,0:T(8,128)(2,1)} %observed_ref.3, ...), custom_call_target="tpu_custom_call" | custom-call | flops 5637144576 | bytes 12000000 | tf_op jit(solution)/shard_map/join/pallas_call | solution.py:633
  116.9 2.8 %collective-permute-done.3.refs_1_ = f32[32,32,256]{2,1,0:T(8,128)S(1)} collective-permute-done((f32[32,32,256]{2,1,0:T(8,128)}, f32[32,32,256]{2,1,0:T(8,128)S(1)}, u32[]{:S(2)}, u32[]{:S(2)}) %collective-permute-start.3) | collective-permute-done | bytes 1048608 | tf_op jit(solution)/shard_map/ppermute | solution.py:483
  119.7 2.2 %fusion.16 = (bf16[32,8,256]{2,1,0:T(8,128)(2,1)S(1)}, bf16[32,8,256]{2,1,0:T(8,128)(2,1)S(1)}) fusion(f32[32,32,256]{2,1,0:T(8,128)S(1)} %collective-permute-done.3.refs_1_, f32[32,32,256]{2,1,0:T(8,128)} %join.2.refs_0_, f32[32,32,256]{2,1,0:T(8,128)} %refs_3_.1, pred[]{:T(512)S(6)} %eq.2), kind=kLoop, calls=%fused_computation.29 | loop fusion | flops 917504 | bytes 3407873 | tf_op jit(solution)/shard_map/jit(_where)/select_n | solution.py:471
  121.9 3.9 %collective-permute-start.4 = (bf16[32,8,256]{2,1,0:T(8,128)(2,1)S(1)}, bf16[32,8,256]{2,1,0:T(8,128)(2,1)S(1)}, u32[]{:S(2)}, u32[]{:S(2)}) collective-permute-start(bf16[32,8,256]{2,1,0:T(8,128)(2,1)S(1)} %get-tuple-element.12), channel_id=1, source_target_pairs={{0,2},{2,4},{4,6},{6,8},{8,10},{10,12},{12,14},{1,3},{3,5},{5,7},{... | collective-permute-start | bytes 393224 | tf_op jit(solution)/shard_map/ppermute | solution.py:476
  125.8 1.3 collective-permute-start.5
  127.1 2.9 %collective-permute-done.4 = bf16[32,8,256]{2,1,0:T(8,128)(2,1)S(1)} collective-permute-done((bf16[32,8,256]{2,1,0:T(8,128)(2,1)S(1)}, bf16[32,8,256]{2,1,0:T(8,128)(2,1)S(1)}, u32[]{:S(2)}, u32[]{:S(2)}) %collective-permute-start.4) | collective-permute-done | bytes 131104 | tf_op jit(solution)/shard_map/ppermute | solution.py:476
  130.1 2.9 %collective-permute-done.5 = bf16[32,8,256]{2,1,0:T(8,128)(2,1)S(1)} collective-permute-done((bf16[32,8,256]{2,1,0:T(8,128)(2,1)S(1)}, bf16[32,8,256]{2,1,0:T(8,128)(2,1)S(1)}, u32[]{:S(2)}, u32[]{:S(2)}) %collective-permute-start.5) | collective-permute-done | bytes 131104 | tf_op jit(solution)/shard_map/ppermute | solution.py:477
  133.8 5.4 %cross.2 = s16[8,2,4,32,256]{4,3,2,1,0:T(8,128)(2,1)S(1)} custom-call(s32[8]{0:T(128)S(1)} %copy-done.6, s32[2]{0:T(128)S(1)} %copy-done.9, s16[8,2,4,32,256]{4,3,2,1,0:T(8,128)(2,1)S(1)} %all-to-all-done.in_ref, bf16[256,512]{1,0:T(8,128)(2,1)S(1)} %copy-done.5, bf16[256,512]{1,0:T(8,128)(2,1)S(1)} %copy-done.11, f32[4,256,256]{2,1,0:T(8,128)S(1)} %spectrum.1.mine_ref, ...), custom_call_target="tpu_custom_call" | custom-call | flops 1610612736 | bytes 4718592 | tf_op jit(solution)/shard_map/cross/pallas_call | solution.py:555
  139.2 1.0 copy-done.3
  140.2 1.0 copy-done
  141.2 7.2 %all-to-all-start.2 = ((s16[8,2,4,32,256]{4,3,2,1,0:T(8,128)(2,1)}), s16[8,2,4,32,256]{4,3,2,1,0:T(8,128)(2,1)S(1)}, u32[]{:S(2)}, u32[]{:S(2)}) async-start(s16[8,2,4,32,256]{4,3,2,1,0:T(8,128)(2,1)} %copy-done.3), calls=%async_computation.2 | async-start | bytes 2097152 | tf_op jit(solution)/shard_map/all_to_all | solution.py:467
  148.4 13.3 %join.3 = (f32[32,32,256]{2,1,0:T(8,128)}, f32[32,32,256]{2,1,0:T(8,128)}) custom-call(f32[32,32,256]{2,1,0:T(8,128)} %join.2.refs_0_, f32[32,32,256]{2,1,0:T(8,128)} %copy-done.13, s32[2]{0:T(128)} %copy-done.7, f32[32,32,256]{2,1,0:T(8,128)} %refs_3_.1, bf16[2,32,8,256]{3,2,1,0:T(8,128)(2,1)} %pad_maximum_fusion.3.refs_4_, ...), custom_call_target="tpu_custom_call" | custom-call | flops 5637144576 | bytes 12000000 | tf_op jit(solution)/shard_map/join/pallas_call | solution.py:633
  161.9 2.7 %collective-permute-done.7 = f32[32,32,256]{2,1,0:T(8,128)S(1)} collective-permute-done((f32[32,32,256]{2,1,0:T(8,128)}, f32[32,32,256]{2,1,0:T(8,128)S(1)}, u32[]{:S(2)}, u32[]{:S(2)}) %collective-permute-start.7) | collective-permute-done | bytes 1048608 | tf_op jit(solution)/shard_map/ppermute | solution.py:483
  164.6 2.9 %exponential_multiply_fusion = f32[32,32,256]{2,1,0:T(8,128)} fusion(f32[32,32,256]{2,1,0:T(8,128)} %get-tuple-element.10, f32[32,32,256]{2,1,0:T(8,128)} %get-tuple-element.11, f32[32,32,256]{2,1,0:T(8,128)S(1)} %collective-permute-done.7), kind=kLoop, calls=%fused_computation | loop fusion | flops 524288 | bytes 4194304 | tf_op jit(solution)/shard_map/mul | solution.py:686
  167.5 4.0 %last.2.rest_0_ = f32[4,32,32,256]{3,2,1,0:T(8,128)} custom-call(s32[8]{0:T(128)S(1)} %copy-done.6, s16[8,2,4,32,256]{4,3,2,1,0:T(8,128)(2,1)S(1)} %copy-done.1, bf16[256,512]{1,0:T(8,128)(2,1)S(1)} %copy-done.4), custom_call_target="tpu_custom_call" | custom-call | flops 2415919104 | bytes 3145728 | tf_op jit(solution)/shard_map/last/pallas_call | solution.py:586
  171.4 3.4 %all-to-all-done.2.in_ref = s16[8,2,4,32,256]{4,3,2,1,0:T(8,128)(2,1)S(1)} async-done(((s16[8,2,4,32,256]{4,3,2,1,0:T(8,128)(2,1)}), s16[8,2,4,32,256]{4,3,2,1,0:T(8,128)(2,1)S(1)}, u32[]{:S(2)}, u32[]{:S(2)}) %all-to-all-start.2) | async-done | bytes 1048608 | tf_op jit(solution)/shard_map/all_to_all | solution.py:467
  174.8 4.0 %last.3 = f32[4,32,32,256]{3,2,1,0:T(8,128)} custom-call(s32[8]{0:T(128)S(1)} %copy-done.6, s16[8,2,4,32,256]{4,3,2,1,0:T(8,128)(2,1)S(1)} %all-to-all-done.2.in_ref, bf16[256,512]{1,0:T(8,128)(2,1)S(1)} %copy-done.4, f32[4,32,32,256]{3,2,1,0:T(8,128)} %last.2.rest_0_), custom_call_target="tpu_custom_call", output_to_operand_aliasing={{}: (3, {})} | custom-call | flops 2415919104 | bytes 3145728 | tf_op jit(solution)/shard_map/last/pallas_call | solution.py:586
  (53 shorter events, 4.0 us)
Async XLA Ops:
  5.7 33.1 %all-to-all-start.1 = ((s16[8,2,4,32,256]{4,3,2,1,0:T(8,128)(2,1)}), s16[8,2,4,32,256]{4,3,2,1,0:T(8,128)(2,1)S(1)}, u32[]{:S(2)}, u32[]{:S(2)}) async-start(s16[8,2,4,32,256]{4,3,2,1,0:T(8,128)(2,1)} %first.3), calls=%async_computation.1 | async-start | bytes 2097152 | tf_op jit(solution)/shard_map/all_to_all | solution.py:467
  18.1 24.4 %copy-start.12 = (f32[32,32,256]{2,1,0:T(8,128)S(1)}, f32[32,32,256]{2,1,0:T(8,128)}, u32[]{:S(2)}) copy-start(f32[32,32,256]{2,1,0:T(8,128)} %refs_3_.1) | copy-start | bytes 3145732
  18.1 25.7 %copy-start.5 = (bf16[256,512]{1,0:T(8,128)(2,1)S(1)}, bf16[256,512]{1,0:T(8,128)(2,1)}, u32[]{:S(2)}) copy-start(bf16[256,512]{1,0:T(8,128)(2,1)} %constant.20.clone.rows_ref) | copy-start | bytes 786436
  38.8 57.5 %all-to-all-start = ((s16[8,2,4,32,256]{4,3,2,1,0:T(8,128)(2,1)}), s16[8,2,4,32,256]{4,3,2,1,0:T(8,128)(2,1)S(1)}, u32[]{:S(2)}, u32[]{:S(2)}) async-start(s16[8,2,4,32,256]{4,3,2,1,0:T(8,128)(2,1)} %first.2), calls=%async_computation | async-start | bytes 2097152 | tf_op jit(solution)/shard_map/all_to_all | solution.py:467
  42.5 2.6 %copy-start.7 = (s32[2]{0:T(128)}, s32[2]{0:T(128)S(1)}, u32[]{:S(2)}) copy-start(s32[2]{0:T(128)S(1)} %pad_add_fusion.place_ref.refs_0_.refs_2_) | copy-start | bytes 28
  45.0 38.5 %copy-start.16 = (f32[8,3,15]{2,0,1:T(8,128)S(1)}, f32[8,3,15]{2,0,1:T(8,128)}, u32[]{:S(2)}) copy-start(f32[8,3,15]{2,0,1:T(8,128)} %param.11) | copy-start | bytes 4324
  45.0 39.1 %copy-start.17 = (s32[8,2]{0,1:T(2,128)S(1)}, s32[8,2]{0,1:T(2,128)}, u32[]{:S(2)}) copy-start(s32[8,2]{0,1:T(2,128)} %param.12) | copy-start | bytes 196
  45.1 43.8 %copy-start.6 = (s32[8]{0:T(128)S(1)}, s32[8]{0:T(128)}, u32[]{:S(2)}) copy-start(s32[8]{0:T(128)} %map_ref.13) | copy-start | bytes 100
  45.1 43.8 %collective-permute-start.8 = (f32[4,256,256]{2,1,0:T(8,128)S(1)}, f32[4,256,256]{2,1,0:T(8,128)}, u32[]{:S(2)}, u32[]{:S(2)}) collective-permute-start(f32[4,256,256]{2,1,0:T(8,128)S(1)} %spectrum.1.mine_ref), channel_id=1, source_target_pairs={{0,1},{1,0},{2,3},{3,2},{4,5},{5,4},{6,7},{7,6},{8,9},{9,8},{10,11... | collective-permute-start | bytes 3145736 | tf_op jit(solution)/shard_map/ppermute | solution.py:483
  45.2 43.7 %copy-start.8 = (s32[2]{0:T(128)S(1)}, s32[2]{0:T(128)}, u32[]{:S(2)}) copy-start(s32[2]{0:T(128)} %copy-done.7) | copy-start | bytes 28
  45.2 37.0 %collective-permute-start = (bf16[5,32,8,256]{3,2,1,0:T(8,128)(2,1)S(1)}, bf16[5,32,8,256]{3,2,1,0:T(8,128)(2,1)S(1)}, u32[]{:S(2)}, u32[]{:S(2)}) collective-permute-start(bf16[5,32,8,256]{3,2,1,0:T(8,128)(2,1)S(1)} %pad_maximum_fusion), channel_id=1, source_target_pairs={{0,2},{2,4},{4,6},{6,8},{8,10},{10,12},{12,14},{1,3},{3,5},{5,7},{... | collective-permute-start | bytes 1966088 | tf_op jit(solution)/shard_map/ppermute | solution.py:476
  49.3 33.0 %collective-permute-start.1 = (bf16[5,32,8,256]{3,2,1,0:T(8,128)(2,1)S(1)}, bf16[5,32,8,256]{3,2,1,0:T(8,128)(2,1)S(1)}, u32[]{:S(2)}, u32[]{:S(2)}) collective-permute-start(bf16[5,32,8,256]{3,2,1,0:T(8,128)(2,1)S(1)} %pad_maximum_fusion.1), channel_id=1, source_target_pairs={{2,0},{4,2},{6,4},{8,6},{10,8},{12,10},{14,12},{3,1},{5,3},{7,5},{... | collective-permute-start | bytes 1966088 | tf_op jit(solution)/shard_map/ppermute | solution.py:477
  82.3 0.9 copy-start.14
  82.3 1.2 copy-start.15
  83.2 21.6 %collective-permute-start.2 = (bf16[2,32,8,256]{3,2,1,0:T(8,128)(2,1)}, bf16[2,32,8,256]{3,2,1,0:T(8,128)(2,1)}, u32[]{:S(2)}, u32[]{:S(2)}) collective-permute-start(bf16[2,32,8,256]{3,2,1,0:T(8,128)(2,1)} %pad_maximum_fusion.2.refs_2_), channel_id=1, source_target_pairs={{0,1},{1,0},{2,3},{3,2},{4,5},{5,4},{6,7},{7,6},{8,9},{9,8},{10,11... | collective-permute-start | bytes 786440 | tf_op jit(solution)/shard_map/ppermute | solution.py:483
  88.8 1.0 copy-start.10
  95.3 1.0 copy-start.2
  96.2 43.9 %all-to-all-start.3 = ((s16[8,2,4,32,256]{4,3,2,1,0:T(8,128)(2,1)}), s16[8,2,4,32,256]{4,3,2,1,0:T(8,128)(2,1)S(1)}, u32[]{:S(2)}, u32[]{:S(2)}) async-start(s16[8,2,4,32,256]{4,3,2,1,0:T(8,128)(2,1)} %copy-done.2), calls=%async_computation.3 | async-start | bytes 2097152 | tf_op jit(solution)/shard_map/all_to_all | solution.py:467
  116.8 17.0 %copy-start.9 = (s32[2]{0:T(128)S(1)}, s32[2]{0:T(128)}, u32[]{:S(2)}) copy-start(s32[2]{0:T(128)} %copy-done.7) | copy-start | bytes 28
  116.8 17.0 %copy-start.11 = (bf16[256,512]{1,0:T(8,128)(2,1)S(1)}, bf16[256,512]{1,0:T(8,128)(2,1)}, u32[]{:S(2)}) copy-start(bf16[256,512]{1,0:T(8,128)(2,1)} %constant.21.clone.back_ref) | copy-start | bytes 786436
  116.8 2.9 %collective-permute-start.3 = (f32[32,32,256]{2,1,0:T(8,128)}, f32[32,32,256]{2,1,0:T(8,128)S(1)}, u32[]{:S(2)}, u32[]{:S(2)}) collective-permute-start(f32[32,32,256]{2,1,0:T(8,128)} %join.2.refs_0_), channel_id=1, source_target_pairs={{0,1},{1,0},{2,3},{3,2},{4,5},{5,4},{6,7},{7,6},{8,9},{9,8},{10,11... | collective-permute-start | bytes 3145736 | tf_op jit(solution)/shard_map/ppermute | solution.py:483
  119.7 14.0 %copy-start.13 = (f32[32,32,256]{2,1,0:T(8,128)}, f32[32,32,256]{2,1,0:T(8,128)S(1)}, u32[]{:S(2)}) copy-start(f32[32,32,256]{2,1,0:T(8,128)S(1)} %collective-permute-done.3.refs_1_) | copy-start | bytes 3145732
  121.9 8.2 %collective-permute-start.4 = (bf16[32,8,256]{2,1,0:T(8,128)(2,1)S(1)}, bf16[32,8,256]{2,1,0:T(8,128)(2,1)S(1)}, u32[]{:S(2)}, u32[]{:S(2)}) collective-permute-start(bf16[32,8,256]{2,1,0:T(8,128)(2,1)S(1)} %get-tuple-element.12), channel_id=1, source_target_pairs={{0,2},{2,4},{4,6},{6,8},{8,10},{10,12},{12,14},{1,3},{3,5},{5,7},{... | collective-permute-start | bytes 393224 | tf_op jit(solution)/shard_map/ppermute | solution.py:476
  125.8 7.2 %collective-permute-start.5 = (bf16[32,8,256]{2,1,0:T(8,128)(2,1)S(1)}, bf16[32,8,256]{2,1,0:T(8,128)(2,1)S(1)}, u32[]{:S(2)}, u32[]{:S(2)}) collective-permute-start(bf16[32,8,256]{2,1,0:T(8,128)(2,1)S(1)} %get-tuple-element.13), channel_id=1, source_target_pairs={{2,0},{4,2},{6,4},{8,6},{10,8},{12,10},{14,12},{3,1},{5,3},{7,5},{... | collective-permute-start | bytes 393224 | tf_op jit(solution)/shard_map/ppermute | solution.py:477
  133.7 14.7 %collective-permute-start.6 = (bf16[2,32,8,256]{3,2,1,0:T(8,128)(2,1)}, bf16[2,32,8,256]{3,2,1,0:T(8,128)(2,1)}, u32[]{:S(2)}, u32[]{:S(2)}) collective-permute-start(bf16[2,32,8,256]{3,2,1,0:T(8,128)(2,1)} %pad_maximum_fusion.3.refs_4_), channel_id=1, source_target_pairs={{0,1},{1,0},{2,3},{3,2},{4,5},{5,4},{6,7},{7,6},{8,9},{9,8},{10,11... | collective-permute-start | bytes 786440 | tf_op jit(solution)/shard_map/ppermute | solution.py:483
  139.2 1.0 copy-start.3
  140.2 1.0 copy-start
  141.2 33.7 %all-to-all-start.2 = ((s16[8,2,4,32,256]{4,3,2,1,0:T(8,128)(2,1)}), s16[8,2,4,32,256]{4,3,2,1,0:T(8,128)(2,1)S(1)}, u32[]{:S(2)}, u32[]{:S(2)}) async-start(s16[8,2,4,32,256]{4,3,2,1,0:T(8,128)(2,1)} %copy-done.3), calls=%async_computation.2 | async-start | bytes 2097152 | tf_op jit(solution)/shard_map/all_to_all | solution.py:467
  161.7 2.9 %collective-permute-start.7 = (f32[32,32,256]{2,1,0:T(8,128)}, f32[32,32,256]{2,1,0:T(8,128)S(1)}, u32[]{:S(2)}, u32[]{:S(2)}) collective-permute-start(f32[32,32,256]{2,1,0:T(8,128)} %get-tuple-element.11), channel_id=1, source_target_pairs={{0,1},{1,0},{2,3},{3,2},{4,5},{5,4},{6,7},{7,6},{8,9},{9,8},{10,11... | collective-permute-start | bytes 3145736 | tf_op jit(solution)/shard_map/ppermute | solution.py:483
  164.6 2.9 %copy-start.1 = (s16[8,2,4,32,256]{4,3,2,1,0:T(8,128)(2,1)S(1)}, s16[8,2,4,32,256]{4,3,2,1,0:T(8,128)(2,1)}, u32[]{:S(2)}) copy-start(s16[8,2,4,32,256]{4,3,2,1,0:T(8,128)(2,1)} %copy-done) | copy-start | bytes 3145732
  164.6 2.9 %copy-start.4 = (bf16[256,512]{1,0:T(8,128)(2,1)S(1)}, bf16[256,512]{1,0:T(8,128)(2,1)}, u32[]{:S(2)}) copy-start(bf16[256,512]{1,0:T(8,128)(2,1)} %constant.19.clone.columns_ref) | copy-start | bytes 786436

commit v4 on v1

--- a/solution.py
+++ b/solution.py
@@ -378,10 +378,13 @@
 def join_kernel(
     views,
     updated,
+    partial,
     *refs,
 ):
     if updated:
         mine_ref, other_ref, *refs = refs
+    if partial:
+        partial_ref, *refs = refs
     (
     place_ref,
     estimate_ref,
@@ -452,7 +455,10 @@
     def _():
         for b in range(blocks):
             logs = jnp.log(product_ref[b]) * (1.0 / views)
-            out_ref[:, b * ROWS : (b + 1) * ROWS] = logs.reshape(depth, ROWS, width)
+            logs = logs.reshape(depth, ROWS, width)
+            if partial:
+                logs = logs + partial_ref[:, b * ROWS : (b + 1) * ROWS]
+            out_ref[:, b * ROWS : (b + 1) * ROWS] = logs
 
 
 def whole(shape):
@@ -547,6 +553,7 @@
             ),
             out_shape=jax.ShapeDtypeStruct(spectrum_shape, F32),
             cost_estimate=cost(row_flops, 6 * volume),
+            compiler_params=pltpu.CompilerParams(vmem_limit_bytes=16 * 1024 * 1024),
             name="spectrum",
         )(place, payload, row_turn)
 
@@ -567,6 +574,7 @@
             ),
             out_shape=jax.ShapeDtypeStruct(payload_shape, jnp.int16),
             cost_estimate=cost(2 * row_flops * chunk, payload_bytes + 10 * volume),
+            compiler_params=pltpu.CompilerParams(vmem_limit_bytes=16 * 1024 * 1024),
             name="cross",
         )(view_map, place, payload, row_turn, row_back, mine, other)
 
@@ -593,6 +601,7 @@
             out_shape=jax.ShapeDtypeStruct((slots, depth, rows, width), F32),
             input_output_aliases=aliases,
             cost_estimate=cost(2 * chunk * volume * 9 * width, payload_bytes * 1.5),
+            compiler_params=pltpu.CompilerParams(vmem_limit_bytes=16 * 1024 * 1024),
             name="last",
         )(*operands)
 
@@ -618,19 +627,18 @@
 
     forward, backward, columns = filters()
 
-    def join(estimate, strips, rims, logs=None):
+    def join(estimate, strips, rims, logs=None, partial=None, start=0, count=slots):
         def slot_block(shape):
-            return pl.BlockSpec((1,) + shape, lambda s: (s,) + (0,) * len(shape))
+            return pl.BlockSpec((1,) + shape, lambda s: (s + start,) + (0,) * len(shape))
 
         updated = logs is not None
         field = jax.ShapeDtypeStruct((depth, rows, width), F32)
-        extra_specs = []
-        if updated:
-            extra_specs = [whole((depth, rows, width))] * 2
+        extra = list(logs or ()) + ([] if partial is None else [partial])
+        at = start // count
         return pl.pallas_call(
-            functools.partial(join_kernel, views, updated),
-            grid=(slots,),
-            in_specs=extra_specs
+            functools.partial(join_kernel, views, updated, partial is not None),
+            grid=(count,),
+            in_specs=[whole((depth, rows, width))] * len(extra)
             + [
                 pl.BlockSpec(memory_space=pltpu.SMEM),
                 whole((depth, rows, width)),
@@ -639,7 +647,7 @@
                 slot_block((depth, rows, width)),
                 slot_block((depth, ROWS, width)),
                 slot_block((depth, ROWS, width)),
-                whole((slots, size, 3 * size)),
+                pl.BlockSpec((count, size, 3 * size), lambda s: (at, 0, 0)),
                 slot_block((size, 3 * size)),
                 slot_block((width, width)),
             ],
@@ -647,14 +655,14 @@
             out_shape=[field] * (1 + updated),
             scratch_shapes=[
                 pltpu.VMEM((blocks + 4, size, width), BF16),
-                pltpu.VMEM((slots, blocks + 2, size, width), BF16),
+                pltpu.VMEM((count, blocks + 2, size, width), BF16),
                 pltpu.VMEM((blocks + 2, size, width), F32),
                 pltpu.VMEM((blocks + 2, size, width), BF16),
                 pltpu.VMEM((blocks, size, width), F32),
             ],
-            cost_estimate=cost(2 * slots * size * width * ((blocks + 2) * (3 * size + 2 * width) + blocks * 3 * size), 12e6),
+            cost_estimate=cost(2 * count * size * width * ((blocks + 2) * (3 * size + 2 * width) + blocks * 3 * size), 12e6),
             name="join",
-        )(*(logs or ()), place, estimate, *strips, observed, *rims, forward, backward, columns)
+        )(*extra, place, estimate, *strips, observed, *rims, forward, backward, columns)
 
     sent_a = turn(first(0))
     payload_b = first(chunk)
@@ -665,7 +673,8 @@
     back_a = turn(crossed_a)
     first_strips = swap_strips([rim[slots] for rim in first_rims])
 
-    (logs,) = join(initial, first_strips, first_rims)
+    (logs,) = join(initial, first_strips, first_rims, start=0, count=chunk)
+    (logs,) = join(initial, first_strips, first_rims, partial=logs, start=chunk, count=chunk)
     total = (logs, swap_cores(logs))
 
     def updated_rows(at):

time: 170 us -> 172 us (1.012)
  Pallas kernels: 66.6 us -> 61.3 us
  waiting for transfers between devices: 52.8 us -> 56.4 us
  other arithmetic: 5.03 us -> 8.4 us
    pallas_call x2, Pallas kernels: 13.5 us -> 8.31 us  [crossed(): pl.pallas_call(cross_kernel, grid_spec=pltpu.PrefetchScalarGridSpec(num_s...]
    pallas_call x2 -> x3, Pallas kernels: 25.2 us -> 29.6 us  [join(): pl.pallas_call(functools.partial(join_kernel, views, updated, partial is...]
    ppermute x2, waiting for transfers between devices: 23.2 us -> 26.6 us  [send_rims(): below = lax.ppermute(high, 'gz', [(i, i + 1) for i in range(count - 1)])]
    unnamed x34 -> x50, local copies, waits for them, and re-layouts: 3.67 us -> 6.73 us
    pallas_call x2, Pallas kernels: 10.2 us -> 7.92 us  [last(): pl.pallas_call(last_kernel, grid_spec=pltpu.PrefetchScalarGridSpec(num_sc...]
    pallas_call x1, Pallas kernels: 3.43 us -> 1.2 us  [reference_spectrum(): pl.pallas_call(spectrum_kernel, grid_spec=pltpu.PrefetchScalarGridSpec(nu...]
  transfers between devices with their start and end apart: 13 -> 13, of which waited for: 5 -> 5; matrix products, arithmetic and copies ran while one was open for 4% -> 4% of each run, Pallas kernels for 36% -> 33%
where the time goes in v4:
time: 172 us; the launch traced here: 171 us
  Pallas kernels  61.3 us (36%)
  waiting for transfers between devices  56.4 us (33%)
  starting transfers between devices  37.2 us (22%)
  other arithmetic  8.4 us (5%)
  local copies, waits for them, and re-layouts  6.82 us (4%)
    pallas_call x3, Pallas kernels, join(): pl.pallas_call(functools.partial(join_kernel, views, updated, partial is...  29.6 us
    ppermute x2, waiting for transfers between devices, send_rims(): below = lax.ppermute(high, 'gz', [(i, i + 1) for i in range(count - 1)])  26.6 us
    all_to_all x4, waiting for transfers between devices, turn(): lax.all_to_all(payload, 'gz', split_axis=0, concat_axis=0, tiled=True)  25.6 us
    all_to_all x4, starting transfers between devices, turn(): lax.all_to_all(payload, 'gz', split_axis=0, concat_axis=0, tiled=True)  25.5 us
    pallas_call x2, Pallas kernels, first(): pl.pallas_call(first_kernel, grid_spec=pltpu.PrefetchScalarGridSpec(num_s...  10.2 us
    ppermute x2, starting transfers between devices, send_rims(): below = lax.ppermute(high, 'gz', [(i, i + 1) for i in range(count - 1)])  8.52 us
    pallas_call x2, Pallas kernels, crossed(): pl.pallas_call(cross_kernel, grid_spec=pltpu.PrefetchScalarGridSpec(num_s...  8.31 us
    pallas_call x2, Pallas kernels, last(): pl.pallas_call(last_kernel, grid_spec=pltpu.PrefetchScalarGridSpec(num_sc...  7.92 us
  transfers between devices with their start and end apart: 13, of which 5 were waited for; matrix products, arithmetic and copies ran while one was open for 4% of the time, Pallas kernels for 33%

profile of v4, /device:TPU:0, one launch (start us, length us, event | category | flops | bytes accessed | tf_op | source)
XLA Modules:
  0.0 171.0 jit_solution(3937413041092427522)
XLA Ops:
  0.6 5.1 %first.2 = s16[8,2,4,32,256]{4,3,2,1,0:T(8,128)(2,1)} custom-call(s32[8]{0:T(128)} %map_ref.13, bf16[4,32,32,256]{3,2,1,0:T(8,128)(2,1)} %observed_ref.3, bf16[256,512]{1,0:T(8,128)(2,1)} %constant.18.clone.columns_ref), custom_call_target="tpu_custom_call" | custom-call | flops 2147483648 | bytes 2097152 | tf_op jit(solution)/shard_map/first/pallas_call | solution.py:522
  5.7 7.3 %all-to-all-start = ((s16[8,2,4,32,256]{4,3,2,1,0:T(8,128)(2,1)}), s16[8,2,4,32,256]{4,3,2,1,0:T(8,128)(2,1)S(1)}, u32[]{:S(2)}, u32[]{:S(2)}) async-start(s16[8,2,4,32,256]{4,3,2,1,0:T(8,128)(2,1)} %first.2), calls=%async_computation | async-start | bytes 2097152 | tf_op jit(solution)/shard_map/all_to_all | solution.py:473
  13.0 5.1 %first.3 = s16[8,2,4,32,256]{4,3,2,1,0:T(8,128)(2,1)} custom-call(s32[8]{0:T(128)} %map_ref.13, bf16[4,32,32,256]{3,2,1,0:T(8,128)(2,1)} %observed_ref.3, bf16[256,512]{1,0:T(8,128)(2,1)} %constant.18.clone.columns_ref), custom_call_target="tpu_custom_call" | custom-call | flops 2147483648 | bytes 2097152 | tf_op jit(solution)/shard_map/first/pallas_call | solution.py:522
  18.1 20.7 %all-to-all-done.in_ref = s16[8,2,4,32,256]{4,3,2,1,0:T(8,128)(2,1)S(1)} async-done(((s16[8,2,4,32,256]{4,3,2,1,0:T(8,128)(2,1)}), s16[8,2,4,32,256]{4,3,2,1,0:T(8,128)(2,1)S(1)}, u32[]{:S(2)}, u32[]{:S(2)}) %all-to-all-start) | async-done | bytes 1048608 | tf_op jit(solution)/shard_map/all_to_all | solution.py:473
  38.8 3.6 %all-to-all-start.1 = ((s16[8,2,4,32,256]{4,3,2,1,0:T(8,128)(2,1)}), s16[8,2,4,32,256]{4,3,2,1,0:T(8,128)(2,1)S(1)}, u32[]{:S(2)}, u32[]{:S(2)}) async-start(s16[8,2,4,32,256]{4,3,2,1,0:T(8,128)(2,1)} %first.3), calls=%async_computation.1 | async-start | bytes 2097152 | tf_op jit(solution)/shard_map/all_to_all | solution.py:473
  42.5 1.2 spectrum.1.mine_ref
  43.8 1.2 fusion.15
  45.2 4.0 %collective-permute-start = (bf16[5,32,8,256]{3,2,1,0:T(8,128)(2,1)S(1)}, bf16[5,32,8,256]{3,2,1,0:T(8,128)(2,1)S(1)}, u32[]{:S(2)}, u32[]{:S(2)}) collective-permute-start(bf16[5,32,8,256]{3,2,1,0:T(8,128)(2,1)S(1)} %pad_maximum_fusion), channel_id=1, source_target_pairs={{0,2},{2,4},{4,6},{6,8},{8,10},{10,12},{12,14},{1,3},{3,5},{5,7},{... | collective-permute-start | bytes 1966088 | tf_op jit(solution)/shard_map/ppermute | solution.py:482
  49.2 1.3 collective-permute-start.1
  50.6 4.1 %cross.2 = s16[8,2,4,32,256]{4,3,2,1,0:T(8,128)(2,1)S(1)} custom-call(s32[8]{0:T(128)S(1)} %copy-done.8, s32[2]{0:T(128)S(1)} %pad_add_fusion.place_ref.refs_0_.refs_1_.refs_2_, s16[8,2,4,32,256]{4,3,2,1,0:T(8,128)(2,1)S(1)} %all-to-all-done.in_ref, bf16[256,512]{1,0:T(8,128)(2,1)S(1)} %copy-done.5, bf16[256,512]{1,0:T(8,128)(2,1)S(1)} %copy-done.12, ...), custom_call_target="tpu_custom_call" | custom-call | flops 1610612736 | bytes 4718592 | tf_op jit(solution)/shard_map/cross/pallas_call | solution.py:561
  54.7 1.0 copy-done.2
  55.7 26.6 %collective-permute-done.refs_5_.refs_6_.refs_7_ = bf16[5,32,8,256]{3,2,1,0:T(8,128)(2,1)S(1)} collective-permute-done((bf16[5,32,8,256]{3,2,1,0:T(8,128)(2,1)S(1)}, bf16[5,32,8,256]{3,2,1,0:T(8,128)(2,1)S(1)}, u32[]{:S(2)}, u32[]{:S(2)}) %collective-permute-start) | collective-permute-done | bytes 655392 | tf_op jit(solution)/shard_map/ppermute | solution.py:482
  83.1 0.9 copy-done.19
  86.1 4.0 %filters.1 = (bf16[4,256,768]{2,1,0:T(8,128)(2,1)}, bf16[4,256,768]{2,1,0:T(8,128)(2,1)}, bf16[4,256,256]{2,1,0:T(8,128)(2,1)}) custom-call(s32[2]{0:T(128)} %copy-done.6, s32[8]{0:T(128)} %map_ref.13, s32[8,2]{1,0:T(8,128)} %copy.12.shift_ref, f32[8,3,15]{2,1,0:T(4,128)} %copy.13.psf_ref), custom_call_target="tpu_custom_call" | custom-call | flops 15728640 | bytes 3670016 | tf_op jit(solution)/shard_map/filters/pallas_call | solution.py:610
  90.1 8.0 %all-to-all-start.3 = ((s16[8,2,4,32,256]{4,3,2,1,0:T(8,128)(2,1)}), s16[8,2,4,32,256]{4,3,2,1,0:T(8,128)(2,1)S(1)}, u32[]{:S(2)}, u32[]{:S(2)}) async-start(s16[8,2,4,32,256]{4,3,2,1,0:T(8,128)(2,1)} %copy-done.2), calls=%async_computation.3 | async-start | bytes 2097152 | tf_op jit(solution)/shard_map/all_to_all | solution.py:473
  98.1 8.0 %join.3.refs_0_ = f32[32,32,256]{2,1,0:T(8,128)} custom-call(s32[2]{0:T(128)} %copy-done.6, f32[32,32,256]{2,1,0:T(8,128)} %refs_3_.1, bf16[2,32,8,256]{3,2,1,0:T(8,128)(2,1)} %pad_maximum_fusion.2.refs_2_.refs_3_, bf16[2,32,8,256]{3,2,1,0:T(8,128)(2,1)} %collective-permute-done.3.refs_3_.refs_4_, bf16[4,32,32,256]{3,2,1,0:T(8,128)(2,1)} %observed_ref.3, ...), custom_call_target="tpu_custom_call" | custom-call | flops 2818572288 | bytes 12000000 | tf_op jit(solution)/shard_map/join/pallas_call | solution.py:638
  106.2 8.3 %join.4.refs_0_ = f32[32,32,256]{2,1,0:T(8,128)} custom-call(f32[32,32,256]{2,1,0:T(8,128)} %join.3.refs_0_, s32[2]{0:T(128)} %copy-done.6, f32[32,32,256]{2,1,0:T(8,128)} %refs_3_.1, bf16[2,32,8,256]{3,2,1,0:T(8,128)(2,1)} %pad_maximum_fusion.2.refs_2_.refs_3_, bf16[2,32,8,256]{3,2,1,0:T(8,128)(2,1)} %collective-permute-done.3.refs_3_.refs_4_, ...), custom_call_target="tpu_custom_call" | custom-call | flops 2818572288 | bytes 12000000 | tf_op jit(solution)/shard_map/join/pallas_call | solution.py:638
  114.8 2.7 %collective-permute-done.4.refs_1_ = f32[32,32,256]{2,1,0:T(8,128)S(1)} collective-permute-done((f32[32,32,256]{2,1,0:T(8,128)}, f32[32,32,256]{2,1,0:T(8,128)S(1)}, u32[]{:S(2)}, u32[]{:S(2)}) %collective-permute-start.4) | collective-permute-done | bytes 1048608 | tf_op jit(solution)/shard_map/ppermute | solution.py:489
  117.5 2.8 %fusion.16 = (bf16[32,8,256]{2,1,0:T(8,128)(2,1)}, bf16[32,8,256]{2,1,0:T(8,128)(2,1)S(1)}) fusion(f32[32,32,256]{2,1,0:T(8,128)S(1)} %collective-permute-done.4.refs_1_, f32[32,32,256]{2,1,0:T(8,128)} %join.4.refs_0_, f32[32,32,256]{2,1,0:T(8,128)} %refs_3_.1, pred[]{:T(512)S(6)} %eq.2), kind=kLoop, calls=%fused_computation.29 | loop fusion | flops 917504 | bytes 3407873 | tf_op jit(solution)/shard_map/jit(_where)/select_n | solution.py:477
  120.2 4.6 %collective-permute-start.5 = (bf16[32,8,256]{2,1,0:T(8,128)(2,1)}, bf16[32,8,256]{2,1,0:T(8,128)(2,1)}, u32[]{:S(2)}, u32[]{:S(2)}) collective-permute-start(bf16[32,8,256]{2,1,0:T(8,128)(2,1)} %get-tuple-element.18), channel_id=1, source_target_pairs={{0,2},{2,4},{4,6},{6,8},{8,10},{10,12},{12,14},{1,3},{3,5},{5,7},{... | collective-permute-start | bytes 393224 | tf_op jit(solution)/shard_map/ppermute | solution.py:482
  124.8 1.3 collective-permute-start.6
  126.1 4.2 %cross.3 = s16[8,2,4,32,256]{4,3,2,1,0:T(8,128)(2,1)S(1)} custom-call(s32[8]{0:T(128)S(1)} %copy-done.9, s32[2]{0:T(128)S(1)} %copy-done.7, s16[8,2,4,32,256]{4,3,2,1,0:T(8,128)(2,1)S(1)} %all-to-all-done.1.in_ref, bf16[256,512]{1,0:T(8,128)(2,1)S(1)} %copy-done.5, bf16[256,512]{1,0:T(8,128)(2,1)S(1)} %copy-done.13, f32[4,256,256]{2,1,0:T(8,128)S(1)} %spectrum.1.mine_ref, ...), custom_call_target="tpu_custom_call" | custom-call | flops 1610612736 | bytes 4718592 | tf_op jit(solution)/shard_map/cross/pallas_call | solution.py:561
  130.4 1.0 copy-done.3
  131.4 1.0 copy-done
  132.3 6.6 %all-to-all-start.2 = ((s16[8,2,4,32,256]{4,3,2,1,0:T(8,128)(2,1)}), s16[8,2,4,32,256]{4,3,2,1,0:T(8,128)(2,1)S(1)}, u32[]{:S(2)}, u32[]{:S(2)}) async-start(s16[8,2,4,32,256]{4,3,2,1,0:T(8,128)(2,1)} %copy-done.3), calls=%async_computation.2 | async-start | bytes 2097152 | tf_op jit(solution)/shard_map/all_to_all | solution.py:473
  138.9 1.0 pad_maximum_fusion.3.refs_4_
  140.1 1.5 collective-permute-done.7.refs_5_
  142.3 13.2 %join.5 = (f32[32,32,256]{2,1,0:T(8,128)}, f32[32,32,256]{2,1,0:T(8,128)}) custom-call(f32[32,32,256]{2,1,0:T(8,128)} %join.4.refs_0_, f32[32,32,256]{2,1,0:T(8,128)} %copy-done.15, s32[2]{0:T(128)} %copy-done.6, f32[32,32,256]{2,1,0:T(8,128)} %refs_3_.1, bf16[2,32,8,256]{3,2,1,0:T(8,128)(2,1)} %copy-done.20, bf16[2,32,8,256]{3,2,1,0:T(8,128)(2,1)} %copy-done.23, ...), custom_call_target="tpu_custom_call" | custom-call | flops 5637144576 | bytes 12000000 | tf_op jit(solution)/shard_map/join/pallas_call | solution.py:638
  155.7 4.0 %last.2.rest_0_ = f32[4,32,32,256]{3,2,1,0:T(8,128)} custom-call(s32[8]{0:T(128)S(1)} %copy-done.9, s16[8,2,4,32,256]{4,3,2,1,0:T(8,128)(2,1)S(1)} %copy-done.1, bf16[256,512]{1,0:T(8,128)(2,1)S(1)} %copy-done.4), custom_call_target="tpu_custom_call" | custom-call | flops 2415919104 | bytes 3145728 | tf_op jit(solution)/shard_map/last/pallas_call | solution.py:592
  159.6 4.9 %all-to-all-done.2.in_ref = s16[8,2,4,32,256]{4,3,2,1,0:T(8,128)(2,1)S(1)} async-done(((s16[8,2,4,32,256]{4,3,2,1,0:T(8,128)(2,1)}), s16[8,2,4,32,256]{4,3,2,1,0:T(8,128)(2,1)S(1)}, u32[]{:S(2)}, u32[]{:S(2)}) %all-to-all-start.2) | async-done | bytes 1048608 | tf_op jit(solution)/shard_map/all_to_all | solution.py:473
  164.5 4.0 %last.3 = f32[4,32,32,256]{3,2,1,0:T(8,128)} custom-call(s32[8]{0:T(128)S(1)} %copy-done.9, s16[8,2,4,32,256]{4,3,2,1,0:T(8,128)(2,1)S(1)} %all-to-all-done.2.in_ref, bf16[256,512]{1,0:T(8,128)(2,1)S(1)} %copy-done.4, f32[4,32,32,256]{3,2,1,0:T(8,128)} %last.2.rest_0_), custom_call_target="tpu_custom_call", output_to_operand_aliasing={{}: (3, {})} | custom-call | flops 2415919104 | bytes 3145728 | tf_op jit(solution)/shard_map/last/pallas_call | solution.py:592
  168.5 2.5 %exponential_multiply_fusion = f32[32,32,256]{2,1,0:T(8,128)} fusion(f32[32,32,256]{2,1,0:T(8,128)S(1)} %copy-done.17, f32[32,32,256]{2,1,0:T(8,128)S(1)} %copy-done.16, f32[32,32,256]{2,1,0:T(8,128)} %collective-permute-done.8), kind=kLoop, calls=%fused_computation | loop fusion | flops 524288 | bytes 4194304 | tf_op jit(solution)/shard_map/mul | solution.py:691
  (66 shorter events, 4.5 us)
Async XLA Ops:
  5.7 33.1 %all-to-all-start = ((s16[8,2,4,32,256]{4,3,2,1,0:T(8,128)(2,1)}), s16[8,2,4,32,256]{4,3,2,1,0:T(8,128)(2,1)S(1)}, u32[]{:S(2)}, u32[]{:S(2)}) async-start(s16[8,2,4,32,256]{4,3,2,1,0:T(8,128)(2,1)} %first.2), calls=%async_computation | async-start | bytes 2097152 | tf_op jit(solution)/shard_map/all_to_all | solution.py:473
  18.1 24.4 %copy-start.5 = (bf16[256,512]{1,0:T(8,128)(2,1)S(1)}, bf16[256,512]{1,0:T(8,128)(2,1)}, u32[]{:S(2)}) copy-start(bf16[256,512]{1,0:T(8,128)(2,1)} %constant.20.clone.rows_ref) | copy-start | bytes 786436
  38.8 51.3 %all-to-all-start.1 = ((s16[8,2,4,32,256]{4,3,2,1,0:T(8,128)(2,1)}), s16[8,2,4,32,256]{4,3,2,1,0:T(8,128)(2,1)S(1)}, u32[]{:S(2)}, u32[]{:S(2)}) async-start(s16[8,2,4,32,256]{4,3,2,1,0:T(8,128)(2,1)} %first.3), calls=%async_computation.1 | async-start | bytes 2097152 | tf_op jit(solution)/shard_map/all_to_all | solution.py:473
  42.5 8.1 %copy-start.6 = (s32[2]{0:T(128)}, s32[2]{0:T(128)S(1)}, u32[]{:S(2)}) copy-start(s32[2]{0:T(128)S(1)} %pad_add_fusion.place_ref.refs_0_.refs_1_.refs_2_) | copy-start | bytes 28
  42.5 2.5 %copy-start.14 = (bf16[4,32,32,256]{3,2,1,0:T(8,128)(2,1)S(1)}, bf16[4,32,32,256]{3,2,1,0:T(8,128)(2,1)}, u32[]{:S(2)}) copy-start(bf16[4,32,32,256]{3,2,1,0:T(8,128)(2,1)} %observed_ref.3) | copy-start | bytes 6291460
  43.7 6.9 %collective-permute-start.2 = (f32[4,256,256]{2,1,0:T(8,128)S(1)}, f32[4,256,256]{2,1,0:T(8,128)S(1)}, u32[]{:S(2)}, u32[]{:S(2)}) collective-permute-start(f32[4,256,256]{2,1,0:T(8,128)S(1)} %spectrum.1.mine_ref), channel_id=1, source_target_pairs={{0,1},{1,0},{2,3},{3,2},{4,5},{5,4},{6,7},{7,6},{8,9},{9,8},{10,11... | collective-permute-start | bytes 3145736 | tf_op jit(solution)/shard_map/ppermute | solution.py:489
  45.0 5.6 %copy-start.8 = (s32[8]{0:T(128)S(1)}, s32[8]{0:T(128)}, u32[]{:S(2)}) copy-start(s32[8]{0:T(128)} %map_ref.13) | copy-start | bytes 100
  45.0 5.6 %copy-start.12 = (bf16[256,512]{1,0:T(8,128)(2,1)S(1)}, bf16[256,512]{1,0:T(8,128)(2,1)}, u32[]{:S(2)}) copy-start(bf16[256,512]{1,0:T(8,128)(2,1)} %constant.21.clone.back_ref) | copy-start | bytes 786436
  45.2 37.1 %collective-permute-start = (bf16[5,32,8,256]{3,2,1,0:T(8,128)(2,1)S(1)}, bf16[5,32,8,256]{3,2,1,0:T(8,128)(2,1)S(1)}, u32[]{:S(2)}, u32[]{:S(2)}) collective-permute-start(bf16[5,32,8,256]{3,2,1,0:T(8,128)(2,1)S(1)} %pad_maximum_fusion), channel_id=1, source_target_pairs={{0,2},{2,4},{4,6},{6,8},{8,10},{10,12},{12,14},{1,3},{3,5},{5,7},{... | collective-permute-start | bytes 1966088 | tf_op jit(solution)/shard_map/ppermute | solution.py:482
  49.2 35.5 %copy-start.21 = (f32[8,3,15]{2,0,1:T(8,128)S(1)}, f32[8,3,15]{2,0,1:T(8,128)}, u32[]{:S(2)}) copy-start(f32[8,3,15]{2,0,1:T(8,128)} %param.11) | copy-start | bytes 4324
  49.2 36.2 %copy-start.22 = (s32[8,2]{0,1:T(2,128)S(1)}, s32[8,2]{0,1:T(2,128)}, u32[]{:S(2)}) copy-start(s32[8,2]{0,1:T(2,128)} %param.12) | copy-start | bytes 196
  49.2 33.0 %collective-permute-start.1 = (bf16[5,32,8,256]{3,2,1,0:T(8,128)(2,1)S(1)}, bf16[5,32,8,256]{3,2,1,0:T(8,128)(2,1)S(1)}, u32[]{:S(2)}, u32[]{:S(2)}) collective-permute-start(bf16[5,32,8,256]{3,2,1,0:T(8,128)(2,1)S(1)} %pad_maximum_fusion.1), channel_id=1, source_target_pairs={{2,0},{4,2},{6,4},{8,6},{10,8},{12,10},{14,12},{3,1},{5,3},{7,5},{... | collective-permute-start | bytes 1966088 | tf_op jit(solution)/shard_map/ppermute | solution.py:483
  50.6 4.1 %copy-start.10 = (f32[4,256,256]{2,1,0:T(8,128)}, f32[4,256,256]{2,1,0:T(8,128)S(1)}, u32[]{:S(2)}) copy-start(f32[4,256,256]{2,1,0:T(8,128)S(1)} %collective-permute-done.2.other_ref) | copy-start | bytes 3145732
  84.8 13.4 %collective-permute-start.3 = (bf16[2,32,8,256]{3,2,1,0:T(8,128)(2,1)}, bf16[2,32,8,256]{3,2,1,0:T(8,128)(2,1)}, u32[]{:S(2)}, u32[]{:S(2)}) collective-permute-start(bf16[2,32,8,256]{3,2,1,0:T(8,128)(2,1)} %pad_maximum_fusion.2.refs_2_.refs_3_), channel_id=1, source_target_pairs={{0,1},{1,0},{2,3},{3,2},{4,5},{5,4},{6,7},{7,6},{8,9},{9,8},{10,11... | collective-permute-start | bytes 786440 | tf_op jit(solution)/shard_map/ppermute | solution.py:489
  90.1 41.2 %all-to-all-start.3 = ((s16[8,2,4,32,256]{4,3,2,1,0:T(8,128)(2,1)}), s16[8,2,4,32,256]{4,3,2,1,0:T(8,128)(2,1)S(1)}, u32[]{:S(2)}, u32[]{:S(2)}) async-start(s16[8,2,4,32,256]{4,3,2,1,0:T(8,128)(2,1)} %copy-done.2), calls=%async_computation.3 | async-start | bytes 2097152 | tf_op jit(solution)/shard_map/all_to_all | solution.py:473
  114.5 11.6 %copy-start.7 = (s32[2]{0:T(128)S(1)}, s32[2]{0:T(128)}, u32[]{:S(2)}) copy-start(s32[2]{0:T(128)} %copy-done.6) | copy-start | bytes 28
  114.5 11.6 %copy-start.9 = (s32[8]{0:T(128)S(1)}, s32[8]{0:T(128)}, u32[]{:S(2)}) copy-start(s32[8]{0:T(128)} %map_ref.13) | copy-start | bytes 100
  114.5 11.6 %copy-start.11 = (f32[4,256,256]{2,1,0:T(8,128)S(1)}, f32[4,256,256]{2,1,0:T(8,128)}, u32[]{:S(2)}) copy-start(f32[4,256,256]{2,1,0:T(8,128)} %copy-done.10) | copy-start | bytes 3145732
  114.5 11.6 %copy-start.13 = (bf16[256,512]{1,0:T(8,128)(2,1)S(1)}, bf16[256,512]{1,0:T(8,128)(2,1)}, u32[]{:S(2)}) copy-start(bf16[256,512]{1,0:T(8,128)(2,1)} %constant.21.clone.back_ref) | copy-start | bytes 786436
  114.5 2.9 %collective-permute-start.4 = (f32[32,32,256]{2,1,0:T(8,128)}, f32[32,32,256]{2,1,0:T(8,128)S(1)}, u32[]{:S(2)}, u32[]{:S(2)}) collective-permute-start(f32[32,32,256]{2,1,0:T(8,128)} %join.4.refs_0_), channel_id=1, source_target_pairs={{0,1},{1,0},{2,3},{3,2},{4,5},{5,4},{6,7},{7,6},{8,9},{9,8},{10,11... | collective-permute-start | bytes 3145736 | tf_op jit(solution)/shard_map/ppermute | solution.py:489
  117.5 7.3 %copy-start.15 = (f32[32,32,256]{2,1,0:T(8,128)}, f32[32,32,256]{2,1,0:T(8,128)S(1)}, u32[]{:S(2)}) copy-start(f32[32,32,256]{2,1,0:T(8,128)S(1)} %collective-permute-done.4.refs_1_) | copy-start | bytes 3145732
  120.2 18.7 %collective-permute-start.5 = (bf16[32,8,256]{2,1,0:T(8,128)(2,1)}, bf16[32,8,256]{2,1,0:T(8,128)(2,1)}, u32[]{:S(2)}, u32[]{:S(2)}) collective-permute-start(bf16[32,8,256]{2,1,0:T(8,128)(2,1)} %get-tuple-element.18), channel_id=1, source_target_pairs={{0,2},{2,4},{4,6},{6,8},{8,10},{10,12},{12,14},{1,3},{3,5},{5,7},{... | collective-permute-start | bytes 393224 | tf_op jit(solution)/shard_map/ppermute | solution.py:482
  124.8 14.1 %collective-permute-start.6 = (bf16[32,8,256]{2,1,0:T(8,128)(2,1)S(1)}, bf16[32,8,256]{2,1,0:T(8,128)(2,1)}, u32[]{:S(2)}, u32[]{:S(2)}) collective-permute-start(bf16[32,8,256]{2,1,0:T(8,128)(2,1)S(1)} %get-tuple-element.19), channel_id=1, source_target_pairs={{2,0},{4,2},{6,4},{8,6},{10,8},{12,10},{14,12},{3,1},{5,3},{7,5},{... | collective-permute-start | bytes 393224 | tf_op jit(solution)/shard_map/ppermute | solution.py:483
  130.4 1.0 copy-start.3
  132.3 32.2 %all-to-all-start.2 = ((s16[8,2,4,32,256]{4,3,2,1,0:T(8,128)(2,1)}), s16[8,2,4,32,256]{4,3,2,1,0:T(8,128)(2,1)S(1)}, u32[]{:S(2)}, u32[]{:S(2)}) async-start(s16[8,2,4,32,256]{4,3,2,1,0:T(8,128)(2,1)} %copy-done.3), calls=%async_computation.2 | async-start | bytes 2097152 | tf_op jit(solution)/shard_map/all_to_all | solution.py:473
  139.9 1.6 copy-start.20
  140.0 15.7 %copy-start.1 = (s16[8,2,4,32,256]{4,3,2,1,0:T(8,128)(2,1)S(1)}, s16[8,2,4,32,256]{4,3,2,1,0:T(8,128)(2,1)}, u32[]{:S(2)}) copy-start(s16[8,2,4,32,256]{4,3,2,1,0:T(8,128)(2,1)} %copy-done) | copy-start | bytes 3145732
  140.0 15.7 %copy-start.4 = (bf16[256,512]{1,0:T(8,128)(2,1)S(1)}, bf16[256,512]{1,0:T(8,128)(2,1)}, u32[]{:S(2)}) copy-start(bf16[256,512]{1,0:T(8,128)(2,1)} %constant.19.clone.columns_ref) | copy-start | bytes 786436
  140.0 1.6 collective-permute-start.7
  155.5 13.0 %collective-permute-start.8 = (f32[32,32,256]{2,1,0:T(8,128)}, f32[32,32,256]{2,1,0:T(8,128)}, u32[]{:S(2)}, u32[]{:S(2)}) collective-permute-start(f32[32,32,256]{2,1,0:T(8,128)} %get-tuple-element.16), channel_id=1, source_target_pairs={{0,1},{1,0},{2,3},{3,2},{4,5},{5,4},{6,7},{7,6},{8,9},{9,8},{10,11... | collective-permute-start | bytes 3145736 | tf_op jit(solution)/shard_map/ppermute | solution.py:489
  159.6 8.9 %copy-start.16 = (f32[32,32,256]{2,1,0:T(8,128)S(1)}, f32[32,32,256]{2,1,0:T(8,128)}, u32[]{:S(2)}) copy-start(f32[32,32,256]{2,1,0:T(8,128)} %get-tuple-element.16) | copy-start | bytes 3145732
  159.6 8.9 %copy-start.17 = (f32[32,32,256]{2,1,0:T(8,128)S(1)}, f32[32,32,256]{2,1,0:T(8,128)}, u32[]{:S(2)}) copy-start(f32[32,32,256]{2,1,0:T(8,128)} %get-tuple-element.15) | copy-start | bytes 3145732
  (5 other events, 4.4 us)

commit v5 on v4

--- a/solution.py
+++ b/solution.py
@@ -391,8 +391,8 @@
     strips_ref,
     swapped_ref,
     observed_ref,
-    seen_below_ref,
-    seen_above_ref,
+    seen_first_ref,
+    seen_second_ref,
     forward_ref,
     backward_ref,
     columns_ref,
@@ -409,6 +409,7 @@
     blocks = rows // ROWS
     slots = forward_ref.shape[0]
     step = pl.program_id(0)
+    odd = place_ref[1] % 2 == 1
 
     @pl.when(step == 0)
     def _():
@@ -416,7 +417,8 @@
             logs = mine_ref[...] + other_ref[...]
             now_ref[...] = estimate_ref[...] * jnp.exp(logs.reshape(depth, rows, width))
         first_core = place_ref[0] == 0
-        for side, near, far in ((0, 1, 0), (1, blocks + 2, blocks + 3)):
+        for below, near, far in ((True, 1, 0), (False, blocks + 2, blocks + 3)):
+            side = jnp.where(odd == below, 0, 1)
             own = strips_ref[side].astype(F32).reshape(size, width)
             swapped = swapped_ref[side].astype(F32).reshape(size, width)
             cells_ref[near] = jnp.where(first_core, own, swapped).astype(BF16)
@@ -437,9 +439,9 @@
     blurred_ref[...] = blurred.reshape(blocks + 2, size, width)
     for b in range(blocks + 2):
         if b == 0:
-            seen = seen_below_ref[0].astype(F32)
+            seen = jnp.where(odd, seen_first_ref[0].astype(F32), seen_second_ref[0].astype(F32))
         elif b == blocks + 1:
-            seen = seen_above_ref[0].astype(F32)
+            seen = jnp.where(odd, seen_second_ref[0].astype(F32), seen_first_ref[0].astype(F32))
         else:
             seen = observed_ref[0, :, (b - 1) * ROWS : b * ROWS].astype(F32)
         seen = seen.reshape(size, width)
@@ -477,11 +479,16 @@
     return jnp.where(lax.axis_index("view") == 0, near, far)
 
 
-def send_rims(low, high):
+def by_parity(for_odd, for_even):
+    return jnp.where(lax.axis_index("gz") % 2 == 1, for_odd, for_even)
+
+
+def send_rims(near_pair, far_pair):
     count = lax.axis_size("gz")
-    below = lax.ppermute(high, "gz", [(i, i + 1) for i in range(count - 1)])
-    above = lax.ppermute(low, "gz", [(i + 1, i) for i in range(count - 1)])
-    return below, above
+    first = lax.ppermute(near_pair, "gz", [(i, i ^ 1) for i in range(count)])
+    links = [(i, i + 1) for i in range(1, count - 1, 2)]
+    second = lax.ppermute(far_pair, "gz", links + [(j, i) for i, j in links])
+    return first, second
 
 
 def swap_cores(field):
@@ -508,9 +515,11 @@
     row_turn, row_back = row_tables(length, depth, width)
 
     strips = [initial[:, at : at + ROWS].astype(BF16) for at in (0, ROWS, rows - 2 * ROWS, rows - ROWS)]
-    low = jnp.concatenate([observed[:, :, :ROWS], own_strip(strips[0], strips[1])[None]], 0)
-    high = jnp.concatenate([observed[:, :, rows - ROWS :], own_strip(strips[3], strips[2])[None]], 0)
-    first_rims = send_rims(low, high)
+    low, high = own_strip(strips[0], strips[1]), own_strip(strips[3], strips[2])
+    seen_low, seen_high = observed[:, :, :ROWS], observed[:, :, rows - ROWS :]
+    near_pair = jnp.concatenate([by_parity(seen_low, seen_high), by_parity(low, high)[None]], 0)
+    far_pair = jnp.concatenate([by_parity(seen_high, seen_low), by_parity(high, low)[None]], 0)
+    first_rims = send_rims(near_pair, far_pair)
 
     chunk = slots // 2
     payload_block = (groups, 1, local_depth, rows, width)
@@ -682,7 +691,8 @@
         return (window[0] * jnp.exp(window[1] + window[2])).astype(BF16)
 
     strips = [updated_rows(at) for at in (0, ROWS, rows - 2 * ROWS, rows - ROWS)]
-    rims = send_rims(own_strip(strips[0], strips[1]), own_strip(strips[3], strips[2]))
+    low, high = own_strip(strips[0], strips[1]), own_strip(strips[3], strips[2])
+    rims = send_rims(by_parity(low, high), by_parity(high, low))
     crossed_b = crossed(sent_b, mine, other)
     strips = swap_strips(rims)
     back_b = turn(crossed_b)

time: 172 us -> 169 us (0.983)
  starting transfers between devices: 37.2 us -> 30.2 us
  waiting for transfers between devices: 56.4 us -> 60.7 us
    all_to_all x4, starting transfers between devices: 25.5 us -> 21.4 us  [turn(): lax.all_to_all(payload, 'gz', split_axis=0, concat_axis=0, tiled=True)]
    ppermute x4, waiting for transfers between devices: 26.6 us -> 29.7 us  [the longest x2 29.7 us: send_rims(): first = lax.ppermute(near_pair, 'gz', [(i, i ^ 1) for i in range(count)])]
    ppermute x4, starting transfers between devices: 11.1 us -> 8.26 us  [the longest x2 6.22 us: send_rims(): first = lax.ppermute(near_pair, 'gz', [(i, i ^ 1) for i in range(count)])]
    unnamed x50 -> x60, local copies, waits for them, and re-layouts: 6.73 us -> 7.18 us
  transfers between devices with their start and end apart: 13 -> 13, of which waited for: 5 -> 6; matrix products, arithmetic and copies ran while one was open for 4% -> 4% of each run, Pallas kernels for 33% -> 34%
where the time goes in v5:
time: 169 us; the launch traced here: 168 us
  Pallas kernels  61.4 us (36%)
  waiting for transfers between devices  60.7 us (36%)
  starting transfers between devices  30.2 us (18%)
  other arithmetic  7.3 us (4%)
  local copies, waits for them, and re-layouts  7.2 us (4%)
    ppermute x2, waiting for transfers between devices, send_rims(): first = lax.ppermute(near_pair, 'gz', [(i, i ^ 1) for i in range(count)])  29.7 us
    pallas_call x3, Pallas kernels, join(): pl.pallas_call(functools.partial(join_kernel, views, updated, partial is...  29.6 us
    all_to_all x4, waiting for transfers between devices, turn(): lax.all_to_all(payload, 'gz', split_axis=0, concat_axis=0, tiled=True)  26.8 us
    all_to_all x4, starting transfers between devices, turn(): lax.all_to_all(payload, 'gz', split_axis=0, concat_axis=0, tiled=True)  21.4 us
    pallas_call x2, Pallas kernels, first(): pl.pallas_call(first_kernel, grid_spec=pltpu.PrefetchScalarGridSpec(num_s...  10.3 us
    pallas_call x2, Pallas kernels, crossed(): pl.pallas_call(cross_kernel, grid_spec=pltpu.PrefetchScalarGridSpec(num_s...  8.27 us
    pallas_call x2, Pallas kernels, last(): pl.pallas_call(last_kernel, grid_spec=pltpu.PrefetchScalarGridSpec(num_sc...  7.92 us
    unnamed x60, local copies, waits for them, and re-layouts  7.18 us
  transfers between devices with their start and end apart: 13, of which 6 were waited for; matrix products, arithmetic and copies ran while one was open for 4% of the time, Pallas kernels for 34%

profile of v5, /device:TPU:0, one launch (start us, length us, event | category | flops | bytes accessed | tf_op | source)
XLA Modules:
  0.0 167.8 jit_solution(15262566962932641367)
XLA Ops:
  0.6 5.1 %first.2 = s16[8,2,4,32,256]{4,3,2,1,0:T(8,128)(2,1)} custom-call(s32[8]{0:T(128)} %map_ref.13, bf16[4,32,32,256]{3,2,1,0:T(8,128)(2,1)} %observed_ref.3, bf16[256,512]{1,0:T(8,128)(2,1)} %constant.41.clone.columns_ref), custom_call_target="tpu_custom_call" | custom-call | flops 2147483648 | bytes 2097152 | tf_op jit(solution)/shard_map/first/pallas_call | solution.py:531
  5.7 7.3 %all-to-all-start = ((s16[8,2,4,32,256]{4,3,2,1,0:T(8,128)(2,1)}), s16[8,2,4,32,256]{4,3,2,1,0:T(8,128)(2,1)S(1)}, u32[]{:S(2)}, u32[]{:S(2)}) async-start(s16[8,2,4,32,256]{4,3,2,1,0:T(8,128)(2,1)} %first.2), calls=%async_computation | async-start | bytes 2097152 | tf_op jit(solution)/shard_map/all_to_all | solution.py:475
  13.1 5.2 %first.3 = s16[8,2,4,32,256]{4,3,2,1,0:T(8,128)(2,1)} custom-call(s32[8]{0:T(128)} %map_ref.13, bf16[4,32,32,256]{3,2,1,0:T(8,128)(2,1)} %observed_ref.3, bf16[256,512]{1,0:T(8,128)(2,1)} %constant.41.clone.columns_ref), custom_call_target="tpu_custom_call" | custom-call | flops 2147483648 | bytes 2097152 | tf_op jit(solution)/shard_map/first/pallas_call | solution.py:531
  18.3 0.7 select_bitcast_fusion
  19.1 19.7 %all-to-all-done.in_ref = s16[8,2,4,32,256]{4,3,2,1,0:T(8,128)(2,1)S(1)} async-done(((s16[8,2,4,32,256]{4,3,2,1,0:T(8,128)(2,1)}), s16[8,2,4,32,256]{4,3,2,1,0:T(8,128)(2,1)S(1)}, u32[]{:S(2)}, u32[]{:S(2)}) %all-to-all-start) | async-done | bytes 1048608 | tf_op jit(solution)/shard_map/all_to_all | solution.py:475
  38.8 3.6 %all-to-all-start.1 = ((s16[8,2,4,32,256]{4,3,2,1,0:T(8,128)(2,1)}), s16[8,2,4,32,256]{4,3,2,1,0:T(8,128)(2,1)S(1)}, u32[]{:S(2)}, u32[]{:S(2)}) async-start(s16[8,2,4,32,256]{4,3,2,1,0:T(8,128)(2,1)} %first.3), calls=%async_computation.1 | async-start | bytes 2097152 | tf_op jit(solution)/shard_map/all_to_all | solution.py:475
  42.4 1.2 spectrum.1.mine_ref
  44.3 2.1 %collective-permute-start = (bf16[5,32,8,256]{3,2,1,0:T(8,128)(2,1)S(1)}, bf16[5,32,8,256]{3,2,1,0:T(8,128)(2,1)S(1)}, u32[]{:S(2)}, u32[]{:S(2)}) collective-permute-start(bf16[5,32,8,256]{3,2,1,0:T(8,128)(2,1)S(1)} %pad_maximum_fusion), channel_id=1, source_target_pairs={{0,2},{2,0},{4,6},{6,4},{8,10},{10,8},{12,14},{14,12},{1,3},{3,1},... | collective-permute-start | bytes 1966088 | tf_op jit(solution)/shard_map/ppermute | solution.py:488
  47.2 4.1 %cross.2 = s16[8,2,4,32,256]{4,3,2,1,0:T(8,128)(2,1)S(1)} custom-call(s32[8]{0:T(128)S(1)} %copy-done.8, s32[2]{0:T(128)S(1)} %pad_add_fusion.place_ref.refs_0_.refs_1_.refs_2_, s16[8,2,4,32,256]{4,3,2,1,0:T(8,128)(2,1)S(1)} %all-to-all-done.in_ref, bf16[256,512]{1,0:T(8,128)(2,1)S(1)} %copy-done.5, bf16[256,512]{1,0:T(8,128)(2,1)S(1)} %copy-done.12, ...), custom_call_target="tpu_custom_call" | custom-call | flops 1610612736 | bytes 4718592 | tf_op jit(solution)/shard_map/cross/pallas_call | solution.py:570
  51.3 1.0 copy-done.2
  52.3 29.7 %collective-permute-done.refs_5_.refs_6_.refs_7_ = bf16[5,32,8,256]{3,2,1,0:T(8,128)(2,1)S(1)} collective-permute-done((bf16[5,32,8,256]{3,2,1,0:T(8,128)(2,1)S(1)}, bf16[5,32,8,256]{3,2,1,0:T(8,128)(2,1)S(1)}, u32[]{:S(2)}, u32[]{:S(2)}) %collective-permute-start) | collective-permute-done | bytes 655392 | tf_op jit(solution)/shard_map/ppermute | solution.py:488
  82.1 0.8 copy-done.20
  84.5 4.0 %filters.1 = (bf16[4,256,768]{2,1,0:T(8,128)(2,1)}, bf16[4,256,768]{2,1,0:T(8,128)(2,1)}, bf16[4,256,256]{2,1,0:T(8,128)(2,1)}) custom-call(s32[2]{0:T(128)} %copy-done.6, s32[8]{0:T(128)} %map_ref.13, s32[8,2]{1,0:T(8,128)} %copy.12.shift_ref, f32[8,3,15]{2,1,0:T(4,128)} %copy.13.psf_ref), custom_call_target="tpu_custom_call" | custom-call | flops 15728640 | bytes 3670016 | tf_op jit(solution)/shard_map/filters/pallas_call | solution.py:619
  89.3 8.0 %join.3.refs_0_ = f32[32,32,256]{2,1,0:T(8,128)} custom-call(s32[2]{0:T(128)} %copy-done.6, f32[32,32,256]{2,1,0:T(8,128)} %refs_3_.1, bf16[2,32,8,256]{3,2,1,0:T(8,128)(2,1)} %copy-done.16, bf16[2,32,8,256]{3,2,1,0:T(8,128)(2,1)} %copy-done.24, bf16[4,32,32,256]{3,2,1,0:T(8,128)(2,1)} %observed_ref.3, bf16[5,32,8,256]{3,2,1,0:T(8,128)(2,1)} %copy-done.20, ...), custom_call_target="tpu_custom_call" | custom-call | flops 2818572288 | bytes 12000000 | tf_op jit(solution)/shard_map/join/pallas_call | solution.py:647
  97.3 6.7 %all-to-all-start.3 = ((s16[8,2,4,32,256]{4,3,2,1,0:T(8,128)(2,1)}), s16[8,2,4,32,256]{4,3,2,1,0:T(8,128)(2,1)S(1)}, u32[]{:S(2)}, u32[]{:S(2)}) async-start(s16[8,2,4,32,256]{4,3,2,1,0:T(8,128)(2,1)} %copy-done.2), calls=%async_computation.3 | async-start | bytes 2097152 | tf_op jit(solution)/shard_map/all_to_all | solution.py:475
  104.0 8.4 %join.4.refs_0_ = f32[32,32,256]{2,1,0:T(8,128)} custom-call(f32[32,32,256]{2,1,0:T(8,128)} %join.3.refs_0_, s32[2]{0:T(128)} %copy-done.6, f32[32,32,256]{2,1,0:T(8,128)} %refs_3_.1, bf16[2,32,8,256]{3,2,1,0:T(8,128)(2,1)} %copy-done.16, bf16[2,32,8,256]{3,2,1,0:T(8,128)(2,1)} %copy-done.24, bf16[4,32,32,256]{3,2,1,0:T(8,128)(2,1)} %observed_ref.3, ...), custom_call_target="tpu_custom_call" | custom-call | flops 2818572288 | bytes 12000000 | tf_op jit(solution)/shard_map/join/pallas_call | solution.py:647
  112.7 2.6 %collective-permute-done.4.refs_1_ = f32[32,32,256]{2,1,0:T(8,128)S(1)} collective-permute-done((f32[32,32,256]{2,1,0:T(8,128)}, f32[32,32,256]{2,1,0:T(8,128)S(1)}, u32[]{:S(2)}, u32[]{:S(2)}) %collective-permute-start.4) | collective-permute-done | bytes 1048608 | tf_op jit(solution)/shard_map/ppermute | solution.py:496
  115.4 2.8 %broadcast_select_fusion.3 = (bf16[32,8,256]{2,1,0:T(8,128)(2,1)}, bf16[32,8,256]{2,1,0:T(8,128)(2,1)S(1)}, bf16[32,8,256]{2,1,0:T(8,128)(2,1)S(1)}) fusion(pred[]{:T(512)S(6)} %eq.11, f32[32,32,256]{2,1,0:T(8,128)S(1)} %collective-permute-done.4.refs_1_, f32[32,32,256]{2,1,0:T(8,128)} %join.4.refs_0_, f32[32,32,256]{2,1,0:T(8,128)} %refs_3_.1, pred[]{:T(512)S(6)} %eq.22), kind=kLoop, calls=%fused_computation.34 | loop fusion | flops 983040 | bytes 3538946 | tf_op jit(solution)/shard_map/jit(_where)/select_n | solution.py:483
  118.2 1.3 collective-permute-start.6
  119.5 4.1 %collective-permute-start.5 = (bf16[32,8,256]{2,1,0:T(8,128)(2,1)}, bf16[32,8,256]{2,1,0:T(8,128)(2,1)}, u32[]{:S(2)}, u32[]{:S(2)}) collective-permute-start(bf16[32,8,256]{2,1,0:T(8,128)(2,1)} %get-tuple-element.18), channel_id=1, source_target_pairs={{0,2},{2,0},{4,6},{6,4},{8,10},{10,8},{12,14},{14,12},{1,3},{3,1},... | collective-permute-start | bytes 393224 | tf_op jit(solution)/shard_map/ppermute | solution.py:488
  123.7 4.2 %cross.3 = s16[8,2,4,32,256]{4,3,2,1,0:T(8,128)(2,1)S(1)} custom-call(s32[8]{0:T(128)S(1)} %copy-done.9, s32[2]{0:T(128)S(1)} %copy-done.7, s16[8,2,4,32,256]{4,3,2,1,0:T(8,128)(2,1)S(1)} %all-to-all-done.1.in_ref, bf16[256,512]{1,0:T(8,128)(2,1)S(1)} %copy-done.5, bf16[256,512]{1,0:T(8,128)(2,1)S(1)} %copy-done.13, f32[4,256,256]{2,1,0:T(8,128)S(1)} %spectrum.1.mine_ref, ...), custom_call_target="tpu_custom_call" | custom-call | flops 1610612736 | bytes 4718592 | tf_op jit(solution)/shard_map/cross/pallas_call | solution.py:570
  127.9 1.0 copy-done.3
  128.9 2.5 %all-to-all-done.3.in_ref = s16[8,2,4,32,256]{4,3,2,1,0:T(8,128)(2,1)S(1)} async-done(((s16[8,2,4,32,256]{4,3,2,1,0:T(8,128)(2,1)}), s16[8,2,4,32,256]{4,3,2,1,0:T(8,128)(2,1)S(1)}, u32[]{:S(2)}, u32[]{:S(2)}) %all-to-all-start.3) | async-done | bytes 1048608 | tf_op jit(solution)/shard_map/all_to_all | solution.py:475
  131.3 1.0 copy-done
  132.3 3.7 %all-to-all-start.2 = ((s16[8,2,4,32,256]{4,3,2,1,0:T(8,128)(2,1)}), s16[8,2,4,32,256]{4,3,2,1,0:T(8,128)(2,1)S(1)}, u32[]{:S(2)}, u32[]{:S(2)}) async-start(s16[8,2,4,32,256]{4,3,2,1,0:T(8,128)(2,1)} %copy-done.3), calls=%async_computation.2 | async-start | bytes 2097152 | tf_op jit(solution)/shard_map/all_to_all | solution.py:475
  136.1 1.0 pad_maximum_fusion.3.refs_4_
  137.2 1.5 collective-permute-done.7.refs_5_
  139.4 13.3 %join.5 = (f32[32,32,256]{2,1,0:T(8,128)}, f32[32,32,256]{2,1,0:T(8,128)}) custom-call(f32[32,32,256]{2,1,0:T(8,128)} %join.4.refs_0_, f32[32,32,256]{2,1,0:T(8,128)} %copy-done.17, s32[2]{0:T(128)} %copy-done.6, f32[32,32,256]{2,1,0:T(8,128)} %refs_3_.1, bf16[2,32,8,256]{3,2,1,0:T(8,128)(2,1)} %copy-done.25, bf16[2,32,8,256]{3,2,1,0:T(8,128)(2,1)} %copy-done.28, ...), custom_call_target="tpu_custom_call" | custom-call | flops 5637144576 | bytes 12000000 | tf_op jit(solution)/shard_map/join/pallas_call | solution.py:647
  152.8 4.0 %last.2.rest_0_ = f32[4,32,32,256]{3,2,1,0:T(8,128)} custom-call(s32[8]{0:T(128)S(1)} %copy-done.9, s16[8,2,4,32,256]{4,3,2,1,0:T(8,128)(2,1)S(1)} %copy-done.1, bf16[256,512]{1,0:T(8,128)(2,1)S(1)} %copy-done.4), custom_call_target="tpu_custom_call" | custom-call | flops 2415919104 | bytes 3145728 | tf_op jit(solution)/shard_map/last/pallas_call | solution.py:601
  156.8 4.6 %all-to-all-done.2.in_ref = s16[8,2,4,32,256]{4,3,2,1,0:T(8,128)(2,1)S(1)} async-done(((s16[8,2,4,32,256]{4,3,2,1,0:T(8,128)(2,1)}), s16[8,2,4,32,256]{4,3,2,1,0:T(8,128)(2,1)S(1)}, u32[]{:S(2)}, u32[]{:S(2)}) %all-to-all-start.2) | async-done | bytes 1048608 | tf_op jit(solution)/shard_map/all_to_all | solution.py:475
  161.4 4.0 %last.3 = f32[4,32,32,256]{3,2,1,0:T(8,128)} custom-call(s32[8]{0:T(128)S(1)} %copy-done.9, s16[8,2,4,32,256]{4,3,2,1,0:T(8,128)(2,1)S(1)} %all-to-all-done.2.in_ref, bf16[256,512]{1,0:T(8,128)(2,1)S(1)} %copy-done.4, f32[4,32,32,256]{3,2,1,0:T(8,128)} %last.2.rest_0_), custom_call_target="tpu_custom_call", output_to_operand_aliasing={{}: (3, {})} | custom-call | flops 2415919104 | bytes 3145728 | tf_op jit(solution)/shard_map/last/pallas_call | solution.py:601
  165.3 2.5 %exponential_multiply_fusion = f32[32,32,256]{2,1,0:T(8,128)} fusion(f32[32,32,256]{2,1,0:T(8,128)S(1)} %copy-done.19, f32[32,32,256]{2,1,0:T(8,128)S(1)} %copy-done.18, f32[32,32,256]{2,1,0:T(8,128)} %collective-permute-done.8), kind=kLoop, calls=%fused_computation | loop fusion | flops 524288 | bytes 4194304 | tf_op jit(solution)/shard_map/mul | solution.py:701
  (78 shorter events, 5.1 us)
Async XLA Ops:
  5.7 33.1 %all-to-all-start = ((s16[8,2,4,32,256]{4,3,2,1,0:T(8,128)(2,1)}), s16[8,2,4,32,256]{4,3,2,1,0:T(8,128)(2,1)S(1)}, u32[]{:S(2)}, u32[]{:S(2)}) async-start(s16[8,2,4,32,256]{4,3,2,1,0:T(8,128)(2,1)} %first.2), calls=%async_computation | async-start | bytes 2097152 | tf_op jit(solution)/shard_map/all_to_all | solution.py:475
  13.1 34.1 %copy-start.6 = (s32[2]{0:T(128)}, s32[2]{0:T(128)S(1)}, u32[]{:S(2)}) copy-start(s32[2]{0:T(128)S(1)} %pad_add_fusion.place_ref.refs_0_.refs_1_.refs_2_) | copy-start | bytes 28
  13.1 5.2 %copy-start.14 = (f32[32,32,256]{2,1,0:T(8,128)S(1)}, f32[32,32,256]{2,1,0:T(8,128)}, u32[]{:S(2)}) copy-start(f32[32,32,256]{2,1,0:T(8,128)} %refs_3_.1) | copy-start | bytes 3145732
  18.3 24.1 %copy-start.5 = (bf16[256,512]{1,0:T(8,128)(2,1)S(1)}, bf16[256,512]{1,0:T(8,128)(2,1)}, u32[]{:S(2)}) copy-start(bf16[256,512]{1,0:T(8,128)(2,1)} %constant.43.clone.rows_ref) | copy-start | bytes 786436
  38.8 58.5 %all-to-all-start.1 = ((s16[8,2,4,32,256]{4,3,2,1,0:T(8,128)(2,1)}), s16[8,2,4,32,256]{4,3,2,1,0:T(8,128)(2,1)S(1)}, u32[]{:S(2)}, u32[]{:S(2)}) async-start(s16[8,2,4,32,256]{4,3,2,1,0:T(8,128)(2,1)} %first.3), calls=%async_computation.1 | async-start | bytes 2097152 | tf_op jit(solution)/shard_map/all_to_all | solution.py:475
  42.4 1.7 %copy-start.15 = (bf16[4,32,32,256]{3,2,1,0:T(8,128)(2,1)S(1)}, bf16[4,32,32,256]{3,2,1,0:T(8,128)(2,1)}, u32[]{:S(2)}) copy-start(bf16[4,32,32,256]{3,2,1,0:T(8,128)(2,1)} %observed_ref.3) | copy-start | bytes 6291460
  43.6 3.5 %collective-permute-start.2 = (f32[4,256,256]{2,1,0:T(8,128)S(1)}, f32[4,256,256]{2,1,0:T(8,128)S(1)}, u32[]{:S(2)}, u32[]{:S(2)}) collective-permute-start(f32[4,256,256]{2,1,0:T(8,128)S(1)} %spectrum.1.mine_ref), channel_id=1, source_target_pairs={{0,1},{1,0},{2,3},{3,2},{4,5},{5,4},{6,7},{7,6},{8,9},{9,8},{10,11... | collective-permute-start | bytes 3145736 | tf_op jit(solution)/shard_map/ppermute | solution.py:496
  44.1 3.1 %copy-start.8 = (s32[8]{0:T(128)S(1)}, s32[8]{0:T(128)}, u32[]{:S(2)}) copy-start(s32[8]{0:T(128)} %map_ref.13) | copy-start | bytes 100
  44.1 3.1 %copy-start.12 = (bf16[256,512]{1,0:T(8,128)(2,1)S(1)}, bf16[256,512]{1,0:T(8,128)(2,1)}, u32[]{:S(2)}) copy-start(bf16[256,512]{1,0:T(8,128)(2,1)} %constant.44.clone.back_ref) | copy-start | bytes 786436
  44.3 37.8 %collective-permute-start = (bf16[5,32,8,256]{3,2,1,0:T(8,128)(2,1)S(1)}, bf16[5,32,8,256]{3,2,1,0:T(8,128)(2,1)S(1)}, u32[]{:S(2)}, u32[]{:S(2)}) collective-permute-start(bf16[5,32,8,256]{3,2,1,0:T(8,128)(2,1)S(1)} %pad_maximum_fusion), channel_id=1, source_target_pairs={{0,2},{2,0},{4,6},{6,4},{8,10},{10,8},{12,14},{14,12},{1,3},{3,1},... | collective-permute-start | bytes 1966088 | tf_op jit(solution)/shard_map/ppermute | solution.py:488
  46.4 36.8 %copy-start.27 = (s32[8,2]{0,1:T(2,128)S(1)}, s32[8,2]{0,1:T(2,128)}, u32[]{:S(2)}) copy-start(s32[8,2]{0,1:T(2,128)} %param.12) | copy-start | bytes 196
  46.4 37.4 %copy-start.26 = (f32[8,3,15]{2,0,1:T(8,128)S(1)}, f32[8,3,15]{2,0,1:T(8,128)}, u32[]{:S(2)}) copy-start(f32[8,3,15]{2,0,1:T(8,128)} %param.11) | copy-start | bytes 4324
  46.5 35.6 %collective-permute-start.1 = (bf16[5,32,8,256]{3,2,1,0:T(8,128)(2,1)S(1)}, bf16[5,32,8,256]{3,2,1,0:T(8,128)(2,1)S(1)}, u32[]{:S(2)}, u32[]{:S(2)}) collective-permute-start(bf16[5,32,8,256]{3,2,1,0:T(8,128)(2,1)S(1)} %pad_maximum_fusion.1), channel_id=1, source_target_pairs={{2,4},{6,8},{10,12},{4,2},{8,6},{12,10},{3,5},{7,9},{11,13},{5,3},... | collective-permute-start | bytes 1966088 | tf_op jit(solution)/shard_map/ppermute | solution.py:490
  47.2 4.1 %copy-start.10 = (f32[4,256,256]{2,1,0:T(8,128)}, f32[4,256,256]{2,1,0:T(8,128)S(1)}, u32[]{:S(2)}) copy-start(f32[4,256,256]{2,1,0:T(8,128)S(1)} %collective-permute-done.2.other_ref) | copy-start | bytes 3145732
  83.2 5.4 %copy-start.16 = (bf16[2,32,8,256]{3,2,1,0:T(8,128)(2,1)}, bf16[2,32,8,256]{3,2,1,0:T(8,128)(2,1)S(1)}, u32[]{:S(2)}) copy-start(bf16[2,32,8,256]{3,2,1,0:T(8,128)(2,1)S(1)} %pad_maximum_fusion.2.refs_2_.refs_3_) | copy-start | bytes 786436
  83.2 5.3 %collective-permute-start.3 = (bf16[2,32,8,256]{3,2,1,0:T(8,128)(2,1)S(1)}, bf16[2,32,8,256]{3,2,1,0:T(8,128)(2,1)S(1)}, u32[]{:S(2)}, u32[]{:S(2)}) collective-permute-start(bf16[2,32,8,256]{3,2,1,0:T(8,128)(2,1)S(1)} %pad_maximum_fusion.2.refs_2_.refs_3_), channel_id=1, source_target_pairs={{0,1},{1,0},{2,3},{3,2},{4,5},{5,4},{6,7},{7,6},{8,9},{9,8},{10,11... | collective-permute-start | bytes 786440 | tf_op jit(solution)/shard_map/ppermute | solution.py:496
  97.3 34.0 %all-to-all-start.3 = ((s16[8,2,4,32,256]{4,3,2,1,0:T(8,128)(2,1)}), s16[8,2,4,32,256]{4,3,2,1,0:T(8,128)(2,1)S(1)}, u32[]{:S(2)}, u32[]{:S(2)}) async-start(s16[8,2,4,32,256]{4,3,2,1,0:T(8,128)(2,1)} %copy-done.2), calls=%async_computation.3 | async-start | bytes 2097152 | tf_op jit(solution)/shard_map/all_to_all | solution.py:475
  112.4 11.3 %copy-start.7 = (s32[2]{0:T(128)S(1)}, s32[2]{0:T(128)}, u32[]{:S(2)}) copy-start(s32[2]{0:T(128)} %copy-done.6) | copy-start | bytes 28
  112.4 11.3 %copy-start.9 = (s32[8]{0:T(128)S(1)}, s32[8]{0:T(128)}, u32[]{:S(2)}) copy-start(s32[8]{0:T(128)} %map_ref.13) | copy-start | bytes 100
  112.4 11.2 %copy-start.11 = (f32[4,256,256]{2,1,0:T(8,128)S(1)}, f32[4,256,256]{2,1,0:T(8,128)}, u32[]{:S(2)}) copy-start(f32[4,256,256]{2,1,0:T(8,128)} %copy-done.10) | copy-start | bytes 3145732
  112.4 11.2 %copy-start.13 = (bf16[256,512]{1,0:T(8,128)(2,1)S(1)}, bf16[256,512]{1,0:T(8,128)(2,1)}, u32[]{:S(2)}) copy-start(bf16[256,512]{1,0:T(8,128)(2,1)} %constant.44.clone.back_ref) | copy-start | bytes 786436
  112.4 2.9 %collective-permute-start.4 = (f32[32,32,256]{2,1,0:T(8,128)}, f32[32,32,256]{2,1,0:T(8,128)S(1)}, u32[]{:S(2)}, u32[]{:S(2)}) collective-permute-start(f32[32,32,256]{2,1,0:T(8,128)} %join.4.refs_0_), channel_id=1, source_target_pairs={{0,1},{1,0},{2,3},{3,2},{4,5},{5,4},{6,7},{7,6},{8,9},{9,8},{10,11... | collective-permute-start | bytes 3145736 | tf_op jit(solution)/shard_map/ppermute | solution.py:496
  115.4 4.1 %copy-start.17 = (f32[32,32,256]{2,1,0:T(8,128)}, f32[32,32,256]{2,1,0:T(8,128)S(1)}, u32[]{:S(2)}) copy-start(f32[32,32,256]{2,1,0:T(8,128)S(1)} %collective-permute-done.4.refs_1_) | copy-start | bytes 3145732
  118.2 17.9 %collective-permute-start.6 = (bf16[32,8,256]{2,1,0:T(8,128)(2,1)S(1)}, bf16[32,8,256]{2,1,0:T(8,128)(2,1)}, u32[]{:S(2)}, u32[]{:S(2)}) collective-permute-start(bf16[32,8,256]{2,1,0:T(8,128)(2,1)S(1)} %broadcast_select_fusion.2), channel_id=1, source_target_pairs={{2,4},{6,8},{10,12},{4,2},{8,6},{12,10},{3,5},{7,9},{11,13},{5,3},... | collective-permute-start | bytes 393224 | tf_op jit(solution)/shard_map/ppermute | solution.py:490
  119.5 16.5 %collective-permute-start.5 = (bf16[32,8,256]{2,1,0:T(8,128)(2,1)}, bf16[32,8,256]{2,1,0:T(8,128)(2,1)}, u32[]{:S(2)}, u32[]{:S(2)}) collective-permute-start(bf16[32,8,256]{2,1,0:T(8,128)(2,1)} %get-tuple-element.18), channel_id=1, source_target_pairs={{0,2},{2,0},{4,6},{6,4},{8,10},{10,8},{12,14},{14,12},{1,3},{3,1},... | collective-permute-start | bytes 393224 | tf_op jit(solution)/shard_map/ppermute | solution.py:488
  132.3 29.1 %all-to-all-start.2 = ((s16[8,2,4,32,256]{4,3,2,1,0:T(8,128)(2,1)}), s16[8,2,4,32,256]{4,3,2,1,0:T(8,128)(2,1)S(1)}, u32[]{:S(2)}, u32[]{:S(2)}) async-start(s16[8,2,4,32,256]{4,3,2,1,0:T(8,128)(2,1)} %copy-done.3), calls=%async_computation.2 | async-start | bytes 2097152 | tf_op jit(solution)/shard_map/all_to_all | solution.py:475
  137.1 15.7 %copy-start.1 = (s16[8,2,4,32,256]{4,3,2,1,0:T(8,128)(2,1)S(1)}, s16[8,2,4,32,256]{4,3,2,1,0:T(8,128)(2,1)}, u32[]{:S(2)}) copy-start(s16[8,2,4,32,256]{4,3,2,1,0:T(8,128)(2,1)} %copy-done) | copy-start | bytes 3145732
  137.1 15.7 %copy-start.4 = (bf16[256,512]{1,0:T(8,128)(2,1)S(1)}, bf16[256,512]{1,0:T(8,128)(2,1)}, u32[]{:S(2)}) copy-start(bf16[256,512]{1,0:T(8,128)(2,1)} %constant.42.clone.columns_ref) | copy-start | bytes 786436
  137.1 1.6 collective-permute-start.7
  152.6 12.7 %collective-permute-start.8 = (f32[32,32,256]{2,1,0:T(8,128)}, f32[32,32,256]{2,1,0:T(8,128)}, u32[]{:S(2)}, u32[]{:S(2)}) collective-permute-start(f32[32,32,256]{2,1,0:T(8,128)} %get-tuple-element.16), channel_id=1, source_target_pairs={{0,1},{1,0},{2,3},{3,2},{4,5},{5,4},{6,7},{7,6},{8,9},{9,8},{10,11... | collective-permute-start | bytes 3145736 | tf_op jit(solution)/shard_map/ppermute | solution.py:496
  156.7 8.6 %copy-start.18 = (f32[32,32,256]{2,1,0:T(8,128)S(1)}, f32[32,32,256]{2,1,0:T(8,128)}, u32[]{:S(2)}) copy-start(f32[32,32,256]{2,1,0:T(8,128)} %get-tuple-element.16) | copy-start | bytes 3145732
  156.8 8.6 %copy-start.19 = (f32[32,32,256]{2,1,0:T(8,128)S(1)}, f32[32,32,256]{2,1,0:T(8,128)}, u32[]{:S(2)}) copy-start(f32[32,32,256]{2,1,0:T(8,128)} %get-tuple-element.15) | copy-start | bytes 3145732
  (10 other events, 10.7 us)
